TPU v7x, 256 devices: a whole 4x4x8 slice. The times are simulated.
256 devices in a mesh: region: 16 (over z, core), tracer: 16 (over y, x).
Axes of the slice: x: 4, y: 4, z: 8, core: 2. Of those that a mesh axis runs over, the one named last changes fastest.
Arguments:
- concentration: float32 [40, 128, 32768], P(None, 'tracer', 'region'), may hold values from 0 to 1
- courant: float32 [2, 3, 40, 32768], P(None, None, None, ('region', 'tracer')), may hold values from -0.3 to 0.3
- diffusivity: float32 [2, 39, 32768], P(None, None, ('region', 'tracer')), may hold values from 0.2 to 5
- release_rate: float32 [40, 128], P(None, 'tracer'), may hold values from 0.2 to 2
- release_cell: int32 [128], P('tracer'), may hold values from 0 to 32767
- neighbour: int32 [3, 32768], P(None, 'region'), may hold values from -1 to 2559, as said below
- send_rows: int32 [16, 16, 32], P('region'), may hold values from -1 to 63, as said below
Outputs:
- final_field: float32 [40, 128, 32768], P(None, 'tracer', 'region')
Inputs may be any that keep to these rules, and one draw needn't show every extreme that they name: `neighbour`: A value n below 2048 is a triangle of the same region; n of 2048 or more names halo slot n - 2048, slot s of the list from region p being p * 32 + s, and only live slots are named; -1 is a closed face. send_rows[p, r, s] is the rim row (triangle 2048 - 64 + row of region p) that region p sends to region r in slot s; -1 marks an empty slot and live slots come first; rows of one list differ; a region sends nothing to itself; every region fills all 32 slots to one peer and receives a full list from one peer.
All inputs are finite; a program needn't handle non-finite values.
Results may differ from a plain program's by a relative error of at most 0.0001.
Values sent between devices are 32-bit elements; how exact they have to be, the bound alone decides.
No kernel may reach another device: no remote copies, remote signals or barrier semaphores. Data moves between devices by JAX's collectives and lax.ppermute only.
A program may use at most 128 MiB of HBM per device.

v0:
```python
import jax
import jax.numpy as jnp
from jax import lax
from jax.sharding import Mesh
from jax.sharding import PartitionSpec as P

HOURS = 2
STEPS = 6
REGION = ("region_0", "region_1")
REGION_TRACER = ("region_0", "region_1", "tracer")


def cut_along(value, dim, devices):
    before, after = (value.shape[:dim], value.shape[dim + 1 :])
    return jnp.moveaxis(value.reshape(*before, devices, -1, *after), dim, 0)


def laid_out(tiles, dim):
    tiles = jnp.moveaxis(tiles, 0, dim)
    shape = tiles.shape
    return tiles.reshape(*shape[:dim], shape[dim] * shape[dim + 1], *shape[dim + 2 :])


def exchange_in_order(tiles, axes, turns):
    inside = tiles.shape[1:]
    result = tiles.reshape(*(lax.axis_size(a) for a in axes), *inside)
    for k in turns:
        result = lax.all_to_all(result, axes[k], k, k, tiled=True)
    return result.reshape(-1, *inside)


def exchange_by_axis(value, axes, turns, split_dim, concat_dim):
    tiles = cut_along(value, split_dim, lax.axis_size(axes))
    return laid_out(exchange_in_order(tiles, axes, turns), concat_dim)


def copy_for_each(value, axis):
    copies = jnp.broadcast_to(value, (lax.axis_size(axis), *value.shape))
    return lax.all_to_all(copies, axis, split_axis=0, concat_axis=0, tiled=True)


def gather_directly(value, axis, dim):
    return laid_out(copy_for_each(value, axis), dim)


def thomas_solve(mixing, source_term):
    layer_count = source_term.shape[0]
    ratios = []
    partial_value = []
    for layer_index in range(layer_count):
        lower_coef = mixing[layer_index - 1] if layer_index > 0 else jnp.zeros_like(mixing[0])
        upper_coef = (
            mixing[layer_index] if layer_index < layer_count - 1 else jnp.zeros_like(mixing[0])
        )
        pivots = 1.0 + lower_coef + upper_coef
        if layer_index > 0:
            pivots = pivots - lower_coef * ratios[layer_index - 1]
            current = (
                source_term[layer_index] + lower_coef[None, :] * partial_value[layer_index - 1]
            ) / pivots[None, :]
        else:
            current = source_term[layer_index] / pivots[None, :]
        ratios.append(upper_coef / pivots)
        partial_value.append(current)
    solved = [None] * layer_count
    solved[layer_count - 1] = partial_value[layer_count - 1]
    for layer_index in range(layer_count - 2, -1, -1):
        solved[layer_index] = (
            partial_value[layer_index] + ratios[layer_index][None, :] * solved[layer_index + 1]
        )
    return jnp.stack(solved)


def on_device(
    concentration, courant, diffusivity, release_rate, release_cell, neighbour, send_rows
):
    layer_count = concentration.shape[0]
    tracer_count = concentration.shape[1]
    cell_count = concentration.shape[2]
    region_count = send_rows.shape[1]
    slot_count = send_rows.shape[2]
    rim_width = 2 * slot_count
    rim_start = cell_count - rim_width
    flat_rows = layer_count * tracer_count
    halo_count = region_count * slot_count
    incoming = exchange_by_axis(send_rows, REGION, (1, 0), 1, 0)
    positions = (
        jnp.arange(region_count, dtype=jnp.int32)[:, None] * rim_width
        + jnp.maximum(incoming[:, 0, :], 0)
    ).reshape(-1)

    def fetch_halo(flat_field):
        whole_rims = gather_directly(flat_field[:, rim_start:], REGION, 1)
        return jnp.take(whole_rims, positions, axis=1)

    global_cell = lax.axis_index(REGION) * cell_count + jnp.arange(cell_count, dtype=jnp.int32)
    release_mask = (global_cell[None, :] == release_cell[:, None]).astype(jnp.float32)
    release_term = release_rate[:, :, None] * release_mask[None, :, :]
    has_edge = neighbour >= 0
    is_halo = neighbour >= cell_count
    local_index = jnp.clip(neighbour, 0, cell_count - 1).reshape(-1)
    halo_index = jnp.clip(neighbour - cell_count, 0, halo_count - 1).reshape(-1)

    def advance(field, flux_faces, outflow, mixing):
        flat_field = field.reshape(flat_rows, cell_count)
        halo_values = fetch_halo(flat_field)
        local_edge = jnp.take(flat_field, local_index, axis=1).reshape(
            layer_count, tracer_count, 3, cell_count
        )
        halo_edge = jnp.take(halo_values, halo_index, axis=1).reshape(
            layer_count, tracer_count, 3, cell_count
        )
        edge_value = jnp.where(
            is_halo[None, None],
            halo_edge,
            jnp.where(has_edge[None, None], local_edge, jnp.float32(0.0)),
        )
        inflow = jnp.sum(flux_faces[:, None, :, :] * edge_value, axis=2)
        updated = field - outflow[:, None, :] * field - inflow + release_term
        return thomas_solve(mixing, updated)

    all_flux, all_mixing = (
        gather_directly(courant, "tracer", 3),
        gather_directly(diffusivity, "tracer", 2),
    )
    field = concentration
    per_hour = STEPS // HOURS
    for hour_index in range(HOURS):
        flux_panel = all_flux[hour_index]
        mixing = all_mixing[hour_index]
        flux_faces = jnp.transpose(jnp.minimum(flux_panel, 0.0), (1, 0, 2))
        outflow = jnp.sum(jnp.maximum(flux_panel, 0.0), axis=0)

        def one_step(step_index, state):
            return advance(state, flux_faces, outflow, mixing)

        field = lax.fori_loop(0, per_hour, one_step, field)
    return field


def solution(mesh):
    torus = Mesh(
        mesh.devices.reshape(8, 2, mesh.shape["tracer"]), ("region_0", "region_1", "tracer")
    )
    return jax.shard_map(
        on_device,
        mesh=torus,
        in_specs=(
            P(None, "tracer", REGION),
            P(None, None, None, REGION_TRACER),
            P(None, None, REGION_TRACER),
            P(None, "tracer"),
            P("tracer"),
            P(None, REGION),
            P(REGION, None, None),
        ),
        out_specs=P(None, "tracer", REGION),
        check_vma=False,
    )
```

profile of v0, /device:TPU:1, one launch (start us, length us, event | category | flops | bytes accessed | tf_op | source)
XLA Modules:
  0.0 984.5 jit_solution(2652820515668113694)
XLA Ops:
  8.6 12.8 %all_to_all.35 = s32[8,2,1,1,32]{4,1,3,2,0:T(2,128)S(1)} all-to-all(s32[8,2,1,1,32]{4,1,3,2,0:T(2,128)S(1)} %copy.103), channel_id=1, replica_groups=mesh['region_0'=8,'region_1'=2,'tracer'=16] {'region_0'}, dimensions={0} | all-to-all | bytes 4096 | tf_op jit(solution)/shard_map/all_to_all | solution.py:28
  29.3 10.9 %all-to-all-done.5 = f32[16,2,39,128]{3,1,2,0:T(2,128)S(1)} async-done(((f32[16,2,39,128]{3,1,2,0:T(2,128)}), f32[16,2,39,128]{3,1,2,0:T(2,128)S(1)}, u32[]{:S(2)}, u32[]{:S(2)}) %all-to-all-start.5) | async-done | bytes 639008 | tf_op jit(solution)/shard_map/all_to_all | solution.py:39
  50.5 18.8 %all-to-all-done.2 = f32[16,2,3,40,128]{4,3,2,1,0:T(8,128)S(1)} async-done(((f32[16,2,3,40,128]{4,3,2,1,0:T(8,128)}), f32[16,2,3,40,128]{4,3,2,1,0:T(8,128)S(1)}, u32[]{:S(2)}, u32[]{:S(2)}) %all-to-all-start.2) | async-done | bytes 1966112 | tf_op jit(solution)/shard_map/all_to_all | solution.py:39
  81.3 451.7 %while.22 = (s32[]{:T(128)}, f32[40,8,2048]{2,1,0:T(8,128)S(1)}, f32[40,2048]{1,0:T(8,128)}, f32[40,3,2048]{2,1,0:T(4,128)}, pred[3,2048]{1,0:T(4,128)(4,1)}, /*...) while((s32[]{:T(128)}, f32[40,8,2048]{2,1,0:T(8,128)S(1)}, ...), condition=%wide.region_3.0_spmd.clone, body=%wide.region_1.6_spmd.clone.sunk | while | flops 19041792 | bytes 207227696 | solution.py:137
  82.9 9.4 all-to-all-start
  95.8 24.3 %gather_fusion.2 = f32[6144,320]{1,0:T(8,128)} fusion(f32[320,2048]{0,1:T(8,128)S(1)} %copy.132, s32[6144]{0:T(1024)S(1)} %get-tuple-element.1190), kind=kCustom, calls=%fused_computation.2.clone.clone.1 | custom fusion | bytes 15753216 | tf_op jit(solution)/shard_map/while/body/eval_jaxpr/jit(_take)/gather | solution.py:107
  120.1 8.6 select_bitcast_fusion.14
  128.7 9.0 copy.133
  137.7 13.6 %reshape.47492 = f32[40,8,3,2048]{3,2,1,0:T(4,128)} reshape(f32[320,6144]{1,0:T(8,128)} %copy.133) | data formatting | bytes 15728640 | tf_op jit(solution)/shard_map/while/body/eval_jaxpr/reshape | solution.py:107
  159.7 24.2 %gather_fusion.1 = f32[6144,320]{1,0:T(8,128)} fusion(f32[320,512]{0,1:T(8,128)S(1)} %select_bitcast_fusion.12, s32[6144]{0:T(1024)S(1)} %copy-done.14), kind=kCustom, calls=%fused_computation.1.clone.clone.1 | custom fusion | bytes 15753216 | tf_op jit(solution)/shard_map/while/body/eval_jaxpr/jit(_take)/gather | solution.py:110
  184.0 8.5 select_bitcast_fusion.13
  192.5 9.1 copy.131
  201.6 13.6 %reshape.47491 = f32[40,8,3,2048]{3,2,1,0:T(4,128)} reshape(f32[320,6144]{1,0:T(8,128)} %copy.131) | data formatting | bytes 15728640 | tf_op jit(solution)/shard_map/while/body/eval_jaxpr/reshape | solution.py:110
  215.2 13.3 %multiply_reduce_fusion.4 = f32[40,8,2048]{2,1,0:T(8,128)S(1)} fusion(f32[40,8,3,2048]{3,2,1,0:T(4,128)} %reshape.47491, f32[40,8,3,2048]{3,2,1,0:T(4,128)} %reshape.47492, f32[40,3,2048]{2,1,0:T(4,128)} %get-tuple-element.1549, pred[3,2048]{1,0:T(4,128)(4,1)S(1)} %copy-done.50, pred[3,2048]{1,0:T(4,128)(4,1)S(1)} %copy-done.52), kind=kLoop, calls=%fused_computation.8.clone.1 | loop fusion | flops 7208960 | bytes 19345408 | tf_op jit(solution)/shard_map/while/body/eval_jaxpr/reduce_sum | solution.py:118
  235.0 7.3 all-to-all-start
  245.8 24.3 %gather_fusion.2 = f32[6144,320]{1,0:T(8,128)} fusion(f32[320,2048]{0,1:T(8,128)S(1)} %copy.132, s32[6144]{0:T(1024)S(1)} %get-tuple-element.1190), kind=kCustom, calls=%fused_computation.2.clone.clone.1 | custom fusion | bytes 15753216 | tf_op jit(solution)/shard_map/while/body/eval_jaxpr/jit(_take)/gather | solution.py:107
  270.0 8.6 select_bitcast_fusion.14
  278.7 9.0 copy.133
  287.7 13.6 %reshape.47492 = f32[40,8,3,2048]{3,2,1,0:T(4,128)} reshape(f32[320,6144]{1,0:T(8,128)} %copy.133) | data formatting | bytes 15728640 | tf_op jit(solution)/shard_map/while/body/eval_jaxpr/reshape | solution.py:107
  309.7 24.2 %gather_fusion.1 = f32[6144,320]{1,0:T(8,128)} fusion(f32[320,512]{0,1:T(8,128)S(1)} %select_bitcast_fusion.12, s32[6144]{0:T(1024)S(1)} %copy-done.14), kind=kCustom, calls=%fused_computation.1.clone.clone.1 | custom fusion | bytes 15753216 | tf_op jit(solution)/shard_map/while/body/eval_jaxpr/jit(_take)/gather | solution.py:110
  333.9 8.5 select_bitcast_fusion.13
  342.5 9.1 copy.131
  351.5 13.6 %reshape.47491 = f32[40,8,3,2048]{3,2,1,0:T(4,128)} reshape(f32[320,6144]{1,0:T(8,128)} %copy.131) | data formatting | bytes 15728640 | tf_op jit(solution)/shard_map/while/body/eval_jaxpr/reshape | solution.py:110
  365.2 13.3 %multiply_reduce_fusion.4 = f32[40,8,2048]{2,1,0:T(8,128)S(1)} fusion(f32[40,8,3,2048]{3,2,1,0:T(4,128)} %reshape.47491, f32[40,8,3,2048]{3,2,1,0:T(4,128)} %reshape.47492, f32[40,3,2048]{2,1,0:T(4,128)} %get-tuple-element.1549, pred[3,2048]{1,0:T(4,128)(4,1)S(1)} %copy-done.50, pred[3,2048]{1,0:T(4,128)(4,1)S(1)} %copy-done.52), kind=kLoop, calls=%fused_computation.8.clone.1 | loop fusion | flops 7208960 | bytes 19345408 | tf_op jit(solution)/shard_map/while/body/eval_jaxpr/reduce_sum | solution.py:118
  384.9 7.2 all-to-all-start
  395.7 24.3 %gather_fusion.2 = f32[6144,320]{1,0:T(8,128)} fusion(f32[320,2048]{0,1:T(8,128)S(1)} %copy.132, s32[6144]{0:T(1024)S(1)} %get-tuple-element.1190), kind=kCustom, calls=%fused_computation.2.clone.clone.1 | custom fusion | bytes 15753216 | tf_op jit(solution)/shard_map/while/body/eval_jaxpr/jit(_take)/gather | solution.py:107
  420.0 8.6 select_bitcast_fusion.14
  428.6 9.0 copy.133
  437.6 13.6 %reshape.47492 = f32[40,8,3,2048]{3,2,1,0:T(4,128)} reshape(f32[320,6144]{1,0:T(8,128)} %copy.133) | data formatting | bytes 15728640 | tf_op jit(solution)/shard_map/while/body/eval_jaxpr/reshape | solution.py:107
  459.6 24.2 %gather_fusion.1 = f32[6144,320]{1,0:T(8,128)} fusion(f32[320,512]{0,1:T(8,128)S(1)} %select_bitcast_fusion.12, s32[6144]{0:T(1024)S(1)} %copy-done.14), kind=kCustom, calls=%fused_computation.1.clone.clone.1 | custom fusion | bytes 15753216 | tf_op jit(solution)/shard_map/while/body/eval_jaxpr/jit(_take)/gather | solution.py:110
  483.8 8.5 select_bitcast_fusion.13
  492.4 9.1 copy.131
  501.4 13.6 %reshape.47491 = f32[40,8,3,2048]{3,2,1,0:T(4,128)} reshape(f32[320,6144]{1,0:T(8,128)} %copy.131) | data formatting | bytes 15728640 | tf_op jit(solution)/shard_map/while/body/eval_jaxpr/reshape | solution.py:110
  515.1 13.3 %multiply_reduce_fusion.4 = f32[40,8,2048]{2,1,0:T(8,128)S(1)} fusion(f32[40,8,3,2048]{3,2,1,0:T(4,128)} %reshape.47491, f32[40,8,3,2048]{3,2,1,0:T(4,128)} %reshape.47492, f32[40,3,2048]{2,1,0:T(4,128)} %get-tuple-element.1549, pred[3,2048]{1,0:T(4,128)(4,1)S(1)} %copy-done.50, pred[3,2048]{1,0:T(4,128)(4,1)S(1)} %copy-done.52), kind=kLoop, calls=%fused_computation.8.clone.1 | loop fusion | flops 7208960 | bytes 19345408 | tf_op jit(solution)/shard_map/while/body/eval_jaxpr/reduce_sum | solution.py:118
  533.0 449.9 %while.23 = (s32[]{:T(128)}, f32[40,8,2048]{2,1,0:T(8,128)S(1)}, f32[40,2048]{1,0:T(8,128)}, f32[40,3,2048]{2,1,0:T(4,128)}, pred[3,2048]{1,0:T(4,128)(4,1)}, /*...) while((s32[]{:T(128)}, f32[40,8,2048]{2,1,0:T(8,128)S(1)}, ...), condition=%wide.region_7.11_spmd.clone, body=%wide.region_5.10_spmd.clone.sunk | while | flops 19041792 | bytes 205982512 | solution.py:137
  545.8 24.3 %gather_fusion.5 = f32[6144,320]{1,0:T(8,128)} fusion(f32[320,2048]{0,1:T(8,128)S(1)} %copy.136, s32[6144]{0:T(1024)S(1)} %get-tuple-element.1363), kind=kCustom, calls=%fused_computation.5.clone.clone.1 | custom fusion | bytes 15753216 | tf_op jit(solution)/shard_map/while/body/eval_jaxpr/jit(_take)/gather | solution.py:107
  570.1 8.6 select_bitcast_fusion.17
  578.7 9.0 copy.137
  587.8 13.5 %reshape.47500 = f32[40,8,3,2048]{3,2,1,0:T(4,128)} reshape(f32[320,6144]{1,0:T(8,128)} %copy.137) | data formatting | bytes 15728640 | tf_op jit(solution)/shard_map/while/body/eval_jaxpr/reshape | solution.py:107
  609.7 24.2 %gather_fusion.4 = f32[6144,320]{1,0:T(8,128)} fusion(f32[320,512]{0,1:T(8,128)S(1)} %select_bitcast_fusion.15, s32[6144]{0:T(1024)S(1)} %copy-done.15), kind=kCustom, calls=%fused_computation.4.clone.clone.1 | custom fusion | bytes 15753216 | tf_op jit(solution)/shard_map/while/body/eval_jaxpr/jit(_take)/gather | solution.py:110
  634.0 8.5 select_bitcast_fusion.16
  642.5 9.1 copy.135
  651.6 13.6 %reshape.47499 = f32[40,8,3,2048]{3,2,1,0:T(4,128)} reshape(f32[320,6144]{1,0:T(8,128)} %copy.135) | data formatting | bytes 15728640 | tf_op jit(solution)/shard_map/while/body/eval_jaxpr/reshape | solution.py:110
  665.2 13.3 %multiply_reduce_fusion.5 = f32[40,8,2048]{2,1,0:T(8,128)S(1)} fusion(f32[40,8,3,2048]{3,2,1,0:T(4,128)} %reshape.47499, f32[40,8,3,2048]{3,2,1,0:T(4,128)} %reshape.47500, f32[40,3,2048]{2,1,0:T(4,128)} %get-tuple-element.1588, pred[3,2048]{1,0:T(4,128)(4,1)S(1)} %copy-done.51, pred[3,2048]{1,0:T(4,128)(4,1)S(1)} %copy-done.53), kind=kLoop, calls=%fused_computation.260.clone.1 | loop fusion | flops 7208960 | bytes 19345408 | tf_op jit(solution)/shard_map/while/body/eval_jaxpr/reduce_sum | solution.py:118
  685.0 7.2 all-to-all-start.1
  695.7 24.3 %gather_fusion.5 = f32[6144,320]{1,0:T(8,128)} fusion(f32[320,2048]{0,1:T(8,128)S(1)} %copy.136, s32[6144]{0:T(1024)S(1)} %get-tuple-element.1363), kind=kCustom, calls=%fused_computation.5.clone.clone.1 | custom fusion | bytes 15753216 | tf_op jit(solution)/shard_map/while/body/eval_jaxpr/jit(_take)/gather | solution.py:107
  720.0 8.6 select_bitcast_fusion.17
  728.6 9.0 copy.137
  737.7 13.5 %reshape.47500 = f32[40,8,3,2048]{3,2,1,0:T(4,128)} reshape(f32[320,6144]{1,0:T(8,128)} %copy.137) | data formatting | bytes 15728640 | tf_op jit(solution)/shard_map/while/body/eval_jaxpr/reshape | solution.py:107
  759.6 24.2 %gather_fusion.4 = f32[6144,320]{1,0:T(8,128)} fusion(f32[320,512]{0,1:T(8,128)S(1)} %select_bitcast_fusion.15, s32[6144]{0:T(1024)S(1)} %copy-done.15), kind=kCustom, calls=%fused_computation.4.clone.clone.1 | custom fusion | bytes 15753216 | tf_op jit(solution)/shard_map/while/body/eval_jaxpr/jit(_take)/gather | solution.py:110
  783.9 8.5 select_bitcast_fusion.16
  792.4 9.1 copy.135
  801.5 13.6 %reshape.47499 = f32[40,8,3,2048]{3,2,1,0:T(4,128)} reshape(f32[320,6144]{1,0:T(8,128)} %copy.135) | data formatting | bytes 15728640 | tf_op jit(solution)/shard_map/while/body/eval_jaxpr/reshape | solution.py:110
  815.1 13.3 %multiply_reduce_fusion.5 = f32[40,8,2048]{2,1,0:T(8,128)S(1)} fusion(f32[40,8,3,2048]{3,2,1,0:T(4,128)} %reshape.47499, f32[40,8,3,2048]{3,2,1,0:T(4,128)} %reshape.47500, f32[40,3,2048]{2,1,0:T(4,128)} %get-tuple-element.1588, pred[3,2048]{1,0:T(4,128)(4,1)S(1)} %copy-done.51, pred[3,2048]{1,0:T(4,128)(4,1)S(1)} %copy-done.53), kind=kLoop, calls=%fused_computation.260.clone.1 | loop fusion | flops 7208960 | bytes 19345408 | tf_op jit(solution)/shard_map/while/body/eval_jaxpr/reduce_sum | solution.py:118
  834.9 7.2 all-to-all-start.1
  845.7 24.3 %gather_fusion.5 = f32[6144,320]{1,0:T(8,128)} fusion(f32[320,2048]{0,1:T(8,128)S(1)} %copy.136, s32[6144]{0:T(1024)S(1)} %get-tuple-element.1363), kind=kCustom, calls=%fused_computation.5.clone.clone.1 | custom fusion | bytes 15753216 | tf_op jit(solution)/shard_map/while/body/eval_jaxpr/jit(_take)/gather | solution.py:107
  869.9 8.6 select_bitcast_fusion.17
  878.5 9.0 copy.137
  887.6 13.5 %reshape.47500 = f32[40,8,3,2048]{3,2,1,0:T(4,128)} reshape(f32[320,6144]{1,0:T(8,128)} %copy.137) | data formatting | bytes 15728640 | tf_op jit(solution)/shard_map/while/body/eval_jaxpr/reshape | solution.py:107
  909.5 24.2 %gather_fusion.4 = f32[6144,320]{1,0:T(8,128)} fusion(f32[320,512]{0,1:T(8,128)S(1)} %select_bitcast_fusion.15, s32[6144]{0:T(1024)S(1)} %copy-done.15), kind=kCustom, calls=%fused_computation.4.clone.clone.1 | custom fusion | bytes 15753216 | tf_op jit(solution)/shard_map/while/body/eval_jaxpr/jit(_take)/gather | solution.py:110
  933.8 8.5 select_bitcast_fusion.16
  942.3 9.1 copy.135
  951.4 13.6 %reshape.47499 = f32[40,8,3,2048]{3,2,1,0:T(4,128)} reshape(f32[320,6144]{1,0:T(8,128)} %copy.135) | data formatting | bytes 15728640 | tf_op jit(solution)/shard_map/while/body/eval_jaxpr/reshape | solution.py:110
  965.0 13.3 %multiply_reduce_fusion.5 = f32[40,8,2048]{2,1,0:T(8,128)S(1)} fusion(f32[40,8,3,2048]{3,2,1,0:T(4,128)} %reshape.47499, f32[40,8,3,2048]{3,2,1,0:T(4,128)} %reshape.47500, f32[40,3,2048]{2,1,0:T(4,128)} %get-tuple-element.1588, pred[3,2048]{1,0:T(4,128)(4,1)S(1)} %copy-done.51, pred[3,2048]{1,0:T(4,128)(4,1)S(1)} %copy-done.53), kind=kLoop, calls=%fused_computation.260.clone.1 | loop fusion | flops 7208960 | bytes 19345408 | tf_op jit(solution)/shard_map/while/body/eval_jaxpr/reduce_sum | solution.py:118
  (940 shorter events, 152.1 us)
Async XLA Ops:
  0.0 40.2 %copy-start.94 = (f32[2,3,40,128]{3,2,1,0:T(8,128)S(1)}, f32[2,3,40,128]{3,2,1,0:T(8,128)}, u32[]{:S(2)}) copy-start(f32[2,3,40,128]{3,2,1,0:T(8,128)} %param.18) | copy-start | bytes 368644
  0.0 21.5 %copy-start.95 = (f32[2,39,128]{2,0,1:T(2,128)S(1)}, f32[2,39,128]{2,0,1:T(2,128)}, u32[]{:S(2)}) copy-start(f32[2,39,128]{2,0,1:T(2,128)} %param.19) | copy-start | bytes 119812
  0.0 29.2 %copy-start.93 = (s32[3,2048]{1,0:T(4,128)S(1)}, s32[3,2048]{1,0:T(4,128)}, u32[]{:S(2)}) copy-start(s32[3,2048]{1,0:T(4,128)} %param.22) | copy-start | bytes 73732
  22.5 17.7 %all-to-all-start.5 = ((f32[16,2,39,128]{3,1,2,0:T(2,128)}), f32[16,2,39,128]{3,1,2,0:T(2,128)S(1)}, u32[]{:S(2)}, u32[]{:S(2)}) async-start(f32[16,2,39,128]{3,1,2,0:T(2,128)} %broadcast_in_dim.69), calls=%async_computation.5 | async-start | bytes 1277952 | tf_op jit(solution)/shard_map/all_to_all | solution.py:39
  29.3 16.2 %copy-start.97 = (f32[40,8]{0,1:T(8,128)S(1)}, f32[40,8]{0,1:T(8,128)}, u32[]{:S(2)}) copy-start(f32[40,8]{0,1:T(8,128)} %param.20) | copy-start | bytes 3844
  29.3 17.5 %copy-start.98 = (s32[8]{0:T(128)S(1)}, s32[8]{0:T(128)}, u32[]{:S(2)}) copy-start(s32[8]{0:T(128)} %param.21) | copy-start | bytes 100
  41.6 27.7 %all-to-all-start.2 = ((f32[16,2,3,40,128]{4,3,2,1,0:T(8,128)}), f32[16,2,3,40,128]{4,3,2,1,0:T(8,128)S(1)}, u32[]{:S(2)}, u32[]{:S(2)}) async-start(f32[16,2,3,40,128]{4,3,2,1,0:T(8,128)} %broadcast_in_dim.68), calls=%async_computation.2 | async-start | bytes 3932160 | tf_op jit(solution)/shard_map/all_to_all | solution.py:39
  81.3 451.7 %copy-start.6 = (f32[5,8,16,128]{3,1,2,0:T(8,128)S(1)}, f32[5,8,16,128]{3,1,2,0:T(8,128)}, u32[]{:S(2)}) copy-start(f32[5,8,16,128]{3,1,2,0:T(8,128)} %copy.115) | copy-start | bytes 983044
  81.3 11.6 %copy-start = (f32[40,8,2048]{2,1,0:T(8,128)}, f32[40,8,2048]{2,1,0:T(8,128)S(1)}, u32[]{:S(2)}) copy-start(f32[40,8,2048]{2,1,0:T(8,128)S(1)} %get-tuple-element.1534) | copy-start | bytes 7864324 | tf_op jit(solution)/shard_map/while
  82.9 73.4 %all-to-all-start = ((f32[16,320,64]{1,2,0:T(8,128)}), f32[16,320,64]{1,2,0:T(8,128)}, u32[]{:S(2)}, u32[]{:S(2)}) async-start(f32[16,320,64]{1,2,0:T(8,128)} %broadcast_in_dim.104), calls=%async_computation | async-start | bytes 3145728 | tf_op jit(solution)/shard_map/while/body/eval_jaxpr/all_to_all | solution.py:39
  137.7 15.0 %copy-start.7 = (f32[39,2048]{1,0:T(8,128)S(1)}, f32[39,2048]{1,0:T(8,128)}, u32[]{:S(2)}) copy-start(f32[39,2048]{1,0:T(8,128)} %get-tuple-element.1555) | copy-start | bytes 958468 | tf_op jit(solution)/shard_map/while
  159.7 24.3 %copy-start.91 = (pred[6144]{0:T(1024)(128)(4,1)S(1)}, pred[6144]{0:T(1024)(128)(4,1)}, u32[]{:S(2)}) copy-start(pred[6144]{0:T(1024)(128)(4,1)} %get-tuple-element.1189) | copy-start | bytes 18436 | tf_op jit(solution)/shard_map/while
  201.6 13.6 %copy-start.50 = (pred[3,2048]{1,0:T(4,128)(4,1)S(1)}, pred[3,2048]{1,0:T(4,128)(4,1)}, u32[]{:S(2)}) copy-start(pred[3,2048]{1,0:T(4,128)(4,1)} %get-tuple-element.1553) | copy-start | bytes 18436 | tf_op jit(solution)/shard_map/while
  201.6 13.6 %copy-start.52 = (pred[3,2048]{1,0:T(4,128)(4,1)S(1)}, pred[3,2048]{1,0:T(4,128)(4,1)}, u32[]{:S(2)}) copy-start(pred[3,2048]{1,0:T(4,128)(4,1)} %get-tuple-element.1550) | copy-start | bytes 18436 | tf_op jit(solution)/shard_map/while
  215.2 13.4 %copy-start.1 = (f32[40,8,2048]{2,1,0:T(8,128)S(1)}, f32[40,8,2048]{2,1,0:T(8,128)}, u32[]{:S(2)}) copy-start(f32[40,8,2048]{2,1,0:T(8,128)} %copy-done) | copy-start | bytes 7864324 | tf_op jit(solution)/shard_map/while
  215.2 13.4 %copy-start.9 = (f32[40,2048]{1,0:T(8,128)S(1)}, f32[40,2048]{1,0:T(8,128)}, u32[]{:S(2)}) copy-start(f32[40,2048]{1,0:T(8,128)} %get-tuple-element.1548) | copy-start | bytes 983044 | tf_op jit(solution)/shard_map/while
  215.2 13.4 %copy-start.10 = (f32[8,2048]{1,0:T(8,128)S(1)}, f32[8,2048]{1,0:T(8,128)}, u32[]{:S(2)}) copy-start(f32[8,2048]{1,0:T(8,128)} %get-tuple-element.1556) | copy-start | bytes 196612 | tf_op jit(solution)/shard_map/while
  215.2 13.4 %copy-start.12 = (f32[40,8]{1,0:T(8,128)S(1)}, f32[40,8]{1,0:T(8,128)}, u32[]{:S(2)}) copy-start(f32[40,8]{1,0:T(8,128)} %get-tuple-element.1557) | copy-start | bytes 3844 | tf_op jit(solution)/shard_map/while
  233.1 9.7 copy-start
  235.0 71.3 %all-to-all-start = ((f32[16,320,64]{1,2,0:T(8,128)}), f32[16,320,64]{1,2,0:T(8,128)}, u32[]{:S(2)}, u32[]{:S(2)}) async-start(f32[16,320,64]{1,2,0:T(8,128)} %broadcast_in_dim.104), calls=%async_computation | async-start | bytes 3145728 | tf_op jit(solution)/shard_map/while/body/eval_jaxpr/all_to_all | solution.py:39
  287.7 15.0 %copy-start.7 = (f32[39,2048]{1,0:T(8,128)S(1)}, f32[39,2048]{1,0:T(8,128)}, u32[]{:S(2)}) copy-start(f32[39,2048]{1,0:T(8,128)} %get-tuple-element.1555) | copy-start | bytes 958468 | tf_op jit(solution)/shard_map/while
  309.7 24.3 %copy-start.91 = (pred[6144]{0:T(1024)(128)(4,1)S(1)}, pred[6144]{0:T(1024)(128)(4,1)}, u32[]{:S(2)}) copy-start(pred[6144]{0:T(1024)(128)(4,1)} %get-tuple-element.1189) | copy-start | bytes 18436 | tf_op jit(solution)/shard_map/while
  351.5 13.6 %copy-start.50 = (pred[3,2048]{1,0:T(4,128)(4,1)S(1)}, pred[3,2048]{1,0:T(4,128)(4,1)}, u32[]{:S(2)}) copy-start(pred[3,2048]{1,0:T(4,128)(4,1)} %get-tuple-element.1553) | copy-start | bytes 18436 | tf_op jit(solution)/shard_map/while
  351.5 13.6 %copy-start.52 = (pred[3,2048]{1,0:T(4,128)(4,1)S(1)}, pred[3,2048]{1,0:T(4,128)(4,1)}, u32[]{:S(2)}) copy-start(pred[3,2048]{1,0:T(4,128)(4,1)} %get-tuple-element.1550) | copy-start | bytes 18436 | tf_op jit(solution)/shard_map/while
  365.1 13.4 %copy-start.1 = (f32[40,8,2048]{2,1,0:T(8,128)S(1)}, f32[40,8,2048]{2,1,0:T(8,128)}, u32[]{:S(2)}) copy-start(f32[40,8,2048]{2,1,0:T(8,128)} %copy-done) | copy-start | bytes 7864324 | tf_op jit(solution)/shard_map/while
  365.1 13.4 %copy-start.9 = (f32[40,2048]{1,0:T(8,128)S(1)}, f32[40,2048]{1,0:T(8,128)}, u32[]{:S(2)}) copy-start(f32[40,2048]{1,0:T(8,128)} %get-tuple-element.1548) | copy-start | bytes 983044 | tf_op jit(solution)/shard_map/while
  365.2 13.4 %copy-start.10 = (f32[8,2048]{1,0:T(8,128)S(1)}, f32[8,2048]{1,0:T(8,128)}, u32[]{:S(2)}) copy-start(f32[8,2048]{1,0:T(8,128)} %get-tuple-element.1556) | copy-start | bytes 196612 | tf_op jit(solution)/shard_map/while
  365.2 13.4 %copy-start.12 = (f32[40,8]{1,0:T(8,128)S(1)}, f32[40,8]{1,0:T(8,128)}, u32[]{:S(2)}) copy-start(f32[40,8]{1,0:T(8,128)} %get-tuple-element.1557) | copy-start | bytes 3844 | tf_op jit(solution)/shard_map/while
  383.1 9.7 copy-start
  384.9 71.2 %all-to-all-start = ((f32[16,320,64]{1,2,0:T(8,128)}), f32[16,320,64]{1,2,0:T(8,128)}, u32[]{:S(2)}, u32[]{:S(2)}) async-start(f32[16,320,64]{1,2,0:T(8,128)} %broadcast_in_dim.104), calls=%async_computation | async-start | bytes 3145728 | tf_op jit(solution)/shard_map/while/body/eval_jaxpr/all_to_all | solution.py:39
  437.6 15.0 %copy-start.7 = (f32[39,2048]{1,0:T(8,128)S(1)}, f32[39,2048]{1,0:T(8,128)}, u32[]{:S(2)}) copy-start(f32[39,2048]{1,0:T(8,128)} %get-tuple-element.1555) | copy-start | bytes 958468 | tf_op jit(solution)/shard_map/while
  459.6 24.3 %copy-start.91 = (pred[6144]{0:T(1024)(128)(4,1)S(1)}, pred[6144]{0:T(1024)(128)(4,1)}, u32[]{:S(2)}) copy-start(pred[6144]{0:T(1024)(128)(4,1)} %get-tuple-element.1189) | copy-start | bytes 18436 | tf_op jit(solution)/shard_map/while
  501.4 13.6 %copy-start.50 = (pred[3,2048]{1,0:T(4,128)(4,1)S(1)}, pred[3,2048]{1,0:T(4,128)(4,1)}, u32[]{:S(2)}) copy-start(pred[3,2048]{1,0:T(4,128)(4,1)} %get-tuple-element.1553) | copy-start | bytes 18436 | tf_op jit(solution)/shard_map/while
  501.4 13.6 %copy-start.52 = (pred[3,2048]{1,0:T(4,128)(4,1)S(1)}, pred[3,2048]{1,0:T(4,128)(4,1)}, u32[]{:S(2)}) copy-start(pred[3,2048]{1,0:T(4,128)(4,1)} %get-tuple-element.1550) | copy-start | bytes 18436 | tf_op jit(solution)/shard_map/while
  515.1 13.4 %copy-start.1 = (f32[40,8,2048]{2,1,0:T(8,128)S(1)}, f32[40,8,2048]{2,1,0:T(8,128)}, u32[]{:S(2)}) copy-start(f32[40,8,2048]{2,1,0:T(8,128)} %copy-done) | copy-start | bytes 7864324 | tf_op jit(solution)/shard_map/while
  515.1 13.4 %copy-start.9 = (f32[40,2048]{1,0:T(8,128)S(1)}, f32[40,2048]{1,0:T(8,128)}, u32[]{:S(2)}) copy-start(f32[40,2048]{1,0:T(8,128)} %get-tuple-element.1548) | copy-start | bytes 983044 | tf_op jit(solution)/shard_map/while
  515.1 13.4 %copy-start.10 = (f32[8,2048]{1,0:T(8,128)S(1)}, f32[8,2048]{1,0:T(8,128)}, u32[]{:S(2)}) copy-start(f32[8,2048]{1,0:T(8,128)} %get-tuple-element.1556) | copy-start | bytes 196612 | tf_op jit(solution)/shard_map/while
  515.1 13.4 %copy-start.12 = (f32[40,8]{1,0:T(8,128)S(1)}, f32[40,8]{1,0:T(8,128)}, u32[]{:S(2)}) copy-start(f32[40,8]{1,0:T(8,128)} %get-tuple-element.1557) | copy-start | bytes 3844 | tf_op jit(solution)/shard_map/while
  533.2 9.7 copy-start.2
  535.1 71.2 %all-to-all-start.1 = ((f32[16,320,64]{1,2,0:T(8,128)}), f32[16,320,64]{1,2,0:T(8,128)}, u32[]{:S(2)}, u32[]{:S(2)}) async-start(f32[16,320,64]{1,2,0:T(8,128)} %broadcast_in_dim.108), calls=%async_computation.1 | async-start | bytes 3145728 | tf_op jit(solution)/shard_map/while/body/eval_jaxpr/all_to_all | solution.py:39
  609.7 24.3 %copy-start.92 = (pred[6144]{0:T(1024)(128)(4,1)S(1)}, pred[6144]{0:T(1024)(128)(4,1)}, u32[]{:S(2)}) copy-start(pred[6144]{0:T(1024)(128)(4,1)} %get-tuple-element.1362) | copy-start | bytes 18436 | tf_op jit(solution)/shard_map/while
  651.6 13.6 %copy-start.51 = (pred[3,2048]{1,0:T(4,128)(4,1)S(1)}, pred[3,2048]{1,0:T(4,128)(4,1)}, u32[]{:S(2)}) copy-start(pred[3,2048]{1,0:T(4,128)(4,1)} %get-tuple-element.1592) | copy-start | bytes 18436 | tf_op jit(solution)/shard_map/while
  651.6 13.6 %copy-start.53 = (pred[3,2048]{1,0:T(4,128)(4,1)S(1)}, pred[3,2048]{1,0:T(4,128)(4,1)}, u32[]{:S(2)}) copy-start(pred[3,2048]{1,0:T(4,128)(4,1)} %get-tuple-element.1589) | copy-start | bytes 18436 | tf_op jit(solution)/shard_map/while
  665.2 13.4 %copy-start.3 = (f32[40,8,2048]{2,1,0:T(8,128)S(1)}, f32[40,8,2048]{2,1,0:T(8,128)}, u32[]{:S(2)}) copy-start(f32[40,8,2048]{2,1,0:T(8,128)} %copy-done.2) | copy-start | bytes 7864324 | tf_op jit(solution)/shard_map/while
  665.2 13.4 %copy-start.8 = (f32[40,2048]{1,0:T(8,128)S(1)}, f32[40,2048]{1,0:T(8,128)}, u32[]{:S(2)}) copy-start(f32[40,2048]{1,0:T(8,128)} %get-tuple-element.1587) | copy-start | bytes 983044 | tf_op jit(solution)/shard_map/while
  665.2 13.4 %copy-start.11 = (f32[8,2048]{1,0:T(8,128)S(1)}, f32[8,2048]{1,0:T(8,128)}, u32[]{:S(2)}) copy-start(f32[8,2048]{1,0:T(8,128)} %get-tuple-element.1595) | copy-start | bytes 196612 | tf_op jit(solution)/shard_map/while
  665.2 13.4 %copy-start.13 = (f32[40,8]{1,0:T(8,128)S(1)}, f32[40,8]{1,0:T(8,128)}, u32[]{:S(2)}) copy-start(f32[40,8]{1,0:T(8,128)} %get-tuple-element.1596) | copy-start | bytes 3844 | tf_op jit(solution)/shard_map/while
  683.2 9.7 copy-start.2
  685.0 71.2 %all-to-all-start.1 = ((f32[16,320,64]{1,2,0:T(8,128)}), f32[16,320,64]{1,2,0:T(8,128)}, u32[]{:S(2)}, u32[]{:S(2)}) async-start(f32[16,320,64]{1,2,0:T(8,128)} %broadcast_in_dim.108), calls=%async_computation.1 | async-start | bytes 3145728 | tf_op jit(solution)/shard_map/while/body/eval_jaxpr/all_to_all | solution.py:39
  759.6 24.3 %copy-start.92 = (pred[6144]{0:T(1024)(128)(4,1)S(1)}, pred[6144]{0:T(1024)(128)(4,1)}, u32[]{:S(2)}) copy-start(pred[6144]{0:T(1024)(128)(4,1)} %get-tuple-element.1362) | copy-start | bytes 18436 | tf_op jit(solution)/shard_map/while
  801.5 13.6 %copy-start.51 = (pred[3,2048]{1,0:T(4,128)(4,1)S(1)}, pred[3,2048]{1,0:T(4,128)(4,1)}, u32[]{:S(2)}) copy-start(pred[3,2048]{1,0:T(4,128)(4,1)} %get-tuple-element.1592) | copy-start | bytes 18436 | tf_op jit(solution)/shard_map/while
  801.5 13.6 %copy-start.53 = (pred[3,2048]{1,0:T(4,128)(4,1)S(1)}, pred[3,2048]{1,0:T(4,128)(4,1)}, u32[]{:S(2)}) copy-start(pred[3,2048]{1,0:T(4,128)(4,1)} %get-tuple-element.1589) | copy-start | bytes 18436 | tf_op jit(solution)/shard_map/while
  815.1 13.4 %copy-start.3 = (f32[40,8,2048]{2,1,0:T(8,128)S(1)}, f32[40,8,2048]{2,1,0:T(8,128)}, u32[]{:S(2)}) copy-start(f32[40,8,2048]{2,1,0:T(8,128)} %copy-done.2) | copy-start | bytes 7864324 | tf_op jit(solution)/shard_map/while
  815.1 13.4 %copy-start.8 = (f32[40,2048]{1,0:T(8,128)S(1)}, f32[40,2048]{1,0:T(8,128)}, u32[]{:S(2)}) copy-start(f32[40,2048]{1,0:T(8,128)} %get-tuple-element.1587) | copy-start | bytes 983044 | tf_op jit(solution)/shard_map/while
  815.1 13.4 %copy-start.11 = (f32[8,2048]{1,0:T(8,128)S(1)}, f32[8,2048]{1,0:T(8,128)}, u32[]{:S(2)}) copy-start(f32[8,2048]{1,0:T(8,128)} %get-tuple-element.1595) | copy-start | bytes 196612 | tf_op jit(solution)/shard_map/while
  815.1 13.4 %copy-start.13 = (f32[40,8]{1,0:T(8,128)S(1)}, f32[40,8]{1,0:T(8,128)}, u32[]{:S(2)}) copy-start(f32[40,8]{1,0:T(8,128)} %get-tuple-element.1596) | copy-start | bytes 3844 | tf_op jit(solution)/shard_map/while
  834.9 71.2 %all-to-all-start.1 = ((f32[16,320,64]{1,2,0:T(8,128)}), f32[16,320,64]{1,2,0:T(8,128)}, u32[]{:S(2)}, u32[]{:S(2)}) async-start(f32[16,320,64]{1,2,0:T(8,128)} %broadcast_in_dim.108), calls=%async_computation.1 | async-start | bytes 3145728 | tf_op jit(solution)/shard_map/while/body/eval_jaxpr/all_to_all | solution.py:39
  909.5 24.3 %copy-start.92 = (pred[6144]{0:T(1024)(128)(4,1)S(1)}, pred[6144]{0:T(1024)(128)(4,1)}, u32[]{:S(2)}) copy-start(pred[6144]{0:T(1024)(128)(4,1)} %get-tuple-element.1362) | copy-start | bytes 18436 | tf_op jit(solution)/shard_map/while
  951.4 13.6 %copy-start.51 = (pred[3,2048]{1,0:T(4,128)(4,1)S(1)}, pred[3,2048]{1,0:T(4,128)(4,1)}, u32[]{:S(2)}) copy-start(pred[3,2048]{1,0:T(4,128)(4,1)} %get-tuple-element.1592) | copy-start | bytes 18436 | tf_op jit(solution)/shard_map/while
  951.4 13.6 %copy-start.53 = (pred[3,2048]{1,0:T(4,128)(4,1)S(1)}, pred[3,2048]{1,0:T(4,128)(4,1)}, u32[]{:S(2)}) copy-start(pred[3,2048]{1,0:T(4,128)(4,1)} %get-tuple-element.1589) | copy-start | bytes 18436 | tf_op jit(solution)/shard_map/while
  965.0 13.4 %copy-start.3 = (f32[40,8,2048]{2,1,0:T(8,128)S(1)}, f32[40,8,2048]{2,1,0:T(8,128)}, u32[]{:S(2)}) copy-start(f32[40,8,2048]{2,1,0:T(8,128)} %copy-done.2) | copy-start | bytes 7864324 | tf_op jit(solution)/shard_map/while
  965.0 13.4 %copy-start.8 = (f32[40,2048]{1,0:T(8,128)S(1)}, f32[40,2048]{1,0:T(8,128)}, u32[]{:S(2)}) copy-start(f32[40,2048]{1,0:T(8,128)} %get-tuple-element.1587) | copy-start | bytes 983044 | tf_op jit(solution)/shard_map/while
  965.0 13.4 %copy-start.11 = (f32[8,2048]{1,0:T(8,128)S(1)}, f32[8,2048]{1,0:T(8,128)}, u32[]{:S(2)}) copy-start(f32[8,2048]{1,0:T(8,128)} %get-tuple-element.1595) | copy-start | bytes 196612 | tf_op jit(solution)/shard_map/while
  965.0 13.4 %copy-start.13 = (f32[40,8]{1,0:T(8,128)S(1)}, f32[40,8]{1,0:T(8,128)}, u32[]{:S(2)}) copy-start(f32[40,8]{1,0:T(8,128)} %get-tuple-element.1596) | copy-start | bytes 3844 | tf_op jit(solution)/shard_map/while
  (223 other events, 284.6 us)
where the time goes:
time: 992 us; the launch traced here: 984 us
  local copies, waits for them, and re-layouts  637 us (64%)
  other arithmetic  237 us (24%)
  starting transfers between devices  56 us (6%)
  waiting for transfers between devices  29.6 us (3%)
  blocking collectives  19.4 us (2%)
    gather x6, local copies, waits for them, and re-layouts, advance(): jnp.take(flat_field, local_index, axis=1)  146 us
    gather x6, local copies, waits for them, and re-layouts, advance(): jnp.take(halo_values, halo_index, axis=1)  145 us
    reshape x6, local copies, waits for them, and re-layouts, advance(): jnp.take(halo_values, halo_index, axis=1)  81.6 us
    reshape x6, local copies, waits for them, and re-layouts, advance(): jnp.take(flat_field, local_index, axis=1)  81.4 us
    reduce_sum x6, other arithmetic, advance(): inflow = jnp.sum(flux_faces[:, None, :, :] * edge_value, axis=2)  79.8 us
    all_to_all x8, starting transfers between devices, copy_for_each(): return lax.all_to_all(copies, axis, split_axis=0, concat_axis=0, tiled=True)  56 us
    select_n x6, local copies, waits for them, and re-layouts, advance(): jnp.take(halo_values, halo_index, axis=1)  54.5 us
    select_n x6, local copies, waits for them, and re-layouts, advance(): jnp.take(flat_field, local_index, axis=1)  54.2 us
  transfers between devices with their start and end apart: 8, of which 2 were waited for; matrix products, arithmetic and copies ran while one was open for 40% of the time, Pallas kernels for 0%

commit v1 on v0

v1 whole, which is shorter than its diff:
```python
import functools
import jax
import jax.numpy as jnp
from jax import lax
from jax.experimental import pallas as pl
from jax.experimental.pallas import tpu as pltpu
from jax.sharding import PartitionSpec as P

HOURS = 2
STEPS = 6
LANES = 128
SMEM = pltpu.MemorySpace.SMEM
VMEM = pltpu.MemorySpace.VMEM

OWN, EDGE, CARRY, RATIO, INV = 0, 1, 4, 5, 6
KINDS = 7


def pick_lanes(values, lanes):
    return jnp.take_along_axis(values, lanes, axis=1, mode="promise_in_bounds")


def send_pieces(send_ref, lanes_ref, load, layers, peers):
    part = lax.broadcasted_iota(jnp.int32, (8, LANES), 1) // 32
    inside = [part == j for j in range(1, 4)]

    def one(r, carry):
        lanes = lanes_ref[r]
        for g in range(layers // 4):
            piece = pick_lanes(load(4 * g), lanes)
            for j in range(1, 4):
                piece = jnp.where(inside[j - 1], pick_lanes(load(4 * g + j), lanes), piece)
            send_ref[r, g] = piece
        return carry

    lax.fori_loop(0, peers, one, 0)


def pack_kernel(rim_ref, lanes_ref, send_ref):
    send_pieces(send_ref, lanes_ref, lambda l: rim_ref[l], rim_ref.shape[0], send_ref.shape[0])


def prepare_kernel(panel_ref, coef_ref):
    blocks, layers = coef_ref.shape[0], coef_ref.shape[2]
    mix = 3 * layers
    zero = jnp.zeros((1, LANES), jnp.float32)
    for start in range(0, blocks, 8):
        group = range(start, start + 8)
        ratio = {b: zero for b in group}
        lower = {b: zero for b in group}
        for l in range(layers):
            for b in group:
                upper = panel_ref[b, mix + l : mix + l + 1, :]
                pivot = 1.0 + lower[b] + upper - lower[b] * ratio[b]
                inverse = 1.0 / pivot
                coef_ref[b, INV, l : l + 1, :] = inverse
                coef_ref[b, CARRY, l : l + 1, :] = lower[b] * inverse
                ratio[b] = upper * inverse
                lower[b] = upper

    def fill(b, carry):
        inverse = coef_ref[b, INV]
        coef_ref[b, RATIO] = panel_ref[b, mix : mix + layers, :] * inverse
        outflow = jnp.zeros((layers, LANES), jnp.float32)
        for f in range(3):
            flux = panel_ref[b, f * layers : (f + 1) * layers, :]
            outflow = outflow + jnp.maximum(flux, 0.0)
            coef_ref[b, EDGE + f] = -jnp.minimum(flux, 0.0) * inverse
        coef_ref[b, OWN] = (1.0 - outflow) * inverse
        return carry

    lax.fori_loop(0, blocks, fill, 0)


def row(coef_ref, c, kind, l):
    return coef_ref[c, kind, pl.ds(l, 8, stride=0), :]


def advect_block(plan_ref, field_ref, halo_ref, coef_ref, near_ref, rate_ref, acc_ref, i, b, c, n):
    layers = field_ref.shape[0]
    local_blocks = field_ref.shape[2] // LANES
    width = plan_ref.shape[1]
    for l in range(layers):
        acc_ref[i, l] = jnp.zeros((8, LANES), jnp.float32)

    @pl.when(plan_ref[b, width - 1] > 0)
    def _():
        cell = b * LANES + lax.broadcasted_iota(jnp.int32, (8, LANES), 1)
        here = near_ref[n, 3] == cell
        for l in range(layers):
            acc_ref[i, l] = jnp.where(here, rate_ref[l], 0.0) * row(coef_ref, c, INV, l)

    def add_from(source_ref, first):
        def one(k, carry):
            s = plan_ref[b, k]
            place = pl.ds(pl.multiple_of((s - first) * LANES, LANES), LANES)
            lanes = [near_ref[n, f] & (LANES - 1) for f in range(3)]
            inside = [(near_ref[n, f] >> 7) == s for f in range(3)]
            for l in range(layers):
                values = source_ref[l, :, place]
                total = acc_ref[i, l]
                for f in range(3):
                    edge = jnp.where(inside[f], pick_lanes(values, lanes[f]), 0.0)
                    total = total + row(coef_ref, c, EDGE + f, l) * edge
                acc_ref[i, l] = total
            return carry

        return one

    local_count, all_count = plan_ref[b, width - 3], plan_ref[b, width - 2]
    lax.fori_loop(0, local_count, add_from(field_ref, 0), 0)
    lax.fori_loop(local_count, all_count, add_from(halo_ref, local_blocks), 0)


def solve_blocks(field_ref, coef_ref, acc_ref, out_ref, where, where_coef, where_out):
    layers = field_ref.shape[0]
    places = [pl.ds(pl.multiple_of(b * LANES, LANES), LANES) for b in where]
    outs = [pl.ds(pl.multiple_of(b * LANES, LANES), LANES) for b in where_out]
    part = [None] * len(where)
    for l in range(layers):
        for i, place in enumerate(places):
            c = where_coef[i]
            now = row(coef_ref, c, OWN, l) * field_ref[l, :, place] + acc_ref[i, l]
            if l > 0:
                now = now + row(coef_ref, c, CARRY, l) * part[i]
            part[i] = now
            if l < layers - 1:
                acc_ref[i, l] = now
            else:
                out_ref[l, :, outs[i]] = now
    for l in range(layers - 2, -1, -1):
        for i in range(len(places)):
            part[i] = acc_ref[i, l] + row(coef_ref, where_coef[i], RATIO, l) * part[i]
            out_ref[l, :, outs[i]] = part[i]


def rim_kernel(
    last, plan_ref, field_ref, received_ref, coef_ref, near_ref, rate_ref, lanes_ref, *refs
):
    if last:
        halo_ref, new_ref, acc_ref = refs
    else:
        send_ref, halo_ref, new_ref, acc_ref = refs
    layers = field_ref.shape[0]
    block = field_ref.shape[2] // LANES - 1
    lane = lax.broadcasted_iota(jnp.int32, (8, LANES), 1)
    part, slot = lane // 32, lane % 32
    inside = [part == k for k in range(1, 4)]
    moved = [slot + 32 * j for j in range(4)]
    quads = received_ref.shape[0] // 4

    def unpack(g, carry):
        for q in range(quads):
            pieces = [received_ref[4 * q + k, g] for k in range(4)]
            for j in range(4):
                value = pick_lanes(pieces[0], moved[j])
                for k in range(1, 4):
                    value = jnp.where(inside[k - 1], pick_lanes(pieces[k], moved[j]), value)
                halo_ref[4 * g + j, :, q * LANES : (q + 1) * LANES] = value
        return carry

    lax.fori_loop(0, layers // 4, unpack, 0)
    advect_block(
        plan_ref, field_ref, halo_ref, coef_ref, near_ref, rate_ref, acc_ref, 0, block, 0, 0
    )
    solve_blocks(field_ref, coef_ref, acc_ref, new_ref, [block], [0], [0])
    if not last:
        send_pieces(send_ref, lanes_ref, lambda l: new_ref[l], layers, send_ref.shape[0])


GROUP = 5


def bulk_kernel(
    plan_ref, field_ref, halo_ref, rim_ref, coef_ref, near_ref, rate_ref, out_ref, acc_ref
):
    blocks = field_ref.shape[2] // LANES

    def group(g, carry):
        def advect(i, inner):
            b = g * GROUP + i
            advect_block(
                plan_ref, field_ref, halo_ref, coef_ref, near_ref, rate_ref, acc_ref, i, b, b, b
            )
            return inner

        lax.fori_loop(0, GROUP, advect, 0)
        where = [g * GROUP + i for i in range(GROUP)]
        solve_blocks(field_ref, coef_ref, acc_ref, out_ref, where, where, where)
        return carry

    lax.fori_loop(0, (blocks - 1) // GROUP, group, 0)
    out_ref[:, :, (blocks - 1) * LANES :] = rim_ref[...]


def share(value, axis):
    copies = jnp.broadcast_to(value, (lax.axis_size(axis), *value.shape))
    return lax.all_to_all(copies, axis, 0, 0, tiled=True)


def on_device(
    concentration, courant, diffusivity, release_rate, release_cell, neighbour, send_rows
):
    layers, tracers, cells = concentration.shape
    blocks = cells // LANES
    peers, slots = send_rows.shape[1], send_rows.shape[2]
    halo_cells = peers * slots
    rim = 64
    f32 = jnp.float32
    full = pl.BlockSpec(memory_space=VMEM)
    scalars = pl.BlockSpec(memory_space=SMEM)
    message = jax.ShapeDtypeStruct((peers, layers // 4, tracers, LANES), f32)

    def params(mib):
        return pltpu.CompilerParams(vmem_limit_bytes=mib << 20)

    def panel(h):
        empty = jnp.zeros((1, LANES), f32)
        rows = jnp.concatenate([courant[h].reshape(-1, LANES), diffusivity[h], empty], 0)
        return rows

    rows = LANES - rim + jnp.maximum(send_rows[0], 0)
    lanes = jnp.broadcast_to(jnp.tile(rows, (1, LANES // slots))[:, None, :], (peers, 8, LANES))

    send = pl.pallas_call(
        pack_kernel,
        out_shape=message,
        grid=(1,),
        in_specs=[
            pl.BlockSpec((layers, tracers, LANES), lambda i: (0, 0, blocks - 1)),
            pl.BlockSpec((peers, 8, LANES), lambda i: (0, 0, 0)),
        ],
        out_specs=pl.BlockSpec(message.shape, lambda i: (0, 0, 0, 0)),
        name="pack",
    )(concentration, lanes)
    received = lax.all_to_all(send, "region", 0, 0, tiled=True)
    tables = [share(panel(0), "tracer"), None]

    sources = blocks + halo_cells // LANES
    of_block = neighbour.reshape(3, blocks, LANES)
    source_id = jnp.arange(sources, dtype=jnp.int32)
    needed = jnp.any((of_block[..., None] >> 7) == source_id, axis=(0, 2))
    rank = jnp.sum(
        needed[:, None, :] & (source_id[None, None, :] < source_id[None, :, None]), axis=2
    )
    listed = jnp.sum(
        jnp.where(
            needed[:, None, :] & (rank[:, None, :] == source_id[None, :, None]),
            source_id[None, None, :],
            0,
        ),
        axis=2,
    )
    home = release_cell - lax.axis_index("region") * cells
    released = jnp.any(
        (home[None, :] >> 7) == jnp.arange(blocks, dtype=jnp.int32)[:, None], axis=1
    )
    plan = jnp.concatenate(
        [
            listed,
            jnp.sum(needed[:, :blocks], axis=1)[:, None],
            jnp.sum(needed, axis=1)[:, None],
            released[:, None],
        ],
        axis=1,
    ).astype(jnp.int32)
    near = jnp.concatenate(
        [
            jnp.broadcast_to(jnp.moveaxis(of_block, 1, 0)[:, :, None, :], (blocks, 3, 8, LANES)),
            jnp.broadcast_to(home[None, None, :, None], (blocks, 1, 8, LANES)),
        ],
        axis=1,
    )
    rate = jnp.broadcast_to(release_rate[:, :, None], (layers, tracers, LANES))

    coef_shape = (blocks, KINDS, layers, LANES)

    def prepare(table):
        return pl.pallas_call(
            prepare_kernel,
            out_shape=jax.ShapeDtypeStruct(coef_shape, f32),
            in_specs=[full],
            out_specs=full,
            compiler_params=params(32),
            name="prepare",
        )(table)

    new_block = jax.ShapeDtypeStruct((layers, tracers, LANES), f32)
    halo_shape = jax.ShapeDtypeStruct((layers, tracers, halo_cells), f32)

    def whole(shape):
        return pl.BlockSpec(shape, lambda i, n=len(shape): (0,) * n)

    def rim_step(field, received, coef, last):
        outs = (halo_shape, new_block) if last else (message, halo_shape, new_block)
        result = pl.pallas_call(
            functools.partial(rim_kernel, last),
            out_shape=outs,
            grid=(1,),
            in_specs=[
                scalars,
                whole(field.shape),
                whole(received.shape),
                pl.BlockSpec((1, *coef_shape[1:]), lambda i: (blocks - 1, 0, 0, 0)),
                pl.BlockSpec((1, 4, 8, LANES), lambda i: (blocks - 1, 0, 0, 0)),
                whole(rate.shape),
                whole(lanes.shape),
            ],
            out_specs=tuple(whole(o.shape) for o in outs),
            scratch_shapes=[pltpu.VMEM((1, layers, tracers, LANES), f32)],
            compiler_params=params(32),
            name="rim",
        )(plan, field, received, coef, near, rate, lanes)
        return result if not last else (None, *result)

    def bulk_step(field, halo, new, coef):
        return pl.pallas_call(
            bulk_kernel,
            out_shape=jax.ShapeDtypeStruct(field.shape, f32),
            in_specs=[scalars] + [full] * 6,
            out_specs=full,
            scratch_shapes=[pltpu.VMEM((GROUP, layers, tracers, LANES), f32)],
            compiler_params=params(32),
            name="bulk",
        )(plan, field, halo, new, coef, near, rate)

    field = concentration
    per_hour = STEPS // HOURS
    coef = None
    for step in range(STEPS):
        h = step // per_hour
        if step % per_hour == 0:
            coef = prepare(tables[h])
        last = step == STEPS - 1
        send, halo, new = rim_step(field, received, coef, last)
        if step == 0:
            later = panel(1)
            later, _ = lax.optimization_barrier((later, new))
            tables[1] = share(later, "tracer")
        if not last:
            received = lax.all_to_all(send, "region", 0, 0, tiled=True)
        field = bulk_step(field, halo, new, coef)
    return field


def solution(mesh):
    both = ("region", "tracer")
    return jax.shard_map(
        on_device,
        mesh=mesh,
        in_specs=(
            P(None, "tracer", "region"),
            P(None, None, None, both),
            P(None, None, both),
            P(None, "tracer"),
            P("tracer"),
            P(None, "region"),
            P("region", None, None),
        ),
        out_specs=P(None, "tracer", "region"),
        check_vma=False,
    )
```

time: 992 us -> 316 us (0.32)
  local copies, waits for them, and re-layouts: 637 us -> 52.9 us
  other arithmetic: 237 us -> 1.7 us
  Pallas kernels: 0 us -> 159 us
  waiting for transfers between devices: 29.6 us -> 49.8 us
  blocking collectives: 19.4 us -> 0 us
    gather x18 -> x0, local copies, waits for them, and re-layouts: 310 us -> none  [the longest x6 146 us: advance(): jnp.take(flat_field, local_index, axis=1)]
    reshape x20 -> x0, local copies, waits for them, and re-layouts: 177 us -> none  [the longest x6 81.6 us: advance(): jnp.take(halo_values, halo_index, axis=1)]
    pallas_call x0 -> x15, Pallas kernels: none -> 159 us  [the longest x6 113 us: bulk_step(): pl.pallas_call(bulk_kernel, out_shape=jax.ShapeDtypeStruct(field.shape, f...]
    select_n x12 -> x0, local copies, waits for them, and re-layouts: 109 us -> none  [the longest x6 54.5 us: advance(): jnp.take(halo_values, halo_index, axis=1)]
    select_n x24 -> x0, other arithmetic: 108 us -> none  [the longest x6 51.7 us: advance(): jnp.take(flat_field, local_index, axis=1)]
    reduce_sum x7 -> x4, other arithmetic: 80.8 us -> 0.97 us  [the longest x1 0.42 us: on_device(): jnp.sum(jnp.where(needed[:, None, :] & (rank[:, None, :] == source_id[Non...]
    unnamed x28 -> x101, local copies, waits for them, and re-layouts: 9.58 us -> 47.3 us
    all_to_all x8, waiting for transfers between devices: 29.6 us -> 49.8 us  [the longest x6 35.8 us: on_device(): received = lax.all_to_all(send, 'region', 0, 0, tiled=True)]
  transfers between devices with their start and end apart: 8 -> 8, of which waited for: 2 -> 3; matrix products, arithmetic and copies ran while one was open for 40% -> 1% of each run, Pallas kernels for 0% -> 34%
where the time goes in v1:
time: 316 us; the launch traced here: 315 us
  Pallas kernels  159 us (50%)
  local copies, waits for them, and re-layouts  52.9 us (17%)
  starting transfers between devices  51.1 us (16%)
  waiting for transfers between devices  49.8 us (16%)
    pallas_call x6, Pallas kernels, bulk_step(): pl.pallas_call(bulk_kernel, out_shape=jax.ShapeDtypeStruct(field.shape, f...  113 us
    unnamed x101, local copies, waits for them, and re-layouts  47.3 us
    all_to_all x6, starting transfers between devices, on_device(): received = lax.all_to_all(send, 'region', 0, 0, tiled=True)  39.1 us
    pallas_call x6, Pallas kernels, rim_step(): pl.pallas_call(functools.partial(rim_kernel, last), out_shape=outs, grid=...  38.9 us
    all_to_all x6, waiting for transfers between devices, on_device(): received = lax.all_to_all(send, 'region', 0, 0, tiled=True)  35.8 us
    all_to_all x2, waiting for transfers between devices, share(): return lax.all_to_all(copies, axis, 0, 0, tiled=True)  14.1 us
    all_to_all x2, starting transfers between devices, share(): return lax.all_to_all(copies, axis, 0, 0, tiled=True)  12 us
  transfers between devices with their start and end apart: 8, of which 3 were waited for; matrix products, arithmetic and copies ran while one was open for 1% of the time, Pallas kernels for 34%

profile of v1, /device:TPU:1, one launch (start us, length us, event | category | flops | bytes accessed | tf_op | source)
XLA Modules:
  0.0 314.7 jit_solution(7935402652257674783)
XLA Ops:
  0.0 0.9 fusion.4
  0.9 0.9 fusion.3
  2.0 1.2 broadcast_in_dim.33
  3.1 7.6 %all-to-all-start.1 = ((f32[16,160,128]{2,1,0:T(8,128)}), f32[16,160,128]{2,1,0:T(8,128)S(1)}, u32[]{:S(2)}, u32[]{:S(2)}) async-start(f32[16,160,128]{2,1,0:T(8,128)} %broadcast_in_dim.33), calls=%async_computation.1 | async-start | bytes 2621440 | tf_op jit(solution)/shard_map/all_to_all | solution.py:198
  12.0 3.6 %pack.1 = f32[16,10,8,128]{3,2,1,0:T(8,128)} custom-call(f32[40,8,2048]{2,1,0:T(8,128)} %field_ref.3, s32[16,8,128]{2,1,0:T(8,128)} %broadcast_in_dim.32.lanes_ref), custom_call_target="tpu_custom_call" | custom-call | tf_op jit(solution)/shard_map/pack/pallas_call | solution.py:225
  15.6 14.1 %all-to-all-done.1.panel_ref = f32[16,160,128]{2,1,0:T(8,128)S(1)} async-done(((f32[16,160,128]{2,1,0:T(8,128)}), f32[16,160,128]{2,1,0:T(8,128)S(1)}, u32[]{:S(2)}, u32[]{:S(2)}) %all-to-all-start.1) | async-done | bytes 1310752 | tf_op jit(solution)/shard_map/all_to_all | solution.py:198
  29.7 11.4 %all-to-all-start = ((f32[16,10,8,128]{3,2,1,0:T(8,128)}), f32[16,10,8,128]{3,2,1,0:T(8,128)S(1)}, u32[]{:S(2)}, u32[]{:S(2)}) async-start(f32[16,10,8,128]{3,2,1,0:T(8,128)} %pack.1), calls=%async_computation | async-start | bytes 1310720 | tf_op jit(solution)/shard_map/all_to_all | solution.py:236
  42.9 1.3 copy-done.19
  44.2 1.0 prepare.2.coef_ref
  45.2 15.8 %all-to-all-done.received_ref = f32[16,10,8,128]{3,2,1,0:T(8,128)S(1)} async-done(((f32[16,10,8,128]{3,2,1,0:T(8,128)}), f32[16,10,8,128]{3,2,1,0:T(8,128)S(1)}, u32[]{:S(2)}, u32[]{:S(2)}) %all-to-all-start) | async-done | bytes 655392 | tf_op jit(solution)/shard_map/all_to_all | solution.py:236
  61.1 1.7 copy-done.16
  62.9 6.8 %rim.6 = (f32[16,10,8,128]{3,2,1,0:T(8,128)S(1)}, f32[40,8,512]{2,1,0:T(8,128)S(1)}, f32[40,8,128]{2,1,0:T(8,128)S(1)}) custom-call(s32[16,23]{1,0:T(8,128)S(1)} %pad_add_fusion.1.plan_ref, f32[40,8,2048]{2,1,0:T(8,128)S(1)} %copy-done.16, f32[16,10,8,128]{3,2,1,0:T(8,128)S(1)} %all-to-all-done.received_ref, f32[16,7,40,128]{3,2,1,0:T(8,128)S(1)} %prepare.2.coef_ref, ...), custom_call_target="tpu_custom_call" | custom-call | tf_op jit(solution)/shard_map/rim/pallas_call | solution.py:296
  70.5 0.8 copy-done.34
  72.0 3.5 %all-to-all-start.2 = ((f32[16,10,8,128]{3,2,1,0:T(8,128)}), f32[16,10,8,128]{3,2,1,0:T(8,128)S(1)}, u32[]{:S(2)}, u32[]{:S(2)}) async-start(f32[16,10,8,128]{3,2,1,0:T(8,128)} %copy-done.34), calls=%async_computation.2 | async-start | bytes 1310720 | tf_op jit(solution)/shard_map/all_to_all | solution.py:341
  75.5 1.7 copy-done.17
  77.3 1.1 copy-done.30
  78.4 0.9 copy-done.45
  79.3 18.6 %bulk.6.field_ref = f32[40,8,2048]{2,1,0:T(8,128)S(1)} custom-call(s32[16,23]{1,0:T(8,128)S(1)} %pad_add_fusion.1.plan_ref, f32[40,8,2048]{2,1,0:T(8,128)S(1)} %copy-done.17, f32[40,8,512]{2,1,0:T(8,128)S(1)} %copy-done.30, f32[40,8,128]{2,1,0:T(8,128)S(1)} %copy-done.45, f32[16,7,40,128]{3,2,1,0:T(8,128)S(1)} %prepare.2.coef_ref, ...), custom_call_target="tpu_custom_call" | custom-call | tf_op jit(solution)/shard_map/bulk/pallas_call | solution.py:317
  97.8 1.5 copy-done.3
  99.3 1.7 copy-done.4
  101.1 6.8 %rim.7 = (f32[16,10,8,128]{3,2,1,0:T(8,128)S(1)}, f32[40,8,512]{2,1,0:T(8,128)S(1)}, f32[40,8,128]{2,1,0:T(8,128)S(1)}) custom-call(s32[16,23]{1,0:T(8,128)S(1)} %pad_add_fusion.1.plan_ref, f32[40,8,2048]{2,1,0:T(8,128)S(1)} %copy-done.4, f32[16,10,8,128]{3,2,1,0:T(8,128)S(1)} %all-to-all-done.2.received_ref, f32[16,7,40,128]{3,2,1,0:T(8,128)S(1)} %prepare.2.coef_ref, ...), custom_call_target="tpu_custom_call" | custom-call | tf_op jit(solution)/shard_map/rim/pallas_call | solution.py:296
  107.9 0.8 copy-done.21
  108.7 0.8 copy-done.35
  110.2 6.8 %all-to-all-start.3 = ((f32[16,10,8,128]{3,2,1,0:T(8,128)}), f32[16,10,8,128]{3,2,1,0:T(8,128)S(1)}, u32[]{:S(2)}, u32[]{:S(2)}) async-start(f32[16,10,8,128]{3,2,1,0:T(8,128)} %copy-done.35), calls=%async_computation.3 | async-start | bytes 1310720 | tf_op jit(solution)/shard_map/all_to_all | solution.py:341
  117.0 19.9 %all-to-all-done.3.received_ref = f32[16,10,8,128]{3,2,1,0:T(8,128)S(1)} async-done(((f32[16,10,8,128]{3,2,1,0:T(8,128)}), f32[16,10,8,128]{3,2,1,0:T(8,128)S(1)}, u32[]{:S(2)}, u32[]{:S(2)}) %all-to-all-start.3) | async-done | bytes 655392 | tf_op jit(solution)/shard_map/all_to_all | solution.py:341
  136.9 1.2 broadcast_in_dim.37
  138.1 4.4 %all-to-all-start.5 = ((f32[16,160,128]{2,1,0:T(8,128)}), f32[16,160,128]{2,1,0:T(8,128)}, u32[]{:S(2)}, u32[]{:S(2)}) async-start(f32[16,160,128]{2,1,0:T(8,128)} %broadcast_in_dim.37), calls=%async_computation.5 | async-start | bytes 2621440 | tf_op jit(solution)/shard_map/all_to_all | solution.py:198
  142.5 1.7 copy-done.5
  144.3 1.1 copy-done.22
  145.4 0.9 copy-done.37
  146.3 18.6 %bulk.7.field_ref = f32[40,8,2048]{2,1,0:T(8,128)S(1)} custom-call(s32[16,23]{1,0:T(8,128)S(1)} %pad_add_fusion.1.plan_ref, f32[40,8,2048]{2,1,0:T(8,128)S(1)} %copy-done.5, f32[40,8,512]{2,1,0:T(8,128)S(1)} %copy-done.22, f32[40,8,128]{2,1,0:T(8,128)S(1)} %copy-done.37, f32[16,7,40,128]{3,2,1,0:T(8,128)S(1)} %prepare.2.coef_ref, ...), custom_call_target="tpu_custom_call" | custom-call | tf_op jit(solution)/shard_map/bulk/pallas_call | solution.py:317
  164.8 6.8 %rim.8 = (f32[16,10,8,128]{3,2,1,0:T(8,128)S(1)}, f32[40,8,512]{2,1,0:T(8,128)S(1)}, f32[40,8,128]{2,1,0:T(8,128)S(1)}) custom-call(s32[16,23]{1,0:T(8,128)S(1)} %pad_add_fusion.1.plan_ref, f32[40,8,2048]{2,1,0:T(8,128)S(1)} %bulk.7.field_ref, f32[16,10,8,128]{3,2,1,0:T(8,128)S(1)} %all-to-all-done.3.received_ref, f32[16,7,40,128]{3,2,1,0:T(8,128)S(1)} %prepare.2.coef_ref, ...), custom_call_target="tpu_custom_call" | custom-call | tf_op jit(solution)/shard_map/rim/pallas_call | solution.py:296
  171.6 1.5 copy-done.6
  173.1 0.8 copy-done.23
  174.0 0.8 copy-done.31
  175.5 3.5 %all-to-all-start.4 = ((f32[16,10,8,128]{3,2,1,0:T(8,128)}), f32[16,10,8,128]{3,2,1,0:T(8,128)S(1)}, u32[]{:S(2)}, u32[]{:S(2)}) async-start(f32[16,10,8,128]{3,2,1,0:T(8,128)} %copy-done.31), calls=%async_computation.4 | async-start | bytes 1310720 | tf_op jit(solution)/shard_map/all_to_all | solution.py:341
  179.0 2.4 prepare.3.coef_ref
  181.5 1.4 copy-done
  182.8 18.6 %bulk.8.field_ref = f32[40,8,2048]{2,1,0:T(8,128)S(1)} custom-call(s32[16,23]{1,0:T(8,128)S(1)} %pad_add_fusion.1.plan_ref, f32[40,8,2048]{2,1,0:T(8,128)S(1)} %copy-done.7, f32[40,8,512]{2,1,0:T(8,128)S(1)} %copy-done.24, f32[40,8,128]{2,1,0:T(8,128)S(1)} %copy-done.39, f32[16,7,40,128]{3,2,1,0:T(8,128)S(1)} %prepare.2.coef_ref, ...), custom_call_target="tpu_custom_call" | custom-call | tf_op jit(solution)/shard_map/bulk/pallas_call | solution.py:317
  201.4 1.5 copy-done.8
  202.9 1.6 copy-done.1
  204.6 1.7 copy-done.9
  206.3 6.8 %rim.9 = (f32[16,10,8,128]{3,2,1,0:T(8,128)S(1)}, f32[40,8,512]{2,1,0:T(8,128)S(1)}, f32[40,8,128]{2,1,0:T(8,128)S(1)}) custom-call(s32[16,23]{1,0:T(8,128)S(1)} %pad_add_fusion.1.plan_ref, f32[40,8,2048]{2,1,0:T(8,128)S(1)} %copy-done.9, f32[16,10,8,128]{3,2,1,0:T(8,128)S(1)} %all-to-all-done.4.received_ref, f32[16,7,40,128]{3,2,1,0:T(8,128)S(1)} %copy-done.1, ...), custom_call_target="tpu_custom_call" | custom-call | tf_op jit(solution)/shard_map/rim/pallas_call | solution.py:296
  213.1 0.8 copy-done.25
  213.9 0.8 copy-done.32
  215.4 6.8 %all-to-all-start.6 = ((f32[16,10,8,128]{3,2,1,0:T(8,128)}), f32[16,10,8,128]{3,2,1,0:T(8,128)S(1)}, u32[]{:S(2)}, u32[]{:S(2)}) async-start(f32[16,10,8,128]{3,2,1,0:T(8,128)} %copy-done.32), calls=%async_computation.6 | async-start | bytes 1310720 | tf_op jit(solution)/shard_map/all_to_all | solution.py:341
  222.2 1.7 copy-done.10
  223.9 1.1 copy-done.26
  225.0 0.9 copy-done.41
  225.9 18.6 %bulk.9.field_ref = f32[40,8,2048]{2,1,0:T(8,128)S(1)} custom-call(s32[16,23]{1,0:T(8,128)S(1)} %pad_add_fusion.1.plan_ref, f32[40,8,2048]{2,1,0:T(8,128)S(1)} %copy-done.10, f32[40,8,512]{2,1,0:T(8,128)S(1)} %copy-done.26, f32[40,8,128]{2,1,0:T(8,128)S(1)} %copy-done.41, f32[16,7,40,128]{3,2,1,0:T(8,128)S(1)} %copy-done.2, ...), custom_call_target="tpu_custom_call" | custom-call | tf_op jit(solution)/shard_map/bulk/pallas_call | solution.py:317
  244.5 1.5 copy-done.11
  246.0 1.7 copy-done.12
  247.7 6.8 %rim.10 = (f32[16,10,8,128]{3,2,1,0:T(8,128)S(1)}, f32[40,8,512]{2,1,0:T(8,128)S(1)}, f32[40,8,128]{2,1,0:T(8,128)S(1)}) custom-call(s32[16,23]{1,0:T(8,128)S(1)} %pad_add_fusion.1.plan_ref, f32[40,8,2048]{2,1,0:T(8,128)S(1)} %copy-done.12, f32[16,10,8,128]{3,2,1,0:T(8,128)S(1)} %all-to-all-done.6.received_ref, f32[16,7,40,128]{3,2,1,0:T(8,128)S(1)} %copy-done.2, ...), custom_call_target="tpu_custom_call" | custom-call | tf_op jit(solution)/shard_map/rim/pallas_call | solution.py:296
  254.5 0.8 copy-done.27
  255.4 0.8 copy-done.33
  256.9 7.2 %all-to-all-start.7 = ((f32[16,10,8,128]{3,2,1,0:T(8,128)}), f32[16,10,8,128]{3,2,1,0:T(8,128)S(1)}, u32[]{:S(2)}, u32[]{:S(2)}) async-start(f32[16,10,8,128]{3,2,1,0:T(8,128)} %copy-done.33), calls=%async_computation.7 | async-start | bytes 1310720 | tf_op jit(solution)/shard_map/all_to_all | solution.py:341
  264.1 1.7 copy-done.13
  265.8 1.1 copy-done.28
  266.9 0.9 copy-done.43
  267.8 18.6 %bulk.10.field_ref = f32[40,8,2048]{2,1,0:T(8,128)S(1)} custom-call(s32[16,23]{1,0:T(8,128)S(1)} %pad_add_fusion.1.plan_ref, f32[40,8,2048]{2,1,0:T(8,128)S(1)} %copy-done.13, f32[40,8,512]{2,1,0:T(8,128)S(1)} %copy-done.28, f32[40,8,128]{2,1,0:T(8,128)S(1)} %copy-done.43, f32[16,7,40,128]{3,2,1,0:T(8,128)S(1)} %copy-done.2, ...), custom_call_target="tpu_custom_call" | custom-call | tf_op jit(solution)/shard_map/bulk/pallas_call | solution.py:317
  286.4 1.5 copy-done.14
  287.9 1.7 copy-done.15
  289.6 5.0 %rim.11 = (f32[40,8,512]{2,1,0:T(8,128)S(1)}, f32[40,8,128]{2,1,0:T(8,128)S(1)}) custom-call(s32[16,23]{1,0:T(8,128)S(1)} %pad_add_fusion.1.plan_ref, f32[40,8,2048]{2,1,0:T(8,128)S(1)} %copy-done.15, f32[16,10,8,128]{3,2,1,0:T(8,128)S(1)} %all-to-all-done.7.received_ref, f32[16,7,40,128]{3,2,1,0:T(8,128)S(1)} %copy-done.2, ...), custom_call_target="tpu_custom_call" | custom-call | tf_op jit(solution)/shard_map/rim/pallas_call | solution.py:296
  294.6 20.1 %bulk.11 = f32[40,8,2048]{2,1,0:T(8,128)} custom-call(s32[16,23]{1,0:T(8,128)S(1)} %pad_add_fusion.1.plan_ref, f32[40,8,2048]{2,1,0:T(8,128)S(1)} %copy-done.15, f32[40,8,512]{2,1,0:T(8,128)S(1)} %get-tuple-element.39.halo_ref, f32[40,8,128]{2,1,0:T(8,128)S(1)} %get-tuple-element.40.rim_ref, f32[16,7,40,128]{3,2,1,0:T(8,128)S(1)} %copy-done.2, ...), custom_call_target="tpu_custom_call" | custom-call | tf_op jit(solution)/shard_map/bulk/pallas_call | solution.py:317
  (100 shorter events, 7.5 us)
Async XLA Ops:
  0.0 10.7 %copy-start.46 = (s32[3,2048]{1,0:T(4,128)S(1)}, s32[3,2048]{1,0:T(4,128)}, u32[]{:S(2)}) copy-start(s32[3,2048]{1,0:T(4,128)} %param.12) | copy-start | bytes 73732
  0.0 11.3 %copy-start.47 = (s32[1,16,32]{2,1,0:T(8,128)S(1)}, s32[1,16,32]{2,1,0:T(8,128)}, u32[]{:S(2)}) copy-start(s32[1,16,32]{2,1,0:T(8,128)} %param.13) | copy-start | bytes 6148
  3.1 26.5 %all-to-all-start.1 = ((f32[16,160,128]{2,1,0:T(8,128)}), f32[16,160,128]{2,1,0:T(8,128)S(1)}, u32[]{:S(2)}, u32[]{:S(2)}) async-start(f32[16,160,128]{2,1,0:T(8,128)} %broadcast_in_dim.33), calls=%async_computation.1 | async-start | bytes 2621440 | tf_op jit(solution)/shard_map/all_to_all | solution.py:198
  10.7 31.7 %copy-start.49 = (s32[8]{0:T(128)S(1)}, s32[8]{0:T(128)}, u32[]{:S(2)}) copy-start(s32[8]{0:T(128)} %param.11) | copy-start | bytes 100
  10.7 31.9 %copy-start.48 = (f32[40,8]{0,1:T(8,128)S(1)}, f32[40,8]{0,1:T(8,128)}, u32[]{:S(2)}) copy-start(f32[40,8]{0,1:T(8,128)} %param.10) | copy-start | bytes 3844
  29.7 13.2 %copy-start.18 = (f32[16,160,128]{2,1,0:T(8,128)}, f32[16,160,128]{2,1,0:T(8,128)S(1)}, u32[]{:S(2)}) copy-start(f32[16,160,128]{2,1,0:T(8,128)S(1)} %all-to-all-done.1.panel_ref) | copy-start | bytes 3932164
  29.7 31.3 %all-to-all-start = ((f32[16,10,8,128]{3,2,1,0:T(8,128)}), f32[16,10,8,128]{3,2,1,0:T(8,128)S(1)}, u32[]{:S(2)}, u32[]{:S(2)}) async-start(f32[16,10,8,128]{3,2,1,0:T(8,128)} %pack.1), calls=%async_computation | async-start | bytes 1310720 | tf_op jit(solution)/shard_map/all_to_all | solution.py:236
  41.1 20.0 %copy-start.20 = (s32[16,8,128]{2,1,0:T(8,128)S(1)}, s32[16,8,128]{2,1,0:T(8,128)}, u32[]{:S(2)}) copy-start(s32[16,8,128]{2,1,0:T(8,128)} %broadcast_in_dim.32.lanes_ref) | copy-start | bytes 196612
  42.9 1.3 copy-start.19
  61.1 1.7 copy-start.16
  69.7 0.8 copy-start.29
  70.5 0.8 copy-start.34
  71.4 0.7 copy-start.44
  72.0 27.3 %all-to-all-start.2 = ((f32[16,10,8,128]{3,2,1,0:T(8,128)}), f32[16,10,8,128]{3,2,1,0:T(8,128)S(1)}, u32[]{:S(2)}, u32[]{:S(2)}) async-start(f32[16,10,8,128]{3,2,1,0:T(8,128)} %copy-done.34), calls=%async_computation.2 | async-start | bytes 1310720 | tf_op jit(solution)/shard_map/all_to_all | solution.py:341
  75.5 1.7 copy-start.17
  77.3 1.1 copy-start.30
  78.3 0.9 copy-start.45
  97.8 1.5 copy-start.3
  99.3 1.7 copy-start.4
  107.9 0.9 copy-start.21
  108.7 0.8 copy-start.35
  109.6 0.6 copy-start.36
  110.2 26.7 %all-to-all-start.3 = ((f32[16,10,8,128]{3,2,1,0:T(8,128)}), f32[16,10,8,128]{3,2,1,0:T(8,128)S(1)}, u32[]{:S(2)}, u32[]{:S(2)}) async-start(f32[16,10,8,128]{3,2,1,0:T(8,128)} %copy-done.35), calls=%async_computation.3 | async-start | bytes 1310720 | tf_op jit(solution)/shard_map/all_to_all | solution.py:341
  138.1 37.4 %all-to-all-start.5 = ((f32[16,160,128]{2,1,0:T(8,128)}), f32[16,160,128]{2,1,0:T(8,128)}, u32[]{:S(2)}, u32[]{:S(2)}) async-start(f32[16,160,128]{2,1,0:T(8,128)} %broadcast_in_dim.37), calls=%async_computation.5 | async-start | bytes 2621440 | tf_op jit(solution)/shard_map/all_to_all | solution.py:198
  142.5 1.7 copy-start.5
  144.3 1.1 copy-start.22
  145.4 0.9 copy-start.37
  171.6 1.5 copy-start.6
  173.1 0.8 copy-start.23
  174.0 0.8 copy-start.31
  174.8 0.7 copy-start.38
  175.5 27.4 %all-to-all-start.4 = ((f32[16,10,8,128]{3,2,1,0:T(8,128)}), f32[16,10,8,128]{3,2,1,0:T(8,128)S(1)}, u32[]{:S(2)}, u32[]{:S(2)}) async-start(f32[16,10,8,128]{3,2,1,0:T(8,128)} %copy-done.31), calls=%async_computation.4 | async-start | bytes 1310720 | tf_op jit(solution)/shard_map/all_to_all | solution.py:341
  179.0 3.9 %copy-start.7 = (f32[40,8,2048]{2,1,0:T(8,128)S(1)}, f32[40,8,2048]{2,1,0:T(8,128)}, u32[]{:S(2)}) copy-start(f32[40,8,2048]{2,1,0:T(8,128)} %copy-done.6) | copy-start | bytes 7864324
  179.0 3.8 %copy-start.24 = (f32[40,8,512]{2,1,0:T(8,128)S(1)}, f32[40,8,512]{2,1,0:T(8,128)}, u32[]{:S(2)}) copy-start(f32[40,8,512]{2,1,0:T(8,128)} %copy-done.23) | copy-start | bytes 1966084
  179.0 3.8 %copy-start.39 = (f32[40,8,128]{2,1,0:T(8,128)S(1)}, f32[40,8,128]{2,1,0:T(8,128)}, u32[]{:S(2)}) copy-start(f32[40,8,128]{2,1,0:T(8,128)} %copy-done.38) | copy-start | bytes 491524
  181.4 1.4 copy-start
  201.4 1.5 copy-start.8
  202.9 1.6 copy-start.1
  204.6 1.7 copy-start.9
  206.3 15.9 %copy-start.2 = (f32[16,7,40,128]{3,2,1,0:T(8,128)S(1)}, f32[16,7,40,128]{3,2,1,0:T(8,128)}, u32[]{:S(2)}) copy-start(f32[16,7,40,128]{3,2,1,0:T(8,128)} %copy-done) | copy-start | bytes 6881284
  213.1 0.8 copy-start.25
  213.9 0.8 copy-start.32
  214.8 0.7 copy-start.40
  215.4 30.6 %all-to-all-start.6 = ((f32[16,10,8,128]{3,2,1,0:T(8,128)}), f32[16,10,8,128]{3,2,1,0:T(8,128)S(1)}, u32[]{:S(2)}, u32[]{:S(2)}) async-start(f32[16,10,8,128]{3,2,1,0:T(8,128)} %copy-done.32), calls=%async_computation.6 | async-start | bytes 1310720 | tf_op jit(solution)/shard_map/all_to_all | solution.py:341
  222.2 1.7 copy-start.10
  223.9 1.1 copy-start.26
  225.0 0.9 copy-start.41
  244.5 1.5 copy-start.11
  246.0 1.7 copy-start.12
  254.5 0.8 copy-start.27
  255.4 0.8 copy-start.33
  256.2 0.7 copy-start.42
  256.9 31.0 %all-to-all-start.7 = ((f32[16,10,8,128]{3,2,1,0:T(8,128)}), f32[16,10,8,128]{3,2,1,0:T(8,128)S(1)}, u32[]{:S(2)}, u32[]{:S(2)}) async-start(f32[16,10,8,128]{3,2,1,0:T(8,128)} %copy-done.33), calls=%async_computation.7 | async-start | bytes 1310720 | tf_op jit(solution)/shard_map/all_to_all | solution.py:341
  264.1 1.7 copy-start.13
  265.8 1.1 copy-start.28
  266.9 0.9 copy-start.43
  286.4 1.5 copy-start.14
  287.9 1.7 copy-start.15

commit v2 on v1

v2 whole, which is shorter than its diff:
```python
import functools
import jax
import jax.numpy as jnp
from jax import lax
from jax.experimental import pallas as pl
from jax.experimental.pallas import tpu as pltpu
from jax.sharding import PartitionSpec as P

HOURS = 2
STEPS = 6
LANES = 128
SMEM = pltpu.MemorySpace.SMEM
VMEM = pltpu.MemorySpace.VMEM

OWN, EDGE, CARRY, RATIO, INV = 0, 1, 4, 5, 6
KINDS = 7


def pick_lanes(values, lanes):
    return jnp.take_along_axis(values, lanes, axis=1, mode="promise_in_bounds")


def turn_quarters(values):
    lane = lax.broadcasted_iota(jnp.int32, (8, LANES), 1)
    low = lane < 64
    even = (lane & 32) == 0
    a, b, c, d = values
    a, c = jnp.where(low, a, pltpu.roll(c, 64, 1)), jnp.where(low, pltpu.roll(a, 64, 1), c)
    b, d = jnp.where(low, b, pltpu.roll(d, 64, 1)), jnp.where(low, pltpu.roll(b, 64, 1), d)
    a, b = jnp.where(even, a, pltpu.roll(b, 32, 1)), jnp.where(even, pltpu.roll(a, 96, 1), b)
    c, d = jnp.where(even, c, pltpu.roll(d, 32, 1)), jnp.where(even, pltpu.roll(c, 96, 1), d)
    return a, b, c, d


def send_pieces(send_ref, lanes_ref, load, layers, q):
    lanes = lanes_ref[q]
    for g in range(layers // 4):
        picked = [pick_lanes(load(4 * g + j), lanes) for j in range(4)]
        for k, piece in enumerate(turn_quarters(picked)):
            send_ref[4 * q + k, g] = piece


def pack_kernel(rim_ref, lanes_ref, send_ref):
    def one(q, carry):
        send_pieces(send_ref, lanes_ref, lambda l: rim_ref[l], rim_ref.shape[0], q)
        return carry

    lax.fori_loop(0, send_ref.shape[0] // 4, one, 0)


def prepare_kernel(home_ref, first_ref, second_ref, coef_ref):
    blocks, layers = coef_ref.shape[0], coef_ref.shape[2]
    side = first_ref.shape[0]
    y, x = home_ref[0], home_ref[1]

    def shifts(b):
        return lax.rem(y - b // side + side, side), lax.rem(x - lax.rem(b, side) + side, side)

    zero = jnp.zeros((1, LANES), jnp.float32)
    for start in range(0, blocks, 8):
        group = range(start, start + 8)
        at = {b: shifts(jnp.int32(b)) for b in group}
        ratio = {b: zero for b in group}
        lower = {b: zero for b in group}
        for l in range(layers):
            for b in group:
                hy, hx = at[b]
                upper = second_ref[hx, hy, layers + l : layers + l + 1, :]
                pivot = 1.0 + lower[b] + upper - lower[b] * ratio[b]
                inverse = 1.0 / pivot
                coef_ref[b, INV, l : l + 1, :] = inverse
                coef_ref[b, CARRY, l : l + 1, :] = lower[b] * inverse
                ratio[b] = upper * inverse
                lower[b] = upper

    def fill(b, carry):
        hy, hx = shifts(b)
        inverse = coef_ref[b, INV]
        coef_ref[b, RATIO] = second_ref[hx, hy, layers : 2 * layers] * inverse
        outflow = jnp.zeros((layers, LANES), jnp.float32)
        for f in range(3):
            if f < 2:
                flux = first_ref[hy, hx, f * layers : (f + 1) * layers]
            else:
                flux = second_ref[hx, hy, :layers]
            outflow = outflow + jnp.maximum(flux, 0.0)
            coef_ref[b, EDGE + f] = -jnp.minimum(flux, 0.0) * inverse
        coef_ref[b, OWN] = (1.0 - outflow) * inverse
        return carry

    lax.fori_loop(0, blocks, fill, 0)


def row(coef_ref, c, kind, l):
    return coef_ref[c, kind, pl.ds(l, 8, stride=0), :]


CHUNK = 20


def advect_block(plan_ref, load, coef_ref, near_ref, rate_ref, acc_ref, i, b, c, n, counts):
    layers = acc_ref.shape[1]
    width = plan_ref.shape[1]
    for l in range(layers):
        acc_ref[i, l] = jnp.zeros((8, LANES), jnp.float32)

    @pl.when(plan_ref[b, width - 1] > 0)
    def _():
        cell = b * LANES + lax.broadcasted_iota(jnp.int32, (8, LANES), 1)
        here = near_ref[n, 3] == cell
        for l in range(layers):
            acc_ref[i, l] = jnp.where(here, rate_ref[l], 0.0) * row(coef_ref, c, INV, l)

    def add_from(take):
        def one(k, carry):
            s = plan_ref[b, k]
            lanes = [near_ref[n, f] & (LANES - 1) for f in range(3)]
            inside = [(near_ref[n, f] >> 7) == s for f in range(3)]
            for start in range(0, layers, CHUNK):
                chunk = range(start, start + CHUNK)
                values = [take(k, s, l) for l in chunk]
                total = [acc_ref[i, l] for l in chunk]
                for f in range(3):
                    for j, l in enumerate(chunk):
                        edge = jnp.where(inside[f], pick_lanes(values[j], lanes[f]), 0.0)
                        total[j] = total[j] + row(coef_ref, c, EDGE + f, l) * edge
                for j, l in enumerate(chunk):
                    acc_ref[i, l] = total[j]
            return carry

        return one

    low = 0
    for take, high in zip(load, counts):
        lax.fori_loop(low, high, add_from(take), 0)
        low = high


def solve_blocks(own, coef_ref, acc_ref, store, where_coef):
    layers = acc_ref.shape[1]
    part = [None] * len(where_coef)
    for l in range(layers):
        for i, c in enumerate(where_coef):
            now = row(coef_ref, c, OWN, l) * own(i, l) + acc_ref[i, l]
            if l > 0:
                now = now + row(coef_ref, c, CARRY, l) * part[i]
            part[i] = now
            if l < layers - 1:
                acc_ref[i, l] = now
            else:
                store(i, l, now)
    for l in range(layers - 2, -1, -1):
        for i, c in enumerate(where_coef):
            part[i] = acc_ref[i, l] + row(coef_ref, c, RATIO, l) * part[i]
            store(i, l, part[i])


def lanes_of(b):
    return pl.ds(pl.multiple_of(b * LANES, LANES), LANES)


def rim_kernel(last, plan_ref, field_hbm, received_ref, coef_hbm, near_hbm, rate_hbm, *refs):
    if last:
        halo_hbm, new_hbm, *scratch = refs
    else:
        lanes_ref, send_hbm, halo_hbm, new_hbm, *scratch = refs
    source_ref, own_ref, coef_ref, near_ref, rate_ref, halo_ref, new_ref, acc_ref, *more = scratch
    in_sem, source_sem, out_sem = more[-3:]
    layers = acc_ref.shape[1]
    blocks = field_hbm.shape[2] // LANES
    rim = blocks - 1
    width = plan_ref.shape[1]
    local_count, all_count = plan_ref[rim, width - 3], plan_ref[rim, width - 2]

    def source_copy(k):
        return pltpu.make_async_copy(
            field_hbm.at[:, :, lanes_of(plan_ref[rim, k])], source_ref.at[k], source_sem.at[k]
        )

    loads = [
        pltpu.make_async_copy(coef_hbm.at[pl.ds(rim, 1)], coef_ref, in_sem.at[0]),
        pltpu.make_async_copy(near_hbm.at[pl.ds(rim, 1)], near_ref, in_sem.at[1]),
        pltpu.make_async_copy(rate_hbm, rate_ref, in_sem.at[2]),
        pltpu.make_async_copy(field_hbm.at[:, :, lanes_of(rim)], own_ref, in_sem.at[3]),
    ]
    for load in loads:
        load.start()

    def begin(k, carry):
        source_copy(k).start()
        return carry

    lax.fori_loop(0, local_count, begin, 0)
    quads = received_ref.shape[0] // 4

    def unpack(q, carry):
        for g in range(layers // 4):
            pieces = [received_ref[4 * q + k, g] for k in range(4)]
            for j, value in enumerate(turn_quarters(pieces)):
                halo_ref[q, 4 * g + j] = value
        return carry

    lax.fori_loop(0, quads, unpack, 0)
    halo_out = pltpu.make_async_copy(halo_ref, halo_hbm, out_sem.at[0])
    halo_out.start()
    for load in loads:
        load.wait()

    def end(k, carry):
        source_copy(k).wait()
        return carry

    lax.fori_loop(0, local_count, end, 0)
    advect_block(
        plan_ref,
        (lambda k, s, l: source_ref[k, l], lambda k, s, l: halo_ref[s - blocks, l]),
        coef_ref,
        near_ref,
        rate_ref,
        acc_ref,
        0,
        rim,
        0,
        0,
        (local_count, all_count),
    )

    def store(i, l, value):
        new_ref[l] = value

    solve_blocks(lambda i, l: own_ref[l], coef_ref, acc_ref, store, [0])
    new_out = pltpu.make_async_copy(new_ref, new_hbm, out_sem.at[1])
    new_out.start()
    if not last:
        send_ref = more[0]

        def message_copy(q):
            return pltpu.make_async_copy(
                send_ref.at[pl.ds(4 * q, 4)], send_hbm.at[pl.ds(4 * q, 4)], out_sem.at[2 + q]
            )

        def one(q, carry):
            send_pieces(send_ref, lanes_ref, lambda l: new_ref[l], layers, q)
            message_copy(q).start()
            return carry

        lax.fori_loop(0, quads, one, 0)
        for q in range(quads):
            message_copy(q).wait()
    halo_out.wait()
    new_out.wait()


GROUP = 5


def bulk_kernel(plan_ref, field_hbm, halo_hbm, rim_hbm, coef_hbm, near_hbm, rate_hbm, out_hbm, *refs):
    field_ref, halo_ref, coef_ref, near_ref, rate_ref, acc_ref, new_ref, in_sem, out_sem = refs
    blocks = field_hbm.shape[2] // LANES
    width = plan_ref.shape[1]
    groups = (blocks - 1) // GROUP
    span = GROUP * LANES

    def coef_copy(g):
        part = pl.ds(g * GROUP, GROUP)
        return pltpu.make_async_copy(coef_hbm.at[part], coef_ref.at[part], in_sem.at[4 + g])

    def out_copy(g):
        lanes = pl.ds(pl.multiple_of(g * span, span), span)
        return pltpu.make_async_copy(new_ref.at[:, :, lanes], out_hbm.at[:, :, lanes], out_sem.at[g])

    loads = [
        pltpu.make_async_copy(field_hbm, field_ref, in_sem.at[0]),
        pltpu.make_async_copy(near_hbm, near_ref, in_sem.at[1]),
        pltpu.make_async_copy(rate_hbm, rate_ref, in_sem.at[2]),
        pltpu.make_async_copy(halo_hbm, halo_ref, in_sem.at[3]),
    ]
    for load in loads:
        load.start()
    for g in range(groups):
        coef_copy(g).start()
    rim_out = pltpu.make_async_copy(
        rim_hbm, out_hbm.at[:, :, (blocks - 1) * LANES :], out_sem.at[groups]
    )
    rim_out.start()
    for load in loads:
        load.wait()

    def group(g, carry):
        coef_copy(g).wait()

        def advect(i, inner):
            b = g * GROUP + i
            advect_block(
                plan_ref,
                (
                    lambda k, s, l: field_ref[l, :, lanes_of(s)],
                    lambda k, s, l: halo_ref[s - blocks, l],
                ),
                coef_ref,
                near_ref,
                rate_ref,
                acc_ref,
                i,
                b,
                b,
                b,
                (plan_ref[b, width - 3], plan_ref[b, width - 2]),
            )
            return inner

        lax.fori_loop(0, GROUP, advect, 0)
        where = [g * GROUP + i for i in range(GROUP)]

        def store(i, l, value):
            new_ref[l, :, lanes_of(where[i])] = value

        solve_blocks(lambda i, l: field_ref[l, :, lanes_of(where[i])], coef_ref, acc_ref, store, where)
        out_copy(g).start()
        return carry

    lax.fori_loop(0, groups, group, 0)
    for g in range(groups):
        out_copy(g).wait()
    rim_out.wait()


def share_side(value, side):
    square = 4
    shifts = [value]
    for hop in range(1, square):
        pairs = []
        for y in range(square):
            for x in range(square):
                to = y * square + (x + hop) % square if side == 0 else (y + hop) % square * square + x
                pairs.append((y * square + x, to))
        shifts.append(lax.ppermute(value, "tracer", pairs))
    return jnp.stack(shifts)


def share(value):
    half = value.shape[0] // 2
    first = share_side(share_side(value[:half], 0), 1)
    second = share_side(share_side(value[half:], 1), 0)
    return first, second


def on_device(
    concentration, courant, diffusivity, release_rate, release_cell, neighbour, send_rows
):
    layers, tracers, cells = concentration.shape
    blocks = cells // LANES
    peers, slots = send_rows.shape[1], send_rows.shape[2]
    halo_cells = peers * slots
    rim = 64
    f32 = jnp.float32
    full = pl.BlockSpec(memory_space=VMEM)
    scalars = pl.BlockSpec(memory_space=SMEM)
    message = pltpu.HBM((peers, layers // 4, tracers, LANES), f32)

    def kept(value):
        return pltpu.with_memory_space_constraint(value, pltpu.HBM)

    def params(mib):
        return pltpu.CompilerParams(vmem_limit_bytes=mib << 20)

    def panel(h):
        empty = jnp.zeros((1, LANES), f32)
        rows = jnp.concatenate([courant[h].reshape(-1, LANES), diffusivity[h], empty], 0)
        return rows

    rows = LANES - rim + jnp.maximum(send_rows[0], 0)
    quads = peers * slots // LANES
    lanes = jnp.broadcast_to(rows.reshape(quads, 1, LANES), (quads, 8, LANES))

    send = pl.pallas_call(
        pack_kernel,
        out_shape=message,
        grid=(1,),
        in_specs=[
            pl.BlockSpec((layers, tracers, LANES), lambda i: (0, 0, blocks - 1)),
            pl.BlockSpec((quads, 8, LANES), lambda i: (0, 0, 0)),
        ],
        out_specs=pl.BlockSpec(message.shape, lambda i: (0, 0, 0, 0)),
        name="pack",
    )(concentration, lanes)
    received = lax.all_to_all(send, "region", 0, 0, tiled=True)
    tables = [share(panel(0)), None]

    sources = blocks + halo_cells // LANES
    of_block = neighbour.reshape(3, blocks, LANES)
    source_id = jnp.arange(sources, dtype=jnp.int32)
    needed = jnp.any((of_block[..., None] >> 7) == source_id, axis=(0, 2))
    rank = jnp.sum(
        needed[:, None, :] & (source_id[None, None, :] < source_id[None, :, None]), axis=2
    )
    listed = jnp.sum(
        jnp.where(
            needed[:, None, :] & (rank[:, None, :] == source_id[None, :, None]),
            source_id[None, None, :],
            0,
        ),
        axis=2,
    )
    home = release_cell - lax.axis_index("region") * cells
    released = jnp.any(
        (home[None, :] >> 7) == jnp.arange(blocks, dtype=jnp.int32)[:, None], axis=1
    )
    plan = jnp.concatenate(
        [
            listed,
            jnp.sum(needed[:, :blocks], axis=1)[:, None],
            jnp.sum(needed, axis=1)[:, None],
            released[:, None],
        ],
        axis=1,
    ).astype(jnp.int32)
    near = jnp.concatenate(
        [
            jnp.broadcast_to(jnp.moveaxis(of_block, 1, 0)[:, :, None, :], (blocks, 3, 8, LANES)),
            jnp.broadcast_to(home[None, None, :, None], (blocks, 1, 8, LANES)),
        ],
        axis=1,
    )
    near = kept(near)
    rate = kept(jnp.broadcast_to(release_rate[:, :, None], (layers, tracers, LANES)))

    coef_shape = (blocks, KINDS, layers, LANES)

    column = lax.axis_index("tracer")
    square = jnp.stack([column // 4, column % 4]).astype(jnp.int32)

    def prepare(table):
        return pl.pallas_call(
            prepare_kernel,
            out_shape=pltpu.HBM(coef_shape, f32),
            in_specs=[scalars, full, full],
            out_specs=full,
            compiler_params=params(16),
            name="prepare",
        )(square, *table)

    tile = (layers, tracers, LANES)
    new_block = pltpu.HBM(tile, f32)
    halo_shape = pltpu.HBM((quads, *tile), f32)
    hbm = pl.BlockSpec(memory_space=pltpu.HBM)
    dma = pltpu.SemaphoreType.DMA

    def rim_step(field, received, coef, last):
        outs = (halo_shape, new_block) if last else (message, halo_shape, new_block)
        vmem = pltpu.VMEM
        scratch = [
            vmem((blocks, *tile), f32),
            vmem(tile, f32),
            vmem((1, *coef_shape[1:]), f32),
            vmem((1, 4, 8, LANES), jnp.int32),
            vmem(tile, f32),
            vmem(halo_shape.shape, f32),
            vmem(tile, f32),
            vmem((1, *tile), f32),
        ]
        scratch += [] if last else [vmem(message.shape, f32)]
        scratch += [dma((4,)), dma((blocks,)), dma((2 + quads,))]
        result = pl.pallas_call(
            functools.partial(rim_kernel, last),
            out_shape=outs,
            in_specs=[scalars, hbm, full, hbm, hbm, hbm] + ([] if last else [full]),
            out_specs=(hbm,) * len(outs),
            scratch_shapes=scratch,
            compiler_params=params(16),
            name="rim",
        )(plan, kept(field), received, kept(coef), near, rate, *(() if last else (lanes,)))
        return result if not last else (None, *result)

    def bulk_step(field, halo, new, coef):
        vmem = pltpu.VMEM
        return pl.pallas_call(
            bulk_kernel,
            out_shape=pltpu.HBM(field.shape, f32),
            in_specs=[scalars] + [hbm] * 6,
            out_specs=hbm,
            scratch_shapes=[
                vmem(field.shape, f32),
                vmem(halo_shape.shape, f32),
                vmem(coef_shape, f32),
                vmem((blocks, 4, 8, LANES), jnp.int32),
                vmem(tile, f32),
                vmem((GROUP, *tile), f32),
                vmem(field.shape, f32),
                dma((4 + (blocks - 1) // GROUP,)),
                dma((1 + (blocks - 1) // GROUP,)),
            ],
            compiler_params=params(24),
            name="bulk",
        )(plan, kept(field), kept(halo), kept(new), kept(coef), near, rate)

    field = concentration
    per_hour = STEPS // HOURS
    coef = None
    for step in range(STEPS):
        h = step // per_hour
        if step % per_hour == 0:
            coef = prepare(tables[h])
        last = step == STEPS - 1
        send, halo, new = rim_step(field, received, coef, last)
        if step == 0:
            later = panel(1)
            later, _ = lax.optimization_barrier((later, new))
            tables[1] = share(later)
        if not last:
            received = lax.all_to_all(send, "region", 0, 0, tiled=True)
        field = bulk_step(field, halo, new, coef)
    return field


def solution(mesh):
    both = ("region", "tracer")
    return jax.shard_map(
        on_device,
        mesh=mesh,
        in_specs=(
            P(None, "tracer", "region"),
            P(None, None, None, both),
            P(None, None, both),
            P(None, "tracer"),
            P("tracer"),
            P(None, "region"),
            P("region", None, None),
        ),
        out_specs=P(None, "tracer", "region"),
        check_vma=False,
    )
```

time: 316 us -> 247 us (0.78)
  local copies, waits for them, and re-layouts: 52.9 us -> 4.87 us
  Pallas kernels: 159 us -> 132 us
  starting transfers between devices: 51.1 us -> 70.7 us
  waiting for transfers between devices: 49.8 us -> 34.2 us
    unnamed x101 -> x11, local copies, waits for them, and re-layouts: 47.3 us -> 0.1 us
    ppermute x0 -> x24, starting transfers between devices: none -> 29.2 us  [share_side(): shifts.append(lax.ppermute(value, 'tracer', pairs))]
    pallas_call x14, Pallas kernels: 155 us -> 129 us  [the longest x6 91.8 us: bulk_step(): pl.pallas_call(bulk_kernel, out_shape=pltpu.HBM(field.shape, f32), in_spe...]
    all_to_all x6, waiting for transfers between devices: 35.8 us -> 17.7 us  [on_device(): received = lax.all_to_all(send, 'region', 0, 0, tiled=True)]
    ppermute x0 -> x24, waiting for transfers between devices: none -> 16.5 us  [share_side(): shifts.append(lax.ppermute(value, 'tracer', pairs))]
    all_to_all x2 -> x0, waiting for transfers between devices: 14.1 us -> none  [share(): return lax.all_to_all(copies, axis, 0, 0, tiled=True)]
    all_to_all x2 -> x0, starting transfers between devices: 12 us -> none  [share(): return lax.all_to_all(copies, axis, 0, 0, tiled=True)]
  transfers between devices with their start and end apart: 8 -> 30, of which waited for: 3 -> 14; matrix products, arithmetic and copies ran while one was open for 1% -> 3% of each run, Pallas kernels for 34% -> 35%
where the time goes in v2:
time: 247 us; the launch traced here: 246 us
  Pallas kernels  132 us (53%)
  starting transfers between devices  70.7 us (29%)
  waiting for transfers between devices  34.2 us (14%)
  local copies, waits for them, and re-layouts  4.87 us (2%)
  other arithmetic  3.51 us (1%)
    pallas_call x6, Pallas kernels, bulk_step(): pl.pallas_call(bulk_kernel, out_shape=pltpu.HBM(field.shape, f32), in_spe...  91.8 us
    all_to_all x6, starting transfers between devices, on_device(): received = lax.all_to_all(send, 'region', 0, 0, tiled=True)  41.5 us
    pallas_call x6, Pallas kernels, rim_step(): pl.pallas_call(functools.partial(rim_kernel, last), out_shape=outs, in_sp...  31.1 us
    ppermute x24, starting transfers between devices, share_side(): shifts.append(lax.ppermute(value, 'tracer', pairs))  29.2 us
    all_to_all x6, waiting for transfers between devices, on_device(): received = lax.all_to_all(send, 'region', 0, 0, tiled=True)  17.7 us
    ppermute x24, waiting for transfers between devices, share_side(): shifts.append(lax.ppermute(value, 'tracer', pairs))  16.5 us
    pallas_call x2, Pallas kernels, prepare(): pl.pallas_call(prepare_kernel, out_shape=pltpu.HBM(coef_shape, f32), in_s...  6.17 us
  transfers between devices with their start and end apart: 30, of which 14 were waited for; matrix products, arithmetic and copies ran while one was open for 3% of the time, Pallas kernels for 35%

profile of v2, /device:TPU:1, one launch (start us, length us, event | category | flops | bytes accessed | tf_op | source)
XLA Modules:
  0.0 245.6 jit_solution(1215522711979519598)
XLA Ops:
  0.0 0.8 slice.32
  0.8 3.3 %collective-permute-start.2 = (f32[80,128]{1,0:T(8,128)S(1)}, f32[80,128]{1,0:T(8,128)S(1)}, u32[]{:S(2)}, u32[]{:S(2)}) collective-permute-start(f32[80,128]{1,0:T(8,128)S(1)} %bitcast.74), channel_id=1, source_target_pairs={{0,3},{1,0},{2,1},{3,2},{4,7},{5,4},{6,5},{7,6},{8,11},{9,8},{10,9... | collective-permute-start | bytes 122888 | tf_op jit(solution)/shard_map/ppermute | solution.py:337
  4.1 0.5 collective-permute-start.1
  4.6 0.6 collective-permute-start
  5.2 0.9 fusion.8
  6.1 0.9 fusion.9
  7.2 2.8 %collective-permute-start.8 = (f32[80,128]{1,0:T(8,128)S(1)}, f32[80,128]{1,0:T(8,128)S(1)}, u32[]{:S(2)}, u32[]{:S(2)}) collective-permute-start(f32[80,128]{1,0:T(8,128)S(1)} %fusion.2), channel_id=1, source_target_pairs={{0,12},{1,13},{2,14},{3,15},{4,0},{5,1},{6,2},{7,3},{8,4},{9,5},{1... | collective-permute-start | bytes 122888 | tf_op jit(solution)/shard_map/ppermute | solution.py:337
  10.0 0.3 collective-permute-start.7
  10.3 0.7 maximum_add_fusion
  11.1 0.6 broadcast_in_dim.28.lanes_ref.refs_0_
  11.7 2.8 %pack.1 = f32[16,10,8,128]{3,2,1,0:T(8,128)} custom-call(f32[40,8,2048]{2,1,0:T(8,128)} %field_hbm.3, s32[4,8,128]{2,1,0:T(8,128)} %broadcast_in_dim.28.lanes_ref.refs_0_), custom_call_target="tpu_custom_call" | custom-call | tf_op jit(solution)/shard_map/pack/pallas_call | solution.py:376
  14.5 10.6 %all-to-all-start = ((f32[16,10,8,128]{3,2,1,0:T(8,128)}), f32[16,10,8,128]{3,2,1,0:T(8,128)S(1)}, u32[]{:S(2)}, u32[]{:S(2)}) async-start(f32[16,10,8,128]{3,2,1,0:T(8,128)} %pack.1), calls=%async_computation | async-start | bytes 1310720 | tf_op jit(solution)/shard_map/all_to_all | solution.py:387
  25.2 0.4 fusion
  25.7 0.4 convert_reduce_fusion
  26.2 0.4 select_reduce_fusion
  26.8 0.7 pad_add_fusion.near_hbm
  27.9 0.7 collective-permute-start.6
  28.7 2.1 collective-permute-start.5
  30.8 1.5 collective-permute-start.4
  32.3 2.1 collective-permute-start.11
  34.5 1.2 collective-permute-start.10
  36.1 1.4 collective-permute-done.4
  37.5 4.5 %collective-permute-done.3 = f32[4,80,128]{2,1,0:T(8,128)S(1)} collective-permute-done((f32[4,80,128]{2,1,0:T(8,128)S(1)}, f32[4,80,128]{2,1,0:T(8,128)S(1)}, u32[]{:S(2)}, u32[]{:S(2)}) %collective-permute-start.3) | collective-permute-done | bytes 163872 | tf_op jit(solution)/shard_map/ppermute | solution.py:337
  42.1 2.3 collective-permute-done.9
  44.5 3.1 %prepare.2.coef_hbm = f32[16,7,40,128]{3,2,1,0:T(8,128)} custom-call(s32[2]{0:T(128)S(1)} %pad_add_fusion.2.home_ref, f32[4,4,80,128]{3,2,1,0:T(8,128)S(1)} %pad_maximum_fusion.first_ref, f32[4,4,80,128]{3,2,1,0:T(8,128)S(1)} %pad_maximum_fusion.1.second_ref), custom_call_target="tpu_custom_call" | custom-call | tf_op jit(solution)/shard_map/prepare/pallas_call | solution.py:434
  47.6 0.8 broadcast_in_dim.31.rate_hbm
  48.4 5.3 %rim.6 = (f32[16,10,8,128]{3,2,1,0:T(8,128)}, f32[4,40,8,128]{3,2,1,0:T(8,128)}, f32[40,8,128]{2,1,0:T(8,128)}) custom-call(s32[16,23]{1,0:T(8,128)S(1)} %pad_add_fusion.1.plan_ref, f32[40,8,2048]{2,1,0:T(8,128)} %field_hbm.3, f32[16,10,8,128]{3,2,1,0:T(8,128)S(1)} %all-to-all-done.received_ref, f32[16,7,40,128]{3,2,1,0:T(8,128)} %prepare.2.coef_hbm, ...), custom_call_target="tpu_custom_call" | custom-call | tf_op jit(solution)/shard_map/rim/pallas_call | solution.py:464
  53.7 8.5 %all-to-all-start.1 = ((f32[16,10,8,128]{3,2,1,0:T(8,128)}), f32[16,10,8,128]{3,2,1,0:T(8,128)S(1)}, u32[]{:S(2)}, u32[]{:S(2)}) async-start(f32[16,10,8,128]{3,2,1,0:T(8,128)} %get-tuple-element.25), calls=%async_computation.1 | async-start | bytes 1310720 | tf_op jit(solution)/shard_map/all_to_all | solution.py:511
  62.3 15.3 %bulk.6.field_hbm = f32[40,8,2048]{2,1,0:T(8,128)} custom-call(s32[16,23]{1,0:T(8,128)S(1)} %pad_add_fusion.1.plan_ref, f32[40,8,2048]{2,1,0:T(8,128)} %field_hbm.3, f32[4,40,8,128]{3,2,1,0:T(8,128)} %get-tuple-element.23.halo_hbm, f32[40,8,128]{2,1,0:T(8,128)} %get-tuple-element.24.rim_hbm, f32[16,7,40,128]{3,2,1,0:T(8,128)} %prepare.2.coef_hbm, ...), custom_call_target="tpu_custom_call" | custom-call | tf_op jit(solution)/shard_map/bulk/pallas_call | solution.py:477
  77.5 4.6 %all-to-all-done.1.received_ref = f32[16,10,8,128]{3,2,1,0:T(8,128)S(1)} async-done(((f32[16,10,8,128]{3,2,1,0:T(8,128)}), f32[16,10,8,128]{3,2,1,0:T(8,128)S(1)}, u32[]{:S(2)}, u32[]{:S(2)}) %all-to-all-start.1) | async-done | bytes 655392 | tf_op jit(solution)/shard_map/all_to_all | solution.py:511
  82.2 5.3 %rim.7 = (f32[16,10,8,128]{3,2,1,0:T(8,128)}, f32[4,40,8,128]{3,2,1,0:T(8,128)}, f32[40,8,128]{2,1,0:T(8,128)}) custom-call(s32[16,23]{1,0:T(8,128)S(1)} %pad_add_fusion.1.plan_ref, f32[40,8,2048]{2,1,0:T(8,128)} %bulk.6.field_hbm, f32[16,10,8,128]{3,2,1,0:T(8,128)S(1)} %all-to-all-done.1.received_ref, f32[16,7,40,128]{3,2,1,0:T(8,128)} %prepare.2.coef_hbm, ...), custom_call_target="tpu_custom_call" | custom-call | tf_op jit(solution)/shard_map/rim/pallas_call | solution.py:464
  87.5 3.5 %all-to-all-start.2 = ((f32[16,10,8,128]{3,2,1,0:T(8,128)}), f32[16,10,8,128]{3,2,1,0:T(8,128)S(1)}, u32[]{:S(2)}, u32[]{:S(2)}) async-start(f32[16,10,8,128]{3,2,1,0:T(8,128)} %get-tuple-element.28), calls=%async_computation.2 | async-start | bytes 1310720 | tf_op jit(solution)/shard_map/all_to_all | solution.py:511
  91.1 15.3 %bulk.7.field_hbm = f32[40,8,2048]{2,1,0:T(8,128)} custom-call(s32[16,23]{1,0:T(8,128)S(1)} %pad_add_fusion.1.plan_ref, f32[40,8,2048]{2,1,0:T(8,128)} %bulk.6.field_hbm, f32[4,40,8,128]{3,2,1,0:T(8,128)} %get-tuple-element.26.halo_hbm, f32[40,8,128]{2,1,0:T(8,128)} %get-tuple-element.27.rim_hbm, f32[16,7,40,128]{3,2,1,0:T(8,128)} %prepare.2.coef_hbm, ...), custom_call_target="tpu_custom_call" | custom-call | tf_op jit(solution)/shard_map/bulk/pallas_call | solution.py:477
  106.4 4.2 %all-to-all-done.2.received_ref = f32[16,10,8,128]{3,2,1,0:T(8,128)S(1)} async-done(((f32[16,10,8,128]{3,2,1,0:T(8,128)}), f32[16,10,8,128]{3,2,1,0:T(8,128)S(1)}, u32[]{:S(2)}, u32[]{:S(2)}) %all-to-all-start.2) | async-done | bytes 655392 | tf_op jit(solution)/shard_map/all_to_all | solution.py:511
  110.6 5.3 %rim.8 = (f32[16,10,8,128]{3,2,1,0:T(8,128)}, f32[4,40,8,128]{3,2,1,0:T(8,128)}, f32[40,8,128]{2,1,0:T(8,128)}) custom-call(s32[16,23]{1,0:T(8,128)S(1)} %pad_add_fusion.1.plan_ref, f32[40,8,2048]{2,1,0:T(8,128)} %bulk.7.field_hbm, f32[16,10,8,128]{3,2,1,0:T(8,128)S(1)} %all-to-all-done.2.received_ref, f32[16,7,40,128]{3,2,1,0:T(8,128)} %prepare.2.coef_hbm, ...), custom_call_target="tpu_custom_call" | custom-call | tf_op jit(solution)/shard_map/rim/pallas_call | solution.py:464
  116.0 3.5 %all-to-all-start.3 = ((f32[16,10,8,128]{3,2,1,0:T(8,128)}), f32[16,10,8,128]{3,2,1,0:T(8,128)S(1)}, u32[]{:S(2)}, u32[]{:S(2)}) async-start(f32[16,10,8,128]{3,2,1,0:T(8,128)} %get-tuple-element.31), calls=%async_computation.3 | async-start | bytes 1310720 | tf_op jit(solution)/shard_map/all_to_all | solution.py:511
  119.6 0.4 collective-permute-start.14
  120.0 1.2 collective-permute-start.13
  121.2 0.6 collective-permute-start.12
  121.8 2.7 %collective-permute-start.20 = (f32[80,128]{1,0:T(8,128)S(1)}, f32[80,128]{1,0:T(8,128)S(1)}, u32[]{:S(2)}, u32[]{:S(2)}) collective-permute-start(f32[80,128]{1,0:T(8,128)S(1)} %get-tuple-element.55), channel_id=1, source_target_pairs={{0,12},{1,13},{2,14},{3,15},{4,0},{5,1},{6,2},{7,3},{8,4},{9,5},{1... | collective-permute-start | bytes 122888 | tf_op jit(solution)/shard_map/ppermute | solution.py:337
  124.7 0.9 collective-permute-done.12
  125.6 3.1 %collective-permute-start.17 = (f32[4,80,128]{2,1,0:T(8,128)S(1)}, f32[4,80,128]{2,1,0:T(8,128)S(1)}, u32[]{:S(2)}, u32[]{:S(2)}) collective-permute-start(f32[4,80,128]{2,1,0:T(8,128)S(1)} %get-tuple-element.46), channel_id=1, source_target_pairs={{0,12},{1,13},{2,14},{3,15},{4,0},{5,1},{6,2},{7,3},{8,4},{9,5},{1... | collective-permute-start | bytes 491528 | tf_op jit(solution)/shard_map/ppermute | solution.py:337
  128.9 0.5 collective-permute-start.18
  129.4 2.3 collective-permute-start.16
  131.7 0.5 collective-permute-start.15
  132.2 1.2 collective-permute-done.19
  133.6 0.7 collective-permute-start.23
  134.3 1.1 collective-permute-start.22
  135.5 0.5 collective-permute-start.21
  136.0 0.5 collective-permute-done.16
  136.5 4.5 %collective-permute-done.15 = f32[4,80,128]{2,1,0:T(8,128)S(1)} collective-permute-done((f32[4,80,128]{2,1,0:T(8,128)S(1)}, f32[4,80,128]{2,1,0:T(8,128)S(1)}, u32[]{:S(2)}, u32[]{:S(2)}) %collective-permute-start.15) | collective-permute-done | bytes 163872 | tf_op jit(solution)/shard_map/ppermute | solution.py:337
  141.0 0.7 collective-permute-done.21
  141.8 3.1 %prepare.3.coef_hbm = f32[16,7,40,128]{3,2,1,0:T(8,128)} custom-call(s32[2]{0:T(128)S(1)} %pad_add_fusion.2.home_ref, f32[4,4,80,128]{3,2,1,0:T(8,128)S(1)} %pad_maximum_fusion.2.first_ref, f32[4,4,80,128]{3,2,1,0:T(8,128)S(1)} %pad_maximum_fusion.3.second_ref), custom_call_target="tpu_custom_call" | custom-call | tf_op jit(solution)/shard_map/prepare/pallas_call | solution.py:434
  144.9 15.3 %bulk.8.field_hbm = f32[40,8,2048]{2,1,0:T(8,128)} custom-call(s32[16,23]{1,0:T(8,128)S(1)} %pad_add_fusion.1.plan_ref, f32[40,8,2048]{2,1,0:T(8,128)} %bulk.7.field_hbm, f32[4,40,8,128]{3,2,1,0:T(8,128)} %get-tuple-element.29.halo_hbm, f32[40,8,128]{2,1,0:T(8,128)} %get-tuple-element.30.rim_hbm, f32[16,7,40,128]{3,2,1,0:T(8,128)} %prepare.2.coef_hbm, ...), custom_call_target="tpu_custom_call" | custom-call | tf_op jit(solution)/shard_map/bulk/pallas_call | solution.py:477
  160.2 5.4 %rim.9 = (f32[16,10,8,128]{3,2,1,0:T(8,128)}, f32[4,40,8,128]{3,2,1,0:T(8,128)}, f32[40,8,128]{2,1,0:T(8,128)}) custom-call(s32[16,23]{1,0:T(8,128)S(1)} %pad_add_fusion.1.plan_ref, f32[40,8,2048]{2,1,0:T(8,128)} %bulk.8.field_hbm, f32[16,10,8,128]{3,2,1,0:T(8,128)S(1)} %all-to-all-done.3.received_ref, f32[16,7,40,128]{3,2,1,0:T(8,128)} %prepare.3.coef_hbm, ...), custom_call_target="tpu_custom_call" | custom-call | tf_op jit(solution)/shard_map/rim/pallas_call | solution.py:464
  165.5 11.9 %all-to-all-start.4 = ((f32[16,10,8,128]{3,2,1,0:T(8,128)}), f32[16,10,8,128]{3,2,1,0:T(8,128)S(1)}, u32[]{:S(2)}, u32[]{:S(2)}) async-start(f32[16,10,8,128]{3,2,1,0:T(8,128)} %get-tuple-element.35), calls=%async_computation.4 | async-start | bytes 1310720 | tf_op jit(solution)/shard_map/all_to_all | solution.py:511
  177.5 15.3 %bulk.9.field_hbm = f32[40,8,2048]{2,1,0:T(8,128)} custom-call(s32[16,23]{1,0:T(8,128)S(1)} %pad_add_fusion.1.plan_ref, f32[40,8,2048]{2,1,0:T(8,128)} %bulk.8.field_hbm, f32[4,40,8,128]{3,2,1,0:T(8,128)} %get-tuple-element.33.halo_hbm, f32[40,8,128]{2,1,0:T(8,128)} %get-tuple-element.34.rim_hbm, f32[16,7,40,128]{3,2,1,0:T(8,128)} %prepare.3.coef_hbm, ...), custom_call_target="tpu_custom_call" | custom-call | tf_op jit(solution)/shard_map/bulk/pallas_call | solution.py:477
  192.8 4.6 %all-to-all-done.4.received_ref = f32[16,10,8,128]{3,2,1,0:T(8,128)S(1)} async-done(((f32[16,10,8,128]{3,2,1,0:T(8,128)}), f32[16,10,8,128]{3,2,1,0:T(8,128)S(1)}, u32[]{:S(2)}, u32[]{:S(2)}) %all-to-all-start.4) | async-done | bytes 655392 | tf_op jit(solution)/shard_map/all_to_all | solution.py:511
  197.4 5.4 %rim.10 = (f32[16,10,8,128]{3,2,1,0:T(8,128)}, f32[4,40,8,128]{3,2,1,0:T(8,128)}, f32[40,8,128]{2,1,0:T(8,128)}) custom-call(s32[16,23]{1,0:T(8,128)S(1)} %pad_add_fusion.1.plan_ref, f32[40,8,2048]{2,1,0:T(8,128)} %bulk.9.field_hbm, f32[16,10,8,128]{3,2,1,0:T(8,128)S(1)} %all-to-all-done.4.received_ref, f32[16,7,40,128]{3,2,1,0:T(8,128)} %prepare.3.coef_hbm, ...), custom_call_target="tpu_custom_call" | custom-call | tf_op jit(solution)/shard_map/rim/pallas_call | solution.py:464
  202.8 3.5 %all-to-all-start.5 = ((f32[16,10,8,128]{3,2,1,0:T(8,128)}), f32[16,10,8,128]{3,2,1,0:T(8,128)S(1)}, u32[]{:S(2)}, u32[]{:S(2)}) async-start(f32[16,10,8,128]{3,2,1,0:T(8,128)} %get-tuple-element.38), calls=%async_computation.5 | async-start | bytes 1310720 | tf_op jit(solution)/shard_map/all_to_all | solution.py:511
  206.3 15.3 %bulk.10.field_hbm = f32[40,8,2048]{2,1,0:T(8,128)} custom-call(s32[16,23]{1,0:T(8,128)S(1)} %pad_add_fusion.1.plan_ref, f32[40,8,2048]{2,1,0:T(8,128)} %bulk.9.field_hbm, f32[4,40,8,128]{3,2,1,0:T(8,128)} %get-tuple-element.36.halo_hbm, f32[40,8,128]{2,1,0:T(8,128)} %get-tuple-element.37.rim_hbm, f32[16,7,40,128]{3,2,1,0:T(8,128)} %prepare.3.coef_hbm, ...), custom_call_target="tpu_custom_call" | custom-call | tf_op jit(solution)/shard_map/bulk/pallas_call | solution.py:477
  221.6 4.2 %all-to-all-done.5.received_ref = f32[16,10,8,128]{3,2,1,0:T(8,128)S(1)} async-done(((f32[16,10,8,128]{3,2,1,0:T(8,128)}), f32[16,10,8,128]{3,2,1,0:T(8,128)S(1)}, u32[]{:S(2)}, u32[]{:S(2)}) %all-to-all-start.5) | async-done | bytes 655392 | tf_op jit(solution)/shard_map/all_to_all | solution.py:511
  225.8 4.3 %rim.11 = (f32[4,40,8,128]{3,2,1,0:T(8,128)}, f32[40,8,128]{2,1,0:T(8,128)}) custom-call(s32[16,23]{1,0:T(8,128)S(1)} %pad_add_fusion.1.plan_ref, f32[40,8,2048]{2,1,0:T(8,128)} %bulk.10.field_hbm, f32[16,10,8,128]{3,2,1,0:T(8,128)S(1)} %all-to-all-done.5.received_ref, f32[16,7,40,128]{3,2,1,0:T(8,128)} %prepare.3.coef_hbm, ...), custom_call_target="tpu_custom_call" | custom-call | tf_op jit(solution)/shard_map/rim/pallas_call | solution.py:464
  230.2 15.3 %bulk.11 = f32[40,8,2048]{2,1,0:T(8,128)} custom-call(s32[16,23]{1,0:T(8,128)S(1)} %pad_add_fusion.1.plan_ref, f32[40,8,2048]{2,1,0:T(8,128)} %bulk.10.field_hbm, f32[4,40,8,128]{3,2,1,0:T(8,128)} %get-tuple-element.39.halo_hbm, f32[40,8,128]{2,1,0:T(8,128)} %get-tuple-element.40.rim_hbm, f32[16,7,40,128]{3,2,1,0:T(8,128)} %prepare.3.coef_hbm, ...), custom_call_target="tpu_custom_call" | custom-call | tf_op jit(solution)/shard_map/bulk/pallas_call | solution.py:477
  (63 shorter events, 2.7 us)
Async XLA Ops:
  0.0 25.1 %copy-start.3 = (s32[8]{0:T(128)S(1)}, s32[8]{0:T(128)}, u32[]{:S(2)}) copy-start(s32[8]{0:T(128)} %param.11) | copy-start | bytes 100
  0.0 25.2 %copy-start.1 = (s32[3,2048]{1,0:T(4,128)S(1)}, s32[3,2048]{1,0:T(4,128)}, u32[]{:S(2)}) copy-start(s32[3,2048]{1,0:T(4,128)} %param.12) | copy-start | bytes 73732
  0.8 27.1 %collective-permute-start.2 = (f32[80,128]{1,0:T(8,128)S(1)}, f32[80,128]{1,0:T(8,128)S(1)}, u32[]{:S(2)}, u32[]{:S(2)}) collective-permute-start(f32[80,128]{1,0:T(8,128)S(1)} %bitcast.74), channel_id=1, source_target_pairs={{0,3},{1,0},{2,1},{3,2},{4,7},{5,4},{6,5},{7,6},{8,11},{9,8},{10,9... | collective-permute-start | bytes 122888 | tf_op jit(solution)/shard_map/ppermute | solution.py:337
  4.1 24.5 %collective-permute-start.1 = (f32[80,128]{1,0:T(8,128)S(1)}, f32[80,128]{1,0:T(8,128)S(1)}, u32[]{:S(2)}, u32[]{:S(2)}) collective-permute-start(f32[80,128]{1,0:T(8,128)S(1)} %bitcast.75), channel_id=1, source_target_pairs={{0,2},{1,3},{2,0},{3,1},{4,6},{5,7},{6,4},{7,5},{8,10},{9,11},{10,... | collective-permute-start | bytes 122888 | tf_op jit(solution)/shard_map/ppermute | solution.py:337
  4.6 24.0 %collective-permute-start = (f32[80,128]{1,0:T(8,128)S(1)}, f32[80,128]{1,0:T(8,128)S(1)}, u32[]{:S(2)}, u32[]{:S(2)}) collective-permute-start(f32[80,128]{1,0:T(8,128)S(1)} %bitcast.76), channel_id=1, source_target_pairs={{0,1},{1,2},{2,3},{3,0},{4,5},{5,6},{6,7},{7,4},{8,9},{9,10},{10,1... | collective-permute-start | bytes 122888 | tf_op jit(solution)/shard_map/ppermute | solution.py:337
  7.2 25.0 %collective-permute-start.8 = (f32[80,128]{1,0:T(8,128)S(1)}, f32[80,128]{1,0:T(8,128)S(1)}, u32[]{:S(2)}, u32[]{:S(2)}) collective-permute-start(f32[80,128]{1,0:T(8,128)S(1)} %fusion.2), channel_id=1, source_target_pairs={{0,12},{1,13},{2,14},{3,15},{4,0},{5,1},{6,2},{7,3},{8,4},{9,5},{1... | collective-permute-start | bytes 122888 | tf_op jit(solution)/shard_map/ppermute | solution.py:337
  10.0 22.3 %collective-permute-start.7 = (f32[80,128]{1,0:T(8,128)S(1)}, f32[80,128]{1,0:T(8,128)S(1)}, u32[]{:S(2)}, u32[]{:S(2)}) collective-permute-start(f32[80,128]{1,0:T(8,128)S(1)} %fusion.2), channel_id=1, source_target_pairs={{0,8},{1,9},{2,10},{3,11},{4,12},{5,13},{6,14},{7,15},{8,0},{9,1},... | collective-permute-start | bytes 122888 | tf_op jit(solution)/shard_map/ppermute | solution.py:337
  11.7 24.3 %copy-start.2 = (f32[40,8]{0,1:T(8,128)S(1)}, f32[40,8]{0,1:T(8,128)}, u32[]{:S(2)}) copy-start(f32[40,8]{0,1:T(8,128)} %param.10) | copy-start | bytes 3844
  14.5 33.1 %all-to-all-start = ((f32[16,10,8,128]{3,2,1,0:T(8,128)}), f32[16,10,8,128]{3,2,1,0:T(8,128)S(1)}, u32[]{:S(2)}, u32[]{:S(2)}) async-start(f32[16,10,8,128]{3,2,1,0:T(8,128)} %pack.1), calls=%async_computation | async-start | bytes 1310720 | tf_op jit(solution)/shard_map/all_to_all | solution.py:387
  27.9 4.4 %collective-permute-start.6 = (f32[80,128]{1,0:T(8,128)S(1)}, f32[80,128]{1,0:T(8,128)S(1)}, u32[]{:S(2)}, u32[]{:S(2)}) collective-permute-start(f32[80,128]{1,0:T(8,128)S(1)} %fusion.2), channel_id=1, source_target_pairs={{0,4},{1,5},{2,6},{3,7},{4,8},{5,9},{6,10},{7,11},{8,12},{9,13},{1... | collective-permute-start | bytes 122888 | tf_op jit(solution)/shard_map/ppermute | solution.py:337
  28.7 7.0 %collective-permute-start.5 = (f32[4,80,128]{2,1,0:T(8,128)S(1)}, f32[4,80,128]{2,1,0:T(8,128)S(1)}, u32[]{:S(2)}, u32[]{:S(2)}) collective-permute-start(f32[4,80,128]{2,1,0:T(8,128)S(1)} %get-tuple-element.50), channel_id=1, source_target_pairs={{0,12},{1,13},{2,14},{3,15},{4,0},{5,1},{6,2},{7,3},{8,4},{9,5},{1... | collective-permute-start | bytes 491528 | tf_op jit(solution)/shard_map/ppermute | solution.py:337
  30.8 6.6 %collective-permute-start.4 = (f32[4,80,128]{2,1,0:T(8,128)S(1)}, f32[4,80,128]{2,1,0:T(8,128)S(1)}, u32[]{:S(2)}, u32[]{:S(2)}) collective-permute-start(f32[4,80,128]{2,1,0:T(8,128)S(1)} %get-tuple-element.50), channel_id=1, source_target_pairs={{0,8},{1,9},{2,10},{3,11},{4,12},{5,13},{6,14},{7,15},{8,0},{9,1},... | collective-permute-start | bytes 491528 | tf_op jit(solution)/shard_map/ppermute | solution.py:337
  32.3 9.7 %collective-permute-start.3 = (f32[4,80,128]{2,1,0:T(8,128)S(1)}, f32[4,80,128]{2,1,0:T(8,128)S(1)}, u32[]{:S(2)}, u32[]{:S(2)}) collective-permute-start(f32[4,80,128]{2,1,0:T(8,128)S(1)} %get-tuple-element.50), channel_id=1, source_target_pairs={{0,4},{1,5},{2,6},{3,7},{4,8},{5,9},{6,10},{7,11},{8,12},{9,13},{1... | collective-permute-start | bytes 491528 | tf_op jit(solution)/shard_map/ppermute | solution.py:337
  32.3 9.7 %collective-permute-start.11 = (f32[4,80,128]{2,1,0:T(8,128)S(1)}, f32[4,80,128]{2,1,0:T(8,128)S(1)}, u32[]{:S(2)}, u32[]{:S(2)}) collective-permute-start(f32[4,80,128]{2,1,0:T(8,128)S(1)} %get-tuple-element.48), channel_id=1, source_target_pairs={{0,3},{1,0},{2,1},{3,2},{4,7},{5,4},{6,5},{7,6},{8,11},{9,8},{10,9... | collective-permute-start | bytes 491528 | tf_op jit(solution)/shard_map/ppermute | solution.py:337
  34.5 7.6 %collective-permute-start.10 = (f32[4,80,128]{2,1,0:T(8,128)S(1)}, f32[4,80,128]{2,1,0:T(8,128)S(1)}, u32[]{:S(2)}, u32[]{:S(2)}) collective-permute-start(f32[4,80,128]{2,1,0:T(8,128)S(1)} %get-tuple-element.48), channel_id=1, source_target_pairs={{0,2},{1,3},{2,0},{3,1},{4,6},{5,7},{6,4},{7,5},{8,10},{9,11},{10,... | collective-permute-start | bytes 491528 | tf_op jit(solution)/shard_map/ppermute | solution.py:337
  35.7 8.7 %collective-permute-start.9 = (f32[4,80,128]{2,1,0:T(8,128)S(1)}, f32[4,80,128]{2,1,0:T(8,128)S(1)}, u32[]{:S(2)}, u32[]{:S(2)}) collective-permute-start(f32[4,80,128]{2,1,0:T(8,128)S(1)} %get-tuple-element.48), channel_id=1, source_target_pairs={{0,1},{1,2},{2,3},{3,0},{4,5},{5,6},{6,7},{7,4},{8,9},{9,10},{10,1... | collective-permute-start | bytes 491528 | tf_op jit(solution)/shard_map/ppermute | solution.py:337
  42.1 6.3 %copy-start = (s32[4,8,128]{2,1,0:T(8,128)S(1)}, s32[4,8,128]{2,1,0:T(8,128)}, u32[]{:S(2)}) copy-start(s32[4,8,128]{2,1,0:T(8,128)} %broadcast_in_dim.28.lanes_ref.refs_0_) | copy-start | bytes 49156
  53.7 28.5 %all-to-all-start.1 = ((f32[16,10,8,128]{3,2,1,0:T(8,128)}), f32[16,10,8,128]{3,2,1,0:T(8,128)S(1)}, u32[]{:S(2)}, u32[]{:S(2)}) async-start(f32[16,10,8,128]{3,2,1,0:T(8,128)} %get-tuple-element.25), calls=%async_computation.1 | async-start | bytes 1310720 | tf_op jit(solution)/shard_map/all_to_all | solution.py:511
  87.5 23.1 %all-to-all-start.2 = ((f32[16,10,8,128]{3,2,1,0:T(8,128)}), f32[16,10,8,128]{3,2,1,0:T(8,128)S(1)}, u32[]{:S(2)}, u32[]{:S(2)}) async-start(f32[16,10,8,128]{3,2,1,0:T(8,128)} %get-tuple-element.28), calls=%async_computation.2 | async-start | bytes 1310720 | tf_op jit(solution)/shard_map/all_to_all | solution.py:511
  116.0 44.2 %all-to-all-start.3 = ((f32[16,10,8,128]{3,2,1,0:T(8,128)}), f32[16,10,8,128]{3,2,1,0:T(8,128)S(1)}, u32[]{:S(2)}, u32[]{:S(2)}) async-start(f32[16,10,8,128]{3,2,1,0:T(8,128)} %get-tuple-element.31), calls=%async_computation.3 | async-start | bytes 1310720 | tf_op jit(solution)/shard_map/all_to_all | solution.py:511
  119.6 4.8 %collective-permute-start.14 = (f32[80,128]{1,0:T(8,128)S(1)}, f32[80,128]{1,0:T(8,128)S(1)}, u32[]{:S(2)}, u32[]{:S(2)}) collective-permute-start(f32[80,128]{1,0:T(8,128)S(1)} %get-tuple-element.56), channel_id=1, source_target_pairs={{0,3},{1,0},{2,1},{3,2},{4,7},{5,4},{6,5},{7,6},{8,11},{9,8},{10,9... | collective-permute-start | bytes 122888 | tf_op jit(solution)/shard_map/ppermute | solution.py:337
  120.0 4.7 %collective-permute-start.13 = (f32[80,128]{1,0:T(8,128)S(1)}, f32[80,128]{1,0:T(8,128)S(1)}, u32[]{:S(2)}, u32[]{:S(2)}) collective-permute-start(f32[80,128]{1,0:T(8,128)S(1)} %get-tuple-element.56), channel_id=1, source_target_pairs={{0,2},{1,3},{2,0},{3,1},{4,6},{5,7},{6,4},{7,5},{8,10},{9,11},{10,... | collective-permute-start | bytes 122888 | tf_op jit(solution)/shard_map/ppermute | solution.py:337
  121.2 4.4 %collective-permute-start.12 = (f32[80,128]{1,0:T(8,128)S(1)}, f32[80,128]{1,0:T(8,128)S(1)}, u32[]{:S(2)}, u32[]{:S(2)}) collective-permute-start(f32[80,128]{1,0:T(8,128)S(1)} %get-tuple-element.56), channel_id=1, source_target_pairs={{0,1},{1,2},{2,3},{3,0},{4,5},{5,6},{6,7},{7,4},{8,9},{9,10},{10,1... | collective-permute-start | bytes 122888 | tf_op jit(solution)/shard_map/ppermute | solution.py:337
  121.8 9.9 %collective-permute-start.20 = (f32[80,128]{1,0:T(8,128)S(1)}, f32[80,128]{1,0:T(8,128)S(1)}, u32[]{:S(2)}, u32[]{:S(2)}) collective-permute-start(f32[80,128]{1,0:T(8,128)S(1)} %get-tuple-element.55), channel_id=1, source_target_pairs={{0,12},{1,13},{2,14},{3,15},{4,0},{5,1},{6,2},{7,3},{8,4},{9,5},{1... | collective-permute-start | bytes 122888 | tf_op jit(solution)/shard_map/ppermute | solution.py:337
  125.6 9.9 %collective-permute-start.17 = (f32[4,80,128]{2,1,0:T(8,128)S(1)}, f32[4,80,128]{2,1,0:T(8,128)S(1)}, u32[]{:S(2)}, u32[]{:S(2)}) collective-permute-start(f32[4,80,128]{2,1,0:T(8,128)S(1)} %get-tuple-element.46), channel_id=1, source_target_pairs={{0,12},{1,13},{2,14},{3,15},{4,0},{5,1},{6,2},{7,3},{8,4},{9,5},{1... | collective-permute-start | bytes 491528 | tf_op jit(solution)/shard_map/ppermute | solution.py:337
  128.7 4.7 %collective-permute-start.19 = (f32[80,128]{1,0:T(8,128)S(1)}, f32[80,128]{1,0:T(8,128)S(1)}, u32[]{:S(2)}, u32[]{:S(2)}) collective-permute-start(f32[80,128]{1,0:T(8,128)S(1)} %get-tuple-element.55), channel_id=1, source_target_pairs={{0,8},{1,9},{2,10},{3,11},{4,12},{5,13},{6,14},{7,15},{8,0},{9,1},... | collective-permute-start | bytes 122888 | tf_op jit(solution)/shard_map/ppermute | solution.py:337
  128.9 4.6 %collective-permute-start.18 = (f32[80,128]{1,0:T(8,128)S(1)}, f32[80,128]{1,0:T(8,128)S(1)}, u32[]{:S(2)}, u32[]{:S(2)}) collective-permute-start(f32[80,128]{1,0:T(8,128)S(1)} %get-tuple-element.55), channel_id=1, source_target_pairs={{0,4},{1,5},{2,6},{3,7},{4,8},{5,9},{6,10},{7,11},{8,12},{9,13},{1... | collective-permute-start | bytes 122888 | tf_op jit(solution)/shard_map/ppermute | solution.py:337
  129.4 7.0 %collective-permute-start.16 = (f32[4,80,128]{2,1,0:T(8,128)S(1)}, f32[4,80,128]{2,1,0:T(8,128)S(1)}, u32[]{:S(2)}, u32[]{:S(2)}) collective-permute-start(f32[4,80,128]{2,1,0:T(8,128)S(1)} %get-tuple-element.46), channel_id=1, source_target_pairs={{0,8},{1,9},{2,10},{3,11},{4,12},{5,13},{6,14},{7,15},{8,0},{9,1},... | collective-permute-start | bytes 491528 | tf_op jit(solution)/shard_map/ppermute | solution.py:337
  131.7 9.3 %collective-permute-start.15 = (f32[4,80,128]{2,1,0:T(8,128)S(1)}, f32[4,80,128]{2,1,0:T(8,128)S(1)}, u32[]{:S(2)}, u32[]{:S(2)}) collective-permute-start(f32[4,80,128]{2,1,0:T(8,128)S(1)} %get-tuple-element.46), channel_id=1, source_target_pairs={{0,4},{1,5},{2,6},{3,7},{4,8},{5,9},{6,10},{7,11},{8,12},{9,13},{1... | collective-permute-start | bytes 491528 | tf_op jit(solution)/shard_map/ppermute | solution.py:337
  133.6 7.4 %collective-permute-start.23 = (f32[4,80,128]{2,1,0:T(8,128)S(1)}, f32[4,80,128]{2,1,0:T(8,128)S(1)}, u32[]{:S(2)}, u32[]{:S(2)}) collective-permute-start(f32[4,80,128]{2,1,0:T(8,128)S(1)} %get-tuple-element.44), channel_id=1, source_target_pairs={{0,3},{1,0},{2,1},{3,2},{4,7},{5,4},{6,5},{7,6},{8,11},{9,8},{10,9... | collective-permute-start | bytes 491528 | tf_op jit(solution)/shard_map/ppermute | solution.py:337
  134.3 6.7 %collective-permute-start.22 = (f32[4,80,128]{2,1,0:T(8,128)S(1)}, f32[4,80,128]{2,1,0:T(8,128)S(1)}, u32[]{:S(2)}, u32[]{:S(2)}) collective-permute-start(f32[4,80,128]{2,1,0:T(8,128)S(1)} %get-tuple-element.44), channel_id=1, source_target_pairs={{0,2},{1,3},{2,0},{3,1},{4,6},{5,7},{6,4},{7,5},{8,10},{9,11},{10,... | collective-permute-start | bytes 491528 | tf_op jit(solution)/shard_map/ppermute | solution.py:337
  135.5 6.3 %collective-permute-start.21 = (f32[4,80,128]{2,1,0:T(8,128)S(1)}, f32[4,80,128]{2,1,0:T(8,128)S(1)}, u32[]{:S(2)}, u32[]{:S(2)}) collective-permute-start(f32[4,80,128]{2,1,0:T(8,128)S(1)} %get-tuple-element.44), channel_id=1, source_target_pairs={{0,1},{1,2},{2,3},{3,0},{4,5},{5,6},{6,7},{7,4},{8,9},{9,10},{10,1... | collective-permute-start | bytes 491528 | tf_op jit(solution)/shard_map/ppermute | solution.py:337
  165.5 31.9 %all-to-all-start.4 = ((f32[16,10,8,128]{3,2,1,0:T(8,128)}), f32[16,10,8,128]{3,2,1,0:T(8,128)S(1)}, u32[]{:S(2)}, u32[]{:S(2)}) async-start(f32[16,10,8,128]{3,2,1,0:T(8,128)} %get-tuple-element.35), calls=%async_computation.4 | async-start | bytes 1310720 | tf_op jit(solution)/shard_map/all_to_all | solution.py:511
  202.8 23.1 %all-to-all-start.5 = ((f32[16,10,8,128]{3,2,1,0:T(8,128)}), f32[16,10,8,128]{3,2,1,0:T(8,128)S(1)}, u32[]{:S(2)}, u32[]{:S(2)}) async-start(f32[16,10,8,128]{3,2,1,0:T(8,128)} %get-tuple-element.38), calls=%async_computation.5 | async-start | bytes 1310720 | tf_op jit(solution)/shard_map/all_to_all | solution.py:511

commit v3 on v2

--- a/solution.py
+++ b/solution.py
@@ -20,24 +20,38 @@
     return jnp.take_along_axis(values, lanes, axis=1, mode="promise_in_bounds")
 
 
-def turn_quarters(values):
-    lane = lax.broadcasted_iota(jnp.int32, (8, LANES), 1)
-    low = lane < 64
-    even = (lane & 32) == 0
-    a, b, c, d = values
-    a, c = jnp.where(low, a, pltpu.roll(c, 64, 1)), jnp.where(low, pltpu.roll(a, 64, 1), c)
-    b, d = jnp.where(low, b, pltpu.roll(d, 64, 1)), jnp.where(low, pltpu.roll(b, 64, 1), d)
-    a, b = jnp.where(even, a, pltpu.roll(b, 32, 1)), jnp.where(even, pltpu.roll(a, 96, 1), b)
-    c, d = jnp.where(even, c, pltpu.roll(d, 32, 1)), jnp.where(even, pltpu.roll(c, 96, 1), d)
-    return a, b, c, d
+def mix_quarters(parts, pieces, first):
+    results = []
+    for i in range(4):
+        value = pieces[first(i) % 4]
+        for p in range(1, 4):
+            value = jnp.where(parts[p], pieces[(first(i) + p) % 4], value)
+        results.append(value)
+    return results
+
+
+def quarter_masks():
+    part = lax.broadcasted_iota(jnp.int32, (8, LANES), 1) // 32
+    return [part == p for p in range(4)]
 
 
 def send_pieces(send_ref, lanes_ref, load, layers, q):
-    lanes = lanes_ref[q]
+    parts = quarter_masks()
     for g in range(layers // 4):
-        picked = [pick_lanes(load(4 * g + j), lanes) for j in range(4)]
-        for k, piece in enumerate(turn_quarters(picked)):
-            send_ref[4 * q + k, g] = piece
+        picked = [pick_lanes(load(4 * g + j), lanes_ref[q, j]) for j in range(4)]
+        for m, piece in enumerate(mix_quarters(parts, picked, lambda m: -m)):
+            send_ref[4 * q + m, g] = piece
+
+
+def unpack_pieces(halo_ref, received_ref, layers, q, own):
+    parts = quarter_masks()
+    for g in range(layers // 4):
+        pieces = [received_ref[4 * q + k, g] for k in range(4)]
+        turned = mix_quarters(parts, pieces, lambda d: -d)
+        turned = [turned[0]] + [pltpu.roll(turned[d], LANES - 32 * d, 1) for d in range(1, 4)]
+        backward = [turned[-k % 4] for k in range(4)]
+        for p, value in enumerate(mix_quarters(parts, backward, lambda p: -p)):
+            halo_ref[q, 4 * g + lax.rem(p - own + 4, 4)] = value
 
 
 def pack_kernel(rim_ref, lanes_ref, send_ref):
@@ -48,13 +62,20 @@
     lax.fori_loop(0, send_ref.shape[0] // 4, one, 0)
 
 
-def prepare_kernel(home_ref, first_ref, second_ref, coef_ref):
+def prepare_kernel(home_ref, *refs):
+    *panels, coef_ref = refs
     blocks, layers = coef_ref.shape[0], coef_ref.shape[2]
-    side = first_ref.shape[0]
+    side = panels[0].shape[0]
     y, x = home_ref[0], home_ref[1]
 
     def shifts(b):
         return lax.rem(y - b // side + side, side), lax.rem(x - lax.rem(b, side) + side, side)
+
+    def rows(hy, hx, first, count):
+        split = panels[0].shape[2]
+        if first < split:
+            return panels[0][hy, hx, first : first + count]
+        return panels[1][hx, hy, first - split : first - split + count]
 
     zero = jnp.zeros((1, LANES), jnp.float32)
     for start in range(0, blocks, 8):
@@ -65,7 +86,7 @@
         for l in range(layers):
             for b in group:
                 hy, hx = at[b]
-                upper = second_ref[hx, hy, layers + l : layers + l + 1, :]
+                upper = rows(hy, hx, 3 * layers + l, 1)
                 pivot = 1.0 + lower[b] + upper - lower[b] * ratio[b]
                 inverse = 1.0 / pivot
                 coef_ref[b, INV, l : l + 1, :] = inverse
@@ -76,13 +97,10 @@
     def fill(b, carry):
         hy, hx = shifts(b)
         inverse = coef_ref[b, INV]
-        coef_ref[b, RATIO] = second_ref[hx, hy, layers : 2 * layers] * inverse
+        coef_ref[b, RATIO] = rows(hy, hx, 3 * layers, layers) * inverse
         outflow = jnp.zeros((layers, LANES), jnp.float32)
         for f in range(3):
-            if f < 2:
-                flux = first_ref[hy, hx, f * layers : (f + 1) * layers]
-            else:
-                flux = second_ref[hx, hy, :layers]
+            flux = rows(hy, hx, f * layers, layers)
             outflow = outflow + jnp.maximum(flux, 0.0)
             coef_ref[b, EDGE + f] = -jnp.minimum(flux, 0.0) * inverse
         coef_ref[b, OWN] = (1.0 - outflow) * inverse
@@ -95,7 +113,7 @@
     return coef_ref[c, kind, pl.ds(l, 8, stride=0), :]
 
 
-CHUNK = 20
+CHUNK = 40
 
 
 def advect_block(plan_ref, load, coef_ref, near_ref, rate_ref, acc_ref, i, b, c, n, counts):
@@ -113,12 +131,12 @@
 
     def add_from(take):
         def one(k, carry):
-            s = plan_ref[b, k]
             lanes = [near_ref[n, f] & (LANES - 1) for f in range(3)]
-            inside = [(near_ref[n, f] >> 7) == s for f in range(3)]
+            inside = [(near_ref[n, f] >> 7) == k for f in range(3)]
+            from_first = near_ref[n, 4] != 0
             for start in range(0, layers, CHUNK):
                 chunk = range(start, start + CHUNK)
-                values = [take(k, s, l) for l in chunk]
+                values = [take(k, from_first, l) for l in chunk]
                 total = [acc_ref[i, l] for l in chunk]
                 for f in range(3):
                     for j, l in enumerate(chunk):
@@ -172,10 +190,21 @@
     width = plan_ref.shape[1]
     local_count, all_count = plan_ref[rim, width - 3], plan_ref[rim, width - 2]
 
-    def source_copy(k):
+    pairs = (width - 4) // 2
+
+    def source_copy(k, second):
+        block = plan_ref[rim, pairs * second + k]
+        to = 2 * k + second
         return pltpu.make_async_copy(
-            field_hbm.at[:, :, lanes_of(plan_ref[rim, k])], source_ref.at[k], source_sem.at[k]
+            field_hbm.at[:, :, lanes_of(block)], source_ref.at[to], source_sem.at[to]
         )
+
+    def double(k):
+        return plan_ref[rim, k] != plan_ref[rim, pairs + k]
+
+    def take_local(k, from_first, l):
+        other = 2 * k + double(k).astype(jnp.int32)
+        return jnp.where(from_first, source_ref[2 * k, l], source_ref[other, l])
 
     loads = [
         pltpu.make_async_copy(coef_hbm.at[pl.ds(rim, 1)], coef_ref, in_sem.at[0]),
@@ -187,17 +216,19 @@
         load.start()
 
     def begin(k, carry):
-        source_copy(k).start()
+        source_copy(k, 0).start()
+
+        @pl.when(double(k))
+        def _():
+            source_copy(k, 1).start()
+
         return carry
 
     lax.fori_loop(0, local_count, begin, 0)
     quads = received_ref.shape[0] // 4
 
     def unpack(q, carry):
-        for g in range(layers // 4):
-            pieces = [received_ref[4 * q + k, g] for k in range(4)]
-            for j, value in enumerate(turn_quarters(pieces)):
-                halo_ref[q, 4 * g + j] = value
+        unpack_pieces(halo_ref, received_ref, layers, q, plan_ref[rim, width - 4])
         return carry
 
     lax.fori_loop(0, quads, unpack, 0)
@@ -207,13 +238,18 @@
         load.wait()
 
     def end(k, carry):
-        source_copy(k).wait()
+        source_copy(k, 0).wait()
+
+        @pl.when(double(k))
+        def _():
+            source_copy(k, 1).wait()
+
         return carry
 
     lax.fori_loop(0, local_count, end, 0)
     advect_block(
         plan_ref,
-        (lambda k, s, l: source_ref[k, l], lambda k, s, l: halo_ref[s - blocks, l]),
+        (take_local, lambda k, from_first, l: halo_ref[plan_ref[rim, k] - blocks, l]),
         coef_ref,
         near_ref,
         rate_ref,
@@ -254,10 +290,14 @@
 GROUP = 5
 
 
-def bulk_kernel(plan_ref, field_hbm, halo_hbm, rim_hbm, coef_hbm, near_hbm, rate_hbm, out_hbm, *refs):
+def bulk_kernel(
+    plan_ref, field_hbm, halo_hbm, rim_hbm, coef_hbm, near_hbm, rate_hbm, early_hbm, out_hbm, *refs
+):
+    del early_hbm
     field_ref, halo_ref, coef_ref, near_ref, rate_ref, acc_ref, new_ref, in_sem, out_sem = refs
     blocks = field_hbm.shape[2] // LANES
     width = plan_ref.shape[1]
+    pairs = (width - 4) // 2
     groups = (blocks - 1) // GROUP
     span = GROUP * LANES
 
@@ -294,8 +334,12 @@
             advect_block(
                 plan_ref,
                 (
-                    lambda k, s, l: field_ref[l, :, lanes_of(s)],
-                    lambda k, s, l: halo_ref[s - blocks, l],
+                    lambda k, from_first, l: jnp.where(
+                        from_first,
+                        field_ref[l, :, lanes_of(plan_ref[b, k])],
+                        field_ref[l, :, lanes_of(plan_ref[b, pairs + k])],
+                    ),
+                    lambda k, from_first, l: halo_ref[plan_ref[b, k] - blocks, l],
                 ),
                 coef_ref,
                 near_ref,
@@ -345,7 +389,7 @@
     return first, second
 
 
-def on_device(
+def transport(
     concentration, courant, diffusivity, release_rate, release_cell, neighbour, send_rows
 ):
     layers, tracers, cells = concentration.shape
@@ -371,7 +415,9 @@
 
     rows = LANES - rim + jnp.maximum(send_rows[0], 0)
     quads = peers * slots // LANES
-    lanes = jnp.broadcast_to(rows.reshape(quads, 1, LANES), (quads, 8, LANES))
+    of_quad = rows.reshape(quads, 4, slots)
+    turned = jnp.stack([jnp.roll(of_quad, j, axis=1) for j in range(4)], axis=1)
+    lanes = jnp.broadcast_to(turned.reshape(quads, 4, 1, LANES), (quads, 4, 8, LANES))
 
     send = pl.pallas_call(
         pack_kernel,
@@ -379,20 +425,38 @@
         grid=(1,),
         in_specs=[
             pl.BlockSpec((layers, tracers, LANES), lambda i: (0, 0, blocks - 1)),
-            pl.BlockSpec((quads, 8, LANES), lambda i: (0, 0, 0)),
+            pl.BlockSpec((quads, 4, 8, LANES), lambda i: (0, 0, 0, 0)),
         ],
         out_specs=pl.BlockSpec(message.shape, lambda i: (0, 0, 0, 0)),
         name="pack",
     )(concentration, lanes)
     received = lax.all_to_all(send, "region", 0, 0, tiled=True)
-    tables = [share(panel(0)), None]
 
     sources = blocks + halo_cells // LANES
     of_block = neighbour.reshape(3, blocks, LANES)
     source_id = jnp.arange(sources, dtype=jnp.int32)
     needed = jnp.any((of_block[..., None] >> 7) == source_id, axis=(0, 2))
+    block_id = jnp.arange(blocks, dtype=jnp.int32)
+    before, after = (block_id - 1) % blocks, (block_id + 1) % blocks
+    entries = jnp.moveaxis(of_block, 1, 0).reshape(blocks, 3 * LANES, 1)
+    lane_id = jnp.arange(LANES, dtype=jnp.int32)
+
+    def wanted(source):
+        return jnp.any(entries == source[:, None, None] * LANES + lane_id, axis=1)
+
+    want_before, want_after = wanted(before), wanted(after)
+    merged = (
+        jnp.any(want_before, axis=1)
+        & jnp.any(want_after, axis=1)
+        & ~jnp.any(want_before & want_after, axis=1)
+    )
+    second = merged[:, None] & (source_id == after[:, None])
+    needed = needed & ~second
     rank = jnp.sum(
         needed[:, None, :] & (source_id[None, None, :] < source_id[None, :, None]), axis=2
+    )
+    place = jnp.where(
+        second, jnp.sum(jnp.where(source_id == before[:, None], rank, 0), axis=1)[:, None], rank
     )
     listed = jnp.sum(
         jnp.where(
@@ -402,6 +466,11 @@
         ),
         axis=2,
     )
+    also = jnp.where(merged[:, None] & (listed == before[:, None]), after[:, None], listed)
+    place_of = jnp.sum(
+        jnp.where((of_block[..., None] >> 7) == source_id, place[None, :, None, :], 0), axis=3
+    )
+    near_id = jnp.where(of_block < 0, -1, place_of * LANES + (of_block & (LANES - 1)))
     home = release_cell - lax.axis_index("region") * cells
     released = jnp.any(
         (home[None, :] >> 7) == jnp.arange(blocks, dtype=jnp.int32)[:, None], axis=1
@@ -409,6 +478,8 @@
     plan = jnp.concatenate(
         [
             listed,
+            also,
+            jnp.broadcast_to(lax.axis_index("region") % 4, (blocks, 1)),
             jnp.sum(needed[:, :blocks], axis=1)[:, None],
             jnp.sum(needed, axis=1)[:, None],
             released[:, None],
@@ -417,8 +488,9 @@
     ).astype(jnp.int32)
     near = jnp.concatenate(
         [
-            jnp.broadcast_to(jnp.moveaxis(of_block, 1, 0)[:, :, None, :], (blocks, 3, 8, LANES)),
+            jnp.broadcast_to(jnp.moveaxis(near_id, 1, 0)[:, :, None, :], (blocks, 3, 8, LANES)),
             jnp.broadcast_to(home[None, None, :, None], (blocks, 1, 8, LANES)),
+            jnp.broadcast_to(want_before[:, None, None, :], (blocks, 1, 8, LANES)).astype(jnp.int32),
         ],
         axis=1,
     )
@@ -434,7 +506,7 @@
         return pl.pallas_call(
             prepare_kernel,
             out_shape=pltpu.HBM(coef_shape, f32),
-            in_specs=[scalars, full, full],
+            in_specs=[scalars] + [full] * len(table),
             out_specs=full,
             compiler_params=params(16),
             name="prepare",
@@ -450,40 +522,40 @@
         outs = (halo_shape, new_block) if last else (message, halo_shape, new_block)
         vmem = pltpu.VMEM
         scratch = [
-            vmem((blocks, *tile), f32),
+            vmem((2 * blocks, *tile), f32),
             vmem(tile, f32),
             vmem((1, *coef_shape[1:]), f32),
-            vmem((1, 4, 8, LANES), jnp.int32),
+            vmem((1, 5, 8, LANES), jnp.int32),
             vmem(tile, f32),
             vmem(halo_shape.shape, f32),
             vmem(tile, f32),
             vmem((1, *tile), f32),
         ]
         scratch += [] if last else [vmem(message.shape, f32)]
-        scratch += [dma((4,)), dma((blocks,)), dma((2 + quads,))]
+        scratch += [dma((4,)), dma((2 * blocks,)), dma((2 + quads,))]
         result = pl.pallas_call(
             functools.partial(rim_kernel, last),
             out_shape=outs,
             in_specs=[scalars, hbm, full, hbm, hbm, hbm] + ([] if last else [full]),
             out_specs=(hbm,) * len(outs),
             scratch_shapes=scratch,
-            compiler_params=params(16),
+            compiler_params=params(20),
             name="rim",
         )(plan, kept(field), received, kept(coef), near, rate, *(() if last else (lanes,)))
         return result if not last else (None, *result)
 
-    def bulk_step(field, halo, new, coef):
+    def bulk_step(field, halo, new, coef, early):
         vmem = pltpu.VMEM
         return pl.pallas_call(
             bulk_kernel,
             out_shape=pltpu.HBM(field.shape, f32),
-            in_specs=[scalars] + [hbm] * 6,
+            in_specs=[scalars] + [hbm] * 7,
             out_specs=hbm,
             scratch_shapes=[
                 vmem(field.shape, f32),
                 vmem(halo_shape.shape, f32),
                 vmem(coef_shape, f32),
-                vmem((blocks, 4, 8, LANES), jnp.int32),
+                vmem((blocks, 5, 8, LANES), jnp.int32),
                 vmem(tile, f32),
                 vmem((GROUP, *tile), f32),
                 vmem(field.shape, f32),
@@ -492,31 +564,34 @@
             ],
             compiler_params=params(24),
             name="bulk",
-        )(plan, kept(field), kept(halo), kept(new), kept(coef), near, rate)
+        )(plan, kept(field), kept(halo), kept(new), kept(coef), near, rate, kept(early))
 
     field = concentration
     per_hour = STEPS // HOURS
-    coef = None
+    coef = prepare(share(panel(0)))
     for step in range(STEPS):
-        h = step // per_hour
-        if step % per_hour == 0:
-            coef = prepare(tables[h])
         last = step == STEPS - 1
+        early = rate
         send, halo, new = rim_step(field, received, coef, last)
-        if step == 0:
-            later = panel(1)
-            later, _ = lax.optimization_barrier((later, new))
-            tables[1] = share(later)
         if not last:
             received = lax.all_to_all(send, "region", 0, 0, tiled=True)
-        field = bulk_step(field, halo, new, coef)
+        if step == 0:
+            later, _ = lax.optimization_barrier((panel(1), new))
+            row_panels = share_side(later, 0)
+        if step == 1:
+            panels = share_side(row_panels, 1)
+        if step == per_hour - 1:
+            early = later_coef = prepare((panels,))
+        field = bulk_step(field, halo, new, coef, early)
+        if step == per_hour - 1:
+            coef = later_coef
     return field
 
 
 def solution(mesh):
     both = ("region", "tracer")
     return jax.shard_map(
-        on_device,
+        transport,
         mesh=mesh,
         in_specs=(
             P(None, "tracer", "region"),

time: 247 us -> 242 us (0.980)
  waiting for transfers between devices: 34.2 us -> 57 us
  Pallas kernels: 132 us -> 111 us
  starting transfers between devices: 70.7 us -> 61.1 us
  other arithmetic: 3.51 us -> 6.32 us
    pallas_call x6, Pallas kernels: 91.8 us -> 72.8 us  [bulk_step(): pl.pallas_call(bulk_kernel, out_shape=pltpu.HBM(field.shape, f32), in_spe...]
    all_to_all x6, waiting for transfers between devices: 17.7 us -> 30.3 us  [transport(): received = lax.all_to_all(send, 'region', 0, 0, tiled=True)]
    ppermute x24 -> x18, waiting for transfers between devices: 16.5 us -> 26.6 us  [share_side(): shifts.append(lax.ppermute(value, 'tracer', pairs))]
    all_to_all x6, starting transfers between devices: 41.5 us -> 36.3 us  [transport(): received = lax.all_to_all(send, 'region', 0, 0, tiled=True)]
    ppermute x24 -> x18, starting transfers between devices: 29.2 us -> 24.8 us  [share_side(): shifts.append(lax.ppermute(value, 'tracer', pairs))]
  transfers between devices with their start and end apart: 30 -> 24, of which waited for: 14 -> 13; matrix products, arithmetic and copies ran while one was open for 3% -> 4% of each run, Pallas kernels for 35% -> 29%
where the time goes in v3:
time: 242 us; the launch traced here: 241 us
  Pallas kernels  111 us (46%)
  starting transfers between devices  61.1 us (25%)
  waiting for transfers between devices  57 us (24%)
  other arithmetic  6.32 us (3%)
  local copies, waits for them, and re-layouts  5.3 us (2%)
    pallas_call x6, Pallas kernels, bulk_step(): pl.pallas_call(bulk_kernel, out_shape=pltpu.HBM(field.shape, f32), in_spe...  72.8 us
    all_to_all x6, starting transfers between devices, transport(): received = lax.all_to_all(send, 'region', 0, 0, tiled=True)  36.3 us
    all_to_all x6, waiting for transfers between devices, transport(): received = lax.all_to_all(send, 'region', 0, 0, tiled=True)  30.3 us
    pallas_call x6, Pallas kernels, rim_step(): pl.pallas_call(functools.partial(rim_kernel, last), out_shape=outs, in_sp...  29.2 us
    ppermute x18, waiting for transfers between devices, share_side(): shifts.append(lax.ppermute(value, 'tracer', pairs))  26.6 us
    ppermute x18, starting transfers between devices, share_side(): shifts.append(lax.ppermute(value, 'tracer', pairs))  24.8 us
    pallas_call x2, Pallas kernels, prepare(): pl.pallas_call(prepare_kernel, out_shape=pltpu.HBM(coef_shape, f32), in_s...  6.19 us
  transfers between devices with their start and end apart: 24, of which 13 were waited for; matrix products, arithmetic and copies ran while one was open for 4% of the time, Pallas kernels for 29%

profile of v3, /device:TPU:1, one launch (start us, length us, event | category | flops | bytes accessed | tf_op | source)
XLA Modules:
  0.0 241.0 jit_solution(2122625097727521300)
XLA Ops:
  0.0 0.8 slice.56
  0.8 3.3 %collective-permute-start.2 = (f32[80,128]{1,0:T(8,128)S(1)}, f32[80,128]{1,0:T(8,128)S(1)}, u32[]{:S(2)}, u32[]{:S(2)}) collective-permute-start(f32[80,128]{1,0:T(8,128)S(1)} %bitcast.88), channel_id=1, source_target_pairs={{0,3},{1,0},{2,1},{3,2},{4,7},{5,4},{6,5},{7,6},{8,11},{9,8},{10,9... | collective-permute-start | bytes 122888 | tf_op jit(solution)/shard_map/ppermute | solution.py:381
  4.1 0.5 collective-permute-start.1
  4.6 0.6 collective-permute-start
  5.2 0.9 fusion.17
  6.2 0.9 fusion.18
  7.2 3.0 %collective-permute-start.7 = (f32[80,128]{1,0:T(8,128)S(1)}, f32[80,128]{1,0:T(8,128)S(1)}, u32[]{:S(2)}, u32[]{:S(2)}) collective-permute-start(f32[80,128]{1,0:T(8,128)S(1)} %fusion.2), channel_id=1, source_target_pairs={{0,8},{1,9},{2,10},{3,11},{4,12},{5,13},{6,14},{7,15},{8,0},{9,1},... | collective-permute-start | bytes 122888 | tf_op jit(solution)/shard_map/ppermute | solution.py:381
  10.2 0.4 collective-permute-start.6
  10.6 0.7 maximum_add_fusion
  11.7 0.6 broadcast_in_dim.67.lanes_ref.refs_0_
  12.3 2.5 %pack.1 = f32[16,10,8,128]{3,2,1,0:T(8,128)} custom-call(f32[40,8,2048]{2,1,0:T(8,128)} %field_hbm.3, s32[4,4,8,128]{3,2,1,0:T(8,128)} %broadcast_in_dim.67.lanes_ref.refs_0_), custom_call_target="tpu_custom_call" | custom-call | tf_op jit(solution)/shard_map/pack/pallas_call | solution.py:422
  14.8 10.7 %all-to-all-start = ((f32[16,10,8,128]{3,2,1,0:T(8,128)}), f32[16,10,8,128]{3,2,1,0:T(8,128)S(1)}, u32[]{:S(2)}, u32[]{:S(2)}) async-start(f32[16,10,8,128]{3,2,1,0:T(8,128)} %pack.1), calls=%async_computation | async-start | bytes 1310720 | tf_op jit(solution)/shard_map/all_to_all | solution.py:433
  25.6 0.4 fusion
  26.2 2.0 compare_reduce_fusion.1
  28.3 0.2 convert_reduce_fusion.1
  28.5 0.4 convert_reduce_fusion
  29.0 0.4 select_reduce_fusion.1
  29.5 0.2 select_reduce_fusion.2
  30.3 0.7 pad_add_fusion.near_hbm
  31.0 2.3 collective-permute-start.8
  33.6 0.7 collective-permute-start.3
  34.2 2.1 collective-permute-start.5
  36.4 1.7 collective-permute-start.10
  38.0 1.1 collective-permute-start.9
  39.1 1.2 collective-permute-done.4
  40.3 2.1 collective-permute-start.11
  42.9 1.5 collective-permute-done.3
  44.5 0.4 collective-permute-done.9
  44.9 1.7 collective-permute-done.11
  46.7 3.1 %prepare.2.coef_hbm = f32[16,7,40,128]{3,2,1,0:T(8,128)} custom-call(s32[2]{0:T(128)S(1)} %pad_add_fusion.4.home_ref, f32[4,4,80,128]{3,2,1,0:T(8,128)S(1)} %pad_maximum_fusion.1.refs_0_, f32[4,4,80,128]{3,2,1,0:T(8,128)S(1)} %pad_maximum_fusion.2.refs_1_), custom_call_target="tpu_custom_call" | custom-call | tf_op jit(solution)/shard_map/prepare/pallas_call | solution.py:506
  49.8 0.8 broadcast_in_dim.124.rate_hbm.early_hbm
  50.5 5.0 %rim.6 = (f32[16,10,8,128]{3,2,1,0:T(8,128)}, f32[4,40,8,128]{3,2,1,0:T(8,128)}, f32[40,8,128]{2,1,0:T(8,128)}) custom-call(s32[16,44]{1,0:T(8,128)S(1)} %concatenate.25.plan_ref, f32[40,8,2048]{2,1,0:T(8,128)} %field_hbm.3, f32[16,10,8,128]{3,2,1,0:T(8,128)S(1)} %all-to-all-done.received_ref, f32[16,7,40,128]{3,2,1,0:T(8,128)} %prepare.2.coef_hbm, ...), custom_call_target="tpu_custom_call" | custom-call | tf_op jit(solution)/shard_map/rim/pallas_call | solution.py:536
  55.5 8.7 %all-to-all-start.1 = ((f32[16,10,8,128]{3,2,1,0:T(8,128)}), f32[16,10,8,128]{3,2,1,0:T(8,128)S(1)}, u32[]{:S(2)}, u32[]{:S(2)}) async-start(f32[16,10,8,128]{3,2,1,0:T(8,128)} %get-tuple-element.25), calls=%async_computation.1 | async-start | bytes 1310720 | tf_op jit(solution)/shard_map/all_to_all | solution.py:577
  64.2 12.1 %bulk.6.field_hbm = f32[40,8,2048]{2,1,0:T(8,128)} custom-call(s32[16,44]{1,0:T(8,128)S(1)} %concatenate.25.plan_ref, f32[40,8,2048]{2,1,0:T(8,128)} %field_hbm.3, f32[4,40,8,128]{3,2,1,0:T(8,128)} %get-tuple-element.23.halo_hbm, f32[40,8,128]{2,1,0:T(8,128)} %get-tuple-element.24.rim_hbm, f32[16,7,40,128]{3,2,1,0:T(8,128)} %prepare.2.coef_hbm, ...), custom_call_target="tpu_custom_call" | custom-call | tf_op jit(solution)/shard_map/bulk/pallas_call | solution.py:549
  76.3 7.8 %all-to-all-done.1.received_ref = f32[16,10,8,128]{3,2,1,0:T(8,128)S(1)} async-done(((f32[16,10,8,128]{3,2,1,0:T(8,128)}), f32[16,10,8,128]{3,2,1,0:T(8,128)S(1)}, u32[]{:S(2)}, u32[]{:S(2)}) %all-to-all-start.1) | async-done | bytes 655392 | tf_op jit(solution)/shard_map/all_to_all | solution.py:577
  84.1 5.0 %rim.7 = (f32[16,10,8,128]{3,2,1,0:T(8,128)}, f32[4,40,8,128]{3,2,1,0:T(8,128)}, f32[40,8,128]{2,1,0:T(8,128)}) custom-call(s32[16,44]{1,0:T(8,128)S(1)} %concatenate.25.plan_ref, f32[40,8,2048]{2,1,0:T(8,128)} %bulk.6.field_hbm, f32[16,10,8,128]{3,2,1,0:T(8,128)S(1)} %all-to-all-done.1.received_ref, f32[16,7,40,128]{3,2,1,0:T(8,128)} %prepare.2.coef_hbm, ...), custom_call_target="tpu_custom_call" | custom-call | tf_op jit(solution)/shard_map/rim/pallas_call | solution.py:536
  89.1 3.5 %all-to-all-start.2 = ((f32[16,10,8,128]{3,2,1,0:T(8,128)}), f32[16,10,8,128]{3,2,1,0:T(8,128)S(1)}, u32[]{:S(2)}, u32[]{:S(2)}) async-start(f32[16,10,8,128]{3,2,1,0:T(8,128)} %get-tuple-element.28), calls=%async_computation.2 | async-start | bytes 1310720 | tf_op jit(solution)/shard_map/all_to_all | solution.py:577
  92.6 12.2 %bulk.7.field_hbm = f32[40,8,2048]{2,1,0:T(8,128)} custom-call(s32[16,44]{1,0:T(8,128)S(1)} %concatenate.25.plan_ref, f32[40,8,2048]{2,1,0:T(8,128)} %bulk.6.field_hbm, f32[4,40,8,128]{3,2,1,0:T(8,128)} %get-tuple-element.26.halo_hbm, f32[40,8,128]{2,1,0:T(8,128)} %get-tuple-element.27.rim_hbm, f32[16,7,40,128]{3,2,1,0:T(8,128)} %prepare.2.coef_hbm, ...), custom_call_target="tpu_custom_call" | custom-call | tf_op jit(solution)/shard_map/bulk/pallas_call | solution.py:549
  104.7 7.4 %all-to-all-done.2.received_ref = f32[16,10,8,128]{3,2,1,0:T(8,128)S(1)} async-done(((f32[16,10,8,128]{3,2,1,0:T(8,128)}), f32[16,10,8,128]{3,2,1,0:T(8,128)S(1)}, u32[]{:S(2)}, u32[]{:S(2)}) %all-to-all-start.2) | async-done | bytes 655392 | tf_op jit(solution)/shard_map/all_to_all | solution.py:577
  112.1 4.9 %rim.8 = (f32[16,10,8,128]{3,2,1,0:T(8,128)}, f32[4,40,8,128]{3,2,1,0:T(8,128)}, f32[40,8,128]{2,1,0:T(8,128)}) custom-call(s32[16,44]{1,0:T(8,128)S(1)} %concatenate.25.plan_ref, f32[40,8,2048]{2,1,0:T(8,128)} %bulk.7.field_hbm, f32[16,10,8,128]{3,2,1,0:T(8,128)S(1)} %all-to-all-done.2.received_ref, f32[16,7,40,128]{3,2,1,0:T(8,128)} %prepare.2.coef_hbm, ...), custom_call_target="tpu_custom_call" | custom-call | tf_op jit(solution)/shard_map/rim/pallas_call | solution.py:536
  117.1 3.5 %all-to-all-start.3 = ((f32[16,10,8,128]{3,2,1,0:T(8,128)}), f32[16,10,8,128]{3,2,1,0:T(8,128)S(1)}, u32[]{:S(2)}, u32[]{:S(2)}) async-start(f32[16,10,8,128]{3,2,1,0:T(8,128)} %get-tuple-element.32), calls=%async_computation.3 | async-start | bytes 1310720 | tf_op jit(solution)/shard_map/all_to_all | solution.py:577
  120.7 2.9 %collective-permute-start.14 = (f32[160,128]{1,0:T(8,128)S(1)}, f32[160,128]{1,0:T(8,128)S(1)}, u32[]{:S(2)}, u32[]{:S(2)}) collective-permute-start(f32[160,128]{1,0:T(8,128)S(1)} %maximum_maximum_fusion), channel_id=1, source_target_pairs={{0,3},{1,0},{2,1},{3,2},{4,7},{5,4},{6,5},{7,6},{8,11},{9,8},{10,9... | collective-permute-start | bytes 245768 | tf_op jit(solution)/shard_map/ppermute | solution.py:381
  123.6 0.5 collective-permute-start.13
  124.1 0.2 collective-permute-start.12
  124.3 3.1 %collective-permute-done.14 = f32[160,128]{1,0:T(8,128)S(1)} collective-permute-done((f32[160,128]{1,0:T(8,128)S(1)}, f32[160,128]{1,0:T(8,128)S(1)}, u32[]{:S(2)}, u32[]{:S(2)}) %collective-permute-start.14) | collective-permute-done | bytes 81952 | tf_op jit(solution)/shard_map/ppermute | solution.py:381
  127.4 1.8 collective-permute-done.13
  129.2 2.0 collective-permute-done.12
  131.3 0.8 collective-permute-start.16
  132.1 2.2 collective-permute-start.15
  134.4 0.4 collective-permute-start.17
  134.8 6.9 %collective-permute-done.16 = f32[4,160,128]{2,1,0:T(8,128)S(1)} collective-permute-done((f32[4,160,128]{2,1,0:T(8,128)S(1)}, f32[4,160,128]{2,1,0:T(8,128)S(1)}, u32[]{:S(2)}, u32[]{:S(2)}) %collective-permute-start.16) | collective-permute-done | bytes 327712 | tf_op jit(solution)/shard_map/ppermute | solution.py:381
  141.8 7.8 %collective-permute-done.15 = f32[4,160,128]{2,1,0:T(8,128)S(1)} collective-permute-done((f32[4,160,128]{2,1,0:T(8,128)S(1)}, f32[4,160,128]{2,1,0:T(8,128)S(1)}, u32[]{:S(2)}, u32[]{:S(2)}) %collective-permute-start.15) | collective-permute-done | bytes 327712 | tf_op jit(solution)/shard_map/ppermute | solution.py:381
  149.6 3.1 %prepare.3.early_hbm.coef_hbm = f32[16,7,40,128]{3,2,1,0:T(8,128)} custom-call(s32[2]{0:T(128)S(1)} %pad_add_fusion.4.home_ref, f32[4,4,160,128]{3,2,1,0:T(8,128)S(1)} %pad_maximum_fusion.refs_0_), custom_call_target="tpu_custom_call" | custom-call | tf_op jit(solution)/shard_map/prepare/pallas_call | solution.py:506
  152.7 12.1 %bulk.8.field_hbm = f32[40,8,2048]{2,1,0:T(8,128)} custom-call(s32[16,44]{1,0:T(8,128)S(1)} %concatenate.25.plan_ref, f32[40,8,2048]{2,1,0:T(8,128)} %bulk.7.field_hbm, f32[4,40,8,128]{3,2,1,0:T(8,128)} %get-tuple-element.29.halo_hbm, f32[40,8,128]{2,1,0:T(8,128)} %get-tuple-element.30.rim_hbm, f32[16,7,40,128]{3,2,1,0:T(8,128)} %prepare.2.coef_hbm, ...), custom_call_target="tpu_custom_call" | custom-call | tf_op jit(solution)/shard_map/bulk/pallas_call | solution.py:549
  164.9 4.9 %rim.9 = (f32[16,10,8,128]{3,2,1,0:T(8,128)}, f32[4,40,8,128]{3,2,1,0:T(8,128)}, f32[40,8,128]{2,1,0:T(8,128)}) custom-call(s32[16,44]{1,0:T(8,128)S(1)} %concatenate.25.plan_ref, f32[40,8,2048]{2,1,0:T(8,128)} %bulk.8.field_hbm, f32[16,10,8,128]{3,2,1,0:T(8,128)S(1)} %all-to-all-done.3.received_ref, f32[16,7,40,128]{3,2,1,0:T(8,128)} %prepare.3.early_hbm.coef_hbm, ...), custom_call_target="tpu_custom_call" | custom-call | tf_op jit(solution)/shard_map/rim/pallas_call | solution.py:536
  169.8 6.4 %all-to-all-start.4 = ((f32[16,10,8,128]{3,2,1,0:T(8,128)}), f32[16,10,8,128]{3,2,1,0:T(8,128)S(1)}, u32[]{:S(2)}, u32[]{:S(2)}) async-start(f32[16,10,8,128]{3,2,1,0:T(8,128)} %get-tuple-element.35), calls=%async_computation.4 | async-start | bytes 1310720 | tf_op jit(solution)/shard_map/all_to_all | solution.py:577
  176.3 12.2 %bulk.9.field_hbm = f32[40,8,2048]{2,1,0:T(8,128)} custom-call(s32[16,44]{1,0:T(8,128)S(1)} %concatenate.25.plan_ref, f32[40,8,2048]{2,1,0:T(8,128)} %bulk.8.field_hbm, f32[4,40,8,128]{3,2,1,0:T(8,128)} %get-tuple-element.33.halo_hbm, f32[40,8,128]{2,1,0:T(8,128)} %get-tuple-element.34.rim_hbm, f32[16,7,40,128]{3,2,1,0:T(8,128)} %prepare.3.early_hbm.coef_hbm, ...), custom_call_target="tpu_custom_call" | custom-call | tf_op jit(solution)/shard_map/bulk/pallas_call | solution.py:549
  188.4 7.8 %all-to-all-done.4.received_ref = f32[16,10,8,128]{3,2,1,0:T(8,128)S(1)} async-done(((f32[16,10,8,128]{3,2,1,0:T(8,128)}), f32[16,10,8,128]{3,2,1,0:T(8,128)S(1)}, u32[]{:S(2)}, u32[]{:S(2)}) %all-to-all-start.4) | async-done | bytes 655392 | tf_op jit(solution)/shard_map/all_to_all | solution.py:577
  196.2 5.2 %rim.10 = (f32[16,10,8,128]{3,2,1,0:T(8,128)}, f32[4,40,8,128]{3,2,1,0:T(8,128)}, f32[40,8,128]{2,1,0:T(8,128)}) custom-call(s32[16,44]{1,0:T(8,128)S(1)} %concatenate.25.plan_ref, f32[40,8,2048]{2,1,0:T(8,128)} %bulk.9.field_hbm, f32[16,10,8,128]{3,2,1,0:T(8,128)S(1)} %all-to-all-done.4.received_ref, f32[16,7,40,128]{3,2,1,0:T(8,128)} %prepare.3.early_hbm.coef_hbm, ...), custom_call_target="tpu_custom_call" | custom-call | tf_op jit(solution)/shard_map/rim/pallas_call | solution.py:536
  201.4 3.5 %all-to-all-start.5 = ((f32[16,10,8,128]{3,2,1,0:T(8,128)}), f32[16,10,8,128]{3,2,1,0:T(8,128)S(1)}, u32[]{:S(2)}, u32[]{:S(2)}) async-start(f32[16,10,8,128]{3,2,1,0:T(8,128)} %get-tuple-element.38), calls=%async_computation.5 | async-start | bytes 1310720 | tf_op jit(solution)/shard_map/all_to_all | solution.py:577
  204.9 12.2 %bulk.10.field_hbm = f32[40,8,2048]{2,1,0:T(8,128)} custom-call(s32[16,44]{1,0:T(8,128)S(1)} %concatenate.25.plan_ref, f32[40,8,2048]{2,1,0:T(8,128)} %bulk.9.field_hbm, f32[4,40,8,128]{3,2,1,0:T(8,128)} %get-tuple-element.36.halo_hbm, f32[40,8,128]{2,1,0:T(8,128)} %get-tuple-element.37.rim_hbm, f32[16,7,40,128]{3,2,1,0:T(8,128)} %prepare.3.early_hbm.coef_hbm, ...), custom_call_target="tpu_custom_call" | custom-call | tf_op jit(solution)/shard_map/bulk/pallas_call | solution.py:549
  217.1 7.4 %all-to-all-done.5.received_ref = f32[16,10,8,128]{3,2,1,0:T(8,128)S(1)} async-done(((f32[16,10,8,128]{3,2,1,0:T(8,128)}), f32[16,10,8,128]{3,2,1,0:T(8,128)S(1)}, u32[]{:S(2)}, u32[]{:S(2)}) %all-to-all-start.5) | async-done | bytes 655392 | tf_op jit(solution)/shard_map/all_to_all | solution.py:577
  224.5 4.2 %rim.11 = (f32[4,40,8,128]{3,2,1,0:T(8,128)}, f32[40,8,128]{2,1,0:T(8,128)}) custom-call(s32[16,44]{1,0:T(8,128)S(1)} %concatenate.25.plan_ref, f32[40,8,2048]{2,1,0:T(8,128)} %bulk.10.field_hbm, f32[16,10,8,128]{3,2,1,0:T(8,128)S(1)} %all-to-all-done.5.received_ref, f32[16,7,40,128]{3,2,1,0:T(8,128)} %prepare.3.early_hbm.coef_hbm, ...), custom_call_target="tpu_custom_call" | custom-call | tf_op jit(solution)/shard_map/rim/pallas_call | solution.py:536
  228.7 12.1 %bulk.11 = f32[40,8,2048]{2,1,0:T(8,128)} custom-call(s32[16,44]{1,0:T(8,128)S(1)} %concatenate.25.plan_ref, f32[40,8,2048]{2,1,0:T(8,128)} %bulk.10.field_hbm, f32[4,40,8,128]{3,2,1,0:T(8,128)} %get-tuple-element.39.halo_hbm, f32[40,8,128]{2,1,0:T(8,128)} %get-tuple-element.40.rim_hbm, f32[16,7,40,128]{3,2,1,0:T(8,128)} %prepare.3.early_hbm.coef_hbm, ...), custom_call_target="tpu_custom_call" | custom-call | tf_op jit(solution)/shard_map/bulk/pallas_call | solution.py:549
  (73 shorter events, 2.7 us)
Async XLA Ops:
  0.8 30.2 %collective-permute-start.2 = (f32[80,128]{1,0:T(8,128)S(1)}, f32[80,128]{1,0:T(8,128)S(1)}, u32[]{:S(2)}, u32[]{:S(2)}) collective-permute-start(f32[80,128]{1,0:T(8,128)S(1)} %bitcast.88), channel_id=1, source_target_pairs={{0,3},{1,0},{2,1},{3,2},{4,7},{5,4},{6,5},{7,6},{8,11},{9,8},{10,9... | collective-permute-start | bytes 122888 | tf_op jit(solution)/shard_map/ppermute | solution.py:381
  4.1 29.2 %collective-permute-start.1 = (f32[80,128]{1,0:T(8,128)S(1)}, f32[80,128]{1,0:T(8,128)S(1)}, u32[]{:S(2)}, u32[]{:S(2)}) collective-permute-start(f32[80,128]{1,0:T(8,128)S(1)} %bitcast.89), channel_id=1, source_target_pairs={{0,2},{1,3},{2,0},{3,1},{4,6},{5,7},{6,4},{7,5},{8,10},{9,11},{10,... | collective-permute-start | bytes 122888 | tf_op jit(solution)/shard_map/ppermute | solution.py:381
  4.6 28.7 %collective-permute-start = (f32[80,128]{1,0:T(8,128)S(1)}, f32[80,128]{1,0:T(8,128)S(1)}, u32[]{:S(2)}, u32[]{:S(2)}) collective-permute-start(f32[80,128]{1,0:T(8,128)S(1)} %bitcast.90), channel_id=1, source_target_pairs={{0,1},{1,2},{2,3},{3,0},{4,5},{5,6},{6,7},{7,4},{8,9},{9,10},{10,1... | collective-permute-start | bytes 122888 | tf_op jit(solution)/shard_map/ppermute | solution.py:381
  6.1 19.5 %copy-start.1 = (s32[3,2048]{1,0:T(4,128)S(1)}, s32[3,2048]{1,0:T(4,128)}, u32[]{:S(2)}) copy-start(s32[3,2048]{1,0:T(4,128)} %param.12) | copy-start | bytes 73732
  7.2 27.0 %collective-permute-start.7 = (f32[80,128]{1,0:T(8,128)S(1)}, f32[80,128]{1,0:T(8,128)S(1)}, u32[]{:S(2)}, u32[]{:S(2)}) collective-permute-start(f32[80,128]{1,0:T(8,128)S(1)} %fusion.2), channel_id=1, source_target_pairs={{0,8},{1,9},{2,10},{3,11},{4,12},{5,13},{6,14},{7,15},{8,0},{9,1},... | collective-permute-start | bytes 122888 | tf_op jit(solution)/shard_map/ppermute | solution.py:381
  10.2 26.1 %collective-permute-start.6 = (f32[80,128]{1,0:T(8,128)S(1)}, f32[80,128]{1,0:T(8,128)S(1)}, u32[]{:S(2)}, u32[]{:S(2)}) collective-permute-start(f32[80,128]{1,0:T(8,128)S(1)} %fusion.2), channel_id=1, source_target_pairs={{0,4},{1,5},{2,6},{3,7},{4,8},{5,9},{6,10},{7,11},{8,12},{9,13},{1... | collective-permute-start | bytes 122888 | tf_op jit(solution)/shard_map/ppermute | solution.py:381
  12.3 17.7 %copy-start.3 = (s32[8]{0:T(128)S(1)}, s32[8]{0:T(128)}, u32[]{:S(2)}) copy-start(s32[8]{0:T(128)} %param.11) | copy-start | bytes 100
  14.8 27.8 %copy-start.2 = (f32[40,8]{0,1:T(8,128)S(1)}, f32[40,8]{0,1:T(8,128)}, u32[]{:S(2)}) copy-start(f32[40,8]{0,1:T(8,128)} %param.10) | copy-start | bytes 3844
  14.8 35.0 %all-to-all-start = ((f32[16,10,8,128]{3,2,1,0:T(8,128)}), f32[16,10,8,128]{3,2,1,0:T(8,128)S(1)}, u32[]{:S(2)}, u32[]{:S(2)}) async-start(f32[16,10,8,128]{3,2,1,0:T(8,128)} %pack.1), calls=%async_computation | async-start | bytes 1310720 | tf_op jit(solution)/shard_map/all_to_all | solution.py:433
  31.0 5.3 %collective-permute-start.8 = (f32[80,128]{1,0:T(8,128)S(1)}, f32[80,128]{1,0:T(8,128)S(1)}, u32[]{:S(2)}, u32[]{:S(2)}) collective-permute-start(f32[80,128]{1,0:T(8,128)S(1)} %fusion.2), channel_id=1, source_target_pairs={{0,12},{1,13},{2,14},{3,15},{4,0},{5,1},{6,2},{7,3},{8,4},{9,5},{1... | collective-permute-start | bytes 122888 | tf_op jit(solution)/shard_map/ppermute | solution.py:381
  33.3 7.0 %collective-permute-start.4 = (f32[4,80,128]{2,1,0:T(8,128)S(1)}, f32[4,80,128]{2,1,0:T(8,128)S(1)}, u32[]{:S(2)}, u32[]{:S(2)}) collective-permute-start(f32[4,80,128]{2,1,0:T(8,128)S(1)} %get-tuple-element.56), channel_id=1, source_target_pairs={{0,8},{1,9},{2,10},{3,11},{4,12},{5,13},{6,14},{7,15},{8,0},{9,1},... | collective-permute-start | bytes 491528 | tf_op jit(solution)/shard_map/ppermute | solution.py:381
  33.6 10.8 %collective-permute-start.3 = (f32[4,80,128]{2,1,0:T(8,128)S(1)}, f32[4,80,128]{2,1,0:T(8,128)S(1)}, u32[]{:S(2)}, u32[]{:S(2)}) collective-permute-start(f32[4,80,128]{2,1,0:T(8,128)S(1)} %get-tuple-element.56), channel_id=1, source_target_pairs={{0,4},{1,5},{2,6},{3,7},{4,8},{5,9},{6,10},{7,11},{8,12},{9,13},{1... | collective-permute-start | bytes 491528 | tf_op jit(solution)/shard_map/ppermute | solution.py:381
  34.2 10.2 %collective-permute-start.5 = (f32[4,80,128]{2,1,0:T(8,128)S(1)}, f32[4,80,128]{2,1,0:T(8,128)S(1)}, u32[]{:S(2)}, u32[]{:S(2)}) collective-permute-start(f32[4,80,128]{2,1,0:T(8,128)S(1)} %get-tuple-element.56), channel_id=1, source_target_pairs={{0,12},{1,13},{2,14},{3,15},{4,0},{5,1},{6,2},{7,3},{8,4},{9,5},{1... | collective-permute-start | bytes 491528 | tf_op jit(solution)/shard_map/ppermute | solution.py:381
  36.4 8.1 %collective-permute-start.10 = (f32[4,80,128]{2,1,0:T(8,128)S(1)}, f32[4,80,128]{2,1,0:T(8,128)S(1)}, u32[]{:S(2)}, u32[]{:S(2)}) collective-permute-start(f32[4,80,128]{2,1,0:T(8,128)S(1)} %get-tuple-element.54), channel_id=1, source_target_pairs={{0,2},{1,3},{2,0},{3,1},{4,6},{5,7},{6,4},{7,5},{8,10},{9,11},{10,... | collective-permute-start | bytes 491528 | tf_op jit(solution)/shard_map/ppermute | solution.py:381
  38.0 6.9 %collective-permute-start.9 = (f32[4,80,128]{2,1,0:T(8,128)S(1)}, f32[4,80,128]{2,1,0:T(8,128)S(1)}, u32[]{:S(2)}, u32[]{:S(2)}) collective-permute-start(f32[4,80,128]{2,1,0:T(8,128)S(1)} %get-tuple-element.54), channel_id=1, source_target_pairs={{0,1},{1,2},{2,3},{3,0},{4,5},{5,6},{6,7},{7,4},{8,9},{9,10},{10,1... | collective-permute-start | bytes 491528 | tf_op jit(solution)/shard_map/ppermute | solution.py:381
  40.3 6.3 %collective-permute-start.11 = (f32[4,80,128]{2,1,0:T(8,128)S(1)}, f32[4,80,128]{2,1,0:T(8,128)S(1)}, u32[]{:S(2)}, u32[]{:S(2)}) collective-permute-start(f32[4,80,128]{2,1,0:T(8,128)S(1)} %get-tuple-element.54), channel_id=1, source_target_pairs={{0,3},{1,0},{2,1},{3,2},{4,7},{5,4},{6,5},{7,6},{8,11},{9,8},{10,9... | collective-permute-start | bytes 491528 | tf_op jit(solution)/shard_map/ppermute | solution.py:381
  44.5 6.1 %copy-start = (s32[4,4,8,128]{3,2,1,0:T(8,128)S(1)}, s32[4,4,8,128]{3,2,1,0:T(8,128)}, u32[]{:S(2)}) copy-start(s32[4,4,8,128]{3,2,1,0:T(8,128)} %broadcast_in_dim.67.lanes_ref.refs_0_) | copy-start | bytes 196612
  55.5 28.6 %all-to-all-start.1 = ((f32[16,10,8,128]{3,2,1,0:T(8,128)}), f32[16,10,8,128]{3,2,1,0:T(8,128)S(1)}, u32[]{:S(2)}, u32[]{:S(2)}) async-start(f32[16,10,8,128]{3,2,1,0:T(8,128)} %get-tuple-element.25), calls=%async_computation.1 | async-start | bytes 1310720 | tf_op jit(solution)/shard_map/all_to_all | solution.py:577
  89.1 23.1 %all-to-all-start.2 = ((f32[16,10,8,128]{3,2,1,0:T(8,128)}), f32[16,10,8,128]{3,2,1,0:T(8,128)S(1)}, u32[]{:S(2)}, u32[]{:S(2)}) async-start(f32[16,10,8,128]{3,2,1,0:T(8,128)} %get-tuple-element.28), calls=%async_computation.2 | async-start | bytes 1310720 | tf_op jit(solution)/shard_map/all_to_all | solution.py:577
  117.1 47.8 %all-to-all-start.3 = ((f32[16,10,8,128]{3,2,1,0:T(8,128)}), f32[16,10,8,128]{3,2,1,0:T(8,128)S(1)}, u32[]{:S(2)}, u32[]{:S(2)}) async-start(f32[16,10,8,128]{3,2,1,0:T(8,128)} %get-tuple-element.32), calls=%async_computation.3 | async-start | bytes 1310720 | tf_op jit(solution)/shard_map/all_to_all | solution.py:577
  120.7 6.7 %collective-permute-start.14 = (f32[160,128]{1,0:T(8,128)S(1)}, f32[160,128]{1,0:T(8,128)S(1)}, u32[]{:S(2)}, u32[]{:S(2)}) collective-permute-start(f32[160,128]{1,0:T(8,128)S(1)} %maximum_maximum_fusion), channel_id=1, source_target_pairs={{0,3},{1,0},{2,1},{3,2},{4,7},{5,4},{6,5},{7,6},{8,11},{9,8},{10,9... | collective-permute-start | bytes 245768 | tf_op jit(solution)/shard_map/ppermute | solution.py:381
  123.6 5.6 %collective-permute-start.13 = (f32[160,128]{1,0:T(8,128)S(1)}, f32[160,128]{1,0:T(8,128)S(1)}, u32[]{:S(2)}, u32[]{:S(2)}) collective-permute-start(f32[160,128]{1,0:T(8,128)S(1)} %maximum_maximum_fusion), channel_id=1, source_target_pairs={{0,2},{1,3},{2,0},{3,1},{4,6},{5,7},{6,4},{7,5},{8,10},{9,11},{10,... | collective-permute-start | bytes 245768 | tf_op jit(solution)/shard_map/ppermute | solution.py:381
  124.1 7.1 %collective-permute-start.12 = (f32[160,128]{1,0:T(8,128)S(1)}, f32[160,128]{1,0:T(8,128)S(1)}, u32[]{:S(2)}, u32[]{:S(2)}) collective-permute-start(f32[160,128]{1,0:T(8,128)S(1)} %maximum_maximum_fusion), channel_id=1, source_target_pairs={{0,1},{1,2},{2,3},{3,0},{4,5},{5,6},{6,7},{7,4},{8,9},{9,10},{10,1... | collective-permute-start | bytes 245768 | tf_op jit(solution)/shard_map/ppermute | solution.py:381
  131.3 10.4 %collective-permute-start.16 = (f32[4,160,128]{2,1,0:T(8,128)S(1)}, f32[4,160,128]{2,1,0:T(8,128)S(1)}, u32[]{:S(2)}, u32[]{:S(2)}) collective-permute-start(f32[4,160,128]{2,1,0:T(8,128)S(1)} %get-tuple-element.52), channel_id=1, source_target_pairs={{0,8},{1,9},{2,10},{3,11},{4,12},{5,13},{6,14},{7,15},{8,0},{9,1},... | collective-permute-start | bytes 983048 | tf_op jit(solution)/shard_map/ppermute | solution.py:381
  132.1 17.4 %collective-permute-start.15 = (f32[4,160,128]{2,1,0:T(8,128)S(1)}, f32[4,160,128]{2,1,0:T(8,128)S(1)}, u32[]{:S(2)}, u32[]{:S(2)}) collective-permute-start(f32[4,160,128]{2,1,0:T(8,128)S(1)} %get-tuple-element.52), channel_id=1, source_target_pairs={{0,4},{1,5},{2,6},{3,7},{4,8},{5,9},{6,10},{7,11},{8,12},{9,13},{1... | collective-permute-start | bytes 983048 | tf_op jit(solution)/shard_map/ppermute | solution.py:381
  134.4 15.2 %collective-permute-start.17 = (f32[4,160,128]{2,1,0:T(8,128)S(1)}, f32[4,160,128]{2,1,0:T(8,128)S(1)}, u32[]{:S(2)}, u32[]{:S(2)}) collective-permute-start(f32[4,160,128]{2,1,0:T(8,128)S(1)} %get-tuple-element.52), channel_id=1, source_target_pairs={{0,12},{1,13},{2,14},{3,15},{4,0},{5,1},{6,2},{7,3},{8,4},{9,5},{1... | collective-permute-start | bytes 983048 | tf_op jit(solution)/shard_map/ppermute | solution.py:381
  169.8 26.4 %all-to-all-start.4 = ((f32[16,10,8,128]{3,2,1,0:T(8,128)}), f32[16,10,8,128]{3,2,1,0:T(8,128)S(1)}, u32[]{:S(2)}, u32[]{:S(2)}) async-start(f32[16,10,8,128]{3,2,1,0:T(8,128)} %get-tuple-element.35), calls=%async_computation.4 | async-start | bytes 1310720 | tf_op jit(solution)/shard_map/all_to_all | solution.py:577
  201.4 23.1 %all-to-all-start.5 = ((f32[16,10,8,128]{3,2,1,0:T(8,128)}), f32[16,10,8,128]{3,2,1,0:T(8,128)S(1)}, u32[]{:S(2)}, u32[]{:S(2)}) async-start(f32[16,10,8,128]{3,2,1,0:T(8,128)} %get-tuple-element.38), calls=%async_computation.5 | async-start | bytes 1310720 | tf_op jit(solution)/shard_map/all_to_all | solution.py:577

commit v4 on v3

--- a/solution.py
+++ b/solution.py
@@ -113,10 +113,7 @@
     return coef_ref[c, kind, pl.ds(l, 8, stride=0), :]
 
 
-CHUNK = 40
-
-
-def advect_block(plan_ref, load, coef_ref, near_ref, rate_ref, acc_ref, i, b, c, n, counts):
+def start_block(plan_ref, coef_ref, near_ref, rate_ref, acc_ref, i, b, c, n):
     layers = acc_ref.shape[1]
     width = plan_ref.shape[1]
     for l in range(layers):
@@ -129,28 +126,32 @@
         for l in range(layers):
             acc_ref[i, l] = jnp.where(here, rate_ref[l], 0.0) * row(coef_ref, c, INV, l)
 
-    def add_from(take):
-        def one(k, carry):
-            lanes = [near_ref[n, f] & (LANES - 1) for f in range(3)]
-            inside = [(near_ref[n, f] >> 7) == k for f in range(3)]
-            from_first = near_ref[n, 4] != 0
-            for start in range(0, layers, CHUNK):
-                chunk = range(start, start + CHUNK)
-                values = [take(k, from_first, l) for l in chunk]
-                total = [acc_ref[i, l] for l in chunk]
-                for f in range(3):
-                    for j, l in enumerate(chunk):
-                        edge = jnp.where(inside[f], pick_lanes(values[j], lanes[f]), 0.0)
-                        total[j] = total[j] + row(coef_ref, c, EDGE + f, l) * edge
-                for j, l in enumerate(chunk):
-                    acc_ref[i, l] = total[j]
-            return carry
-
-        return one
-
+
+def add_edges(take, coef_ref, near_ref, acc_ref, i, c, n, low, high):
+    layers = acc_ref.shape[1]
+
+    def one(k, carry):
+        lanes = [near_ref[n, f] & (LANES - 1) for f in range(3)]
+        inside = [(near_ref[n, f] >> 7) == k for f in range(3)]
+        from_first = near_ref[n, 4] != 0
+        values = [take(k, from_first, l) for l in range(layers)]
+        total = [acc_ref[i, l] for l in range(layers)]
+        for f in range(3):
+            for l in range(layers):
+                edge = jnp.where(inside[f], pick_lanes(values[l], lanes[f]), 0.0)
+                total[l] = total[l] + row(coef_ref, c, EDGE + f, l) * edge
+        for l in range(layers):
+            acc_ref[i, l] = total[l]
+        return carry
+
+    lax.fori_loop(low, high, one, 0)
+
+
+def advect_block(plan_ref, load, coef_ref, near_ref, rate_ref, acc_ref, i, b, c, n, counts):
+    start_block(plan_ref, coef_ref, near_ref, rate_ref, acc_ref, i, b, c, n)
     low = 0
     for take, high in zip(load, counts):
-        lax.fori_loop(low, high, add_from(take), 0)
+        add_edges(take, coef_ref, near_ref, acc_ref, i, c, n, low, high)
         low = high
 
 
@@ -159,7 +160,7 @@
     part = [None] * len(where_coef)
     for l in range(layers):
         for i, c in enumerate(where_coef):
-            now = row(coef_ref, c, OWN, l) * own(i, l) + acc_ref[i, l]
+            now = own(i, l, c) + acc_ref[i, l]
             if l > 0:
                 now = now + row(coef_ref, c, CARRY, l) * part[i]
             part[i] = now
@@ -170,6 +171,25 @@
     for l in range(layers - 2, -1, -1):
         for i, c in enumerate(where_coef):
             part[i] = acc_ref[i, l] + row(coef_ref, c, RATIO, l) * part[i]
+            store(i, l, part[i])
+
+
+def solve_parts(coef_ref, acc_ref, store, where):
+    layers = acc_ref.shape[1]
+    part = [None] * len(where)
+    for l in range(layers):
+        for i, b in enumerate(where):
+            now = acc_ref[b, l]
+            if l > 0:
+                now = now + row(coef_ref, b, CARRY, l) * part[i]
+            part[i] = now
+            if l < layers - 1:
+                acc_ref[b, l] = now
+            else:
+                store(i, l, now)
+    for l in range(layers - 2, -1, -1):
+        for i, b in enumerate(where):
+            part[i] = acc_ref[b, l] + row(coef_ref, b, RATIO, l) * part[i]
             store(i, l, part[i])
 
 
@@ -264,7 +284,10 @@
     def store(i, l, value):
         new_ref[l] = value
 
-    solve_blocks(lambda i, l: own_ref[l], coef_ref, acc_ref, store, [0])
+    def own(i, l, c):
+        return row(coef_ref, c, OWN, l) * own_ref[l]
+
+    solve_blocks(own, coef_ref, acc_ref, store, [0])
     new_out = pltpu.make_async_copy(new_ref, new_hbm, out_sem.at[1])
     new_out.start()
     if not last:
@@ -359,7 +382,10 @@
         def store(i, l, value):
             new_ref[l, :, lanes_of(where[i])] = value
 
-        solve_blocks(lambda i, l: field_ref[l, :, lanes_of(where[i])], coef_ref, acc_ref, store, where)
+        def own(i, l, c):
+            return row(coef_ref, c, OWN, l) * field_ref[l, :, lanes_of(where[i])]
+
+        solve_blocks(own, coef_ref, acc_ref, store, where)
         out_copy(g).start()
         return carry
 
@@ -367,6 +393,117 @@
     for g in range(groups):
         out_copy(g).wait()
     rim_out.wait()
+
+
+def local_kernel(plan_ref, field_hbm, coef_hbm, near_hbm, rate_hbm, part_hbm, *refs):
+    field_ref, coef_ref, near_ref, rate_ref, acc_ref, in_sem, out_sem = refs
+    blocks, layers = acc_ref.shape[0], acc_ref.shape[1]
+    width = plan_ref.shape[1]
+    pairs = (width - 4) // 2
+    loads = [
+        pltpu.make_async_copy(field_hbm, field_ref, in_sem.at[0]),
+        pltpu.make_async_copy(near_hbm, near_ref, in_sem.at[1]),
+        pltpu.make_async_copy(rate_hbm, rate_ref, in_sem.at[2]),
+        pltpu.make_async_copy(coef_hbm, coef_ref, in_sem.at[3]),
+    ]
+    for load in loads:
+        load.start()
+    for load in loads:
+        load.wait()
+
+    def out_copy(b):
+        return pltpu.make_async_copy(acc_ref.at[b], part_hbm.at[b], out_sem.at[b])
+
+    def block(b, carry):
+        start_block(plan_ref, coef_ref, near_ref, rate_ref, acc_ref, b, b, b, b)
+
+        def take(k, from_first, l):
+            return jnp.where(
+                from_first,
+                field_ref[l, :, lanes_of(plan_ref[b, k])],
+                field_ref[l, :, lanes_of(plan_ref[b, pairs + k])],
+            )
+
+        add_edges(take, coef_ref, near_ref, acc_ref, b, b, b, 0, plan_ref[b, width - 3])
+        for l in range(layers):
+            own = row(coef_ref, b, OWN, l) * field_ref[l, :, lanes_of(b)]
+            acc_ref[b, l] = acc_ref[b, l] + own
+        out_copy(b).start()
+        return carry
+
+    lax.fori_loop(0, blocks, block, 0)
+
+    def finish(b, carry):
+        out_copy(b).wait()
+        return carry
+
+    lax.fori_loop(0, blocks, finish, 0)
+
+
+def finish_kernel(plan_ref, part_hbm, received_ref, coef_hbm, near_hbm, out_hbm, *refs):
+    acc_ref, coef_ref, near_ref, halo_ref, new_ref, in_sem, out_sem = refs
+    blocks, layers = acc_ref.shape[0], acc_ref.shape[1]
+    width = plan_ref.shape[1]
+    group = 4
+    span = group * LANES
+    near_copy = pltpu.make_async_copy(near_hbm, near_ref, in_sem.at[0])
+    near_copy.start()
+
+    def copies(g):
+        part = pl.ds(g * group, group)
+        return (
+            pltpu.make_async_copy(part_hbm.at[part], acc_ref.at[part], in_sem.at[1 + 2 * g]),
+            pltpu.make_async_copy(coef_hbm.at[part], coef_ref.at[part], in_sem.at[2 + 2 * g]),
+        )
+
+    def out_copy(g):
+        lanes = pl.ds(pl.multiple_of(g * span, span), span)
+        return pltpu.make_async_copy(new_ref.at[:, :, lanes], out_hbm.at[:, :, lanes], out_sem.at[g])
+
+    groups = blocks // group
+    for g in range(groups):
+        for copy in copies(g):
+            copy.start()
+
+    def unpack(q, carry):
+        unpack_pieces(halo_ref, received_ref, layers, q, plan_ref[0, width - 4])
+        return carry
+
+    lax.fori_loop(0, halo_ref.shape[0], unpack, 0)
+    near_copy.wait()
+
+    def one(g, carry):
+        for copy in copies(g):
+            copy.wait()
+
+        def edges(i, inner):
+            b = g * group + i
+            add_edges(
+                lambda k, from_first, l: halo_ref[plan_ref[b, k] - blocks, l],
+                coef_ref,
+                near_ref,
+                acc_ref,
+                b,
+                b,
+                b,
+                plan_ref[b, width - 3],
+                plan_ref[b, width - 2],
+            )
+            return inner
+
+        lax.fori_loop(0, group, edges, 0)
+        where = [g * group + i for i in range(group)]
+
+        def store(i, l, value):
+            new_ref[l, :, lanes_of(where[i])] = value
+
+        solve_parts(coef_ref, acc_ref, store, where)
+        out_copy(g).start()
+        return carry
+
+    lax.fori_loop(0, groups, one, 0)
+    for g in range(groups):
+        out_copy(g).wait()
 
 
 def share_side(value, side):
@@ -384,8 +521,8 @@
 
 def share(value):
     half = value.shape[0] // 2
-    first = share_side(share_side(value[:half], 0), 1)
-    second = share_side(share_side(value[half:], 1), 0)
+    first, second = share_side(value[:half], 0), share_side(value[half:], 1)
+    first, second = share_side(first, 1), share_side(second, 0)
     return first, second
 
 
@@ -566,15 +703,55 @@
             name="bulk",
         )(plan, kept(field), kept(halo), kept(new), kept(coef), near, rate, kept(early))
 
+    part_shape = pltpu.HBM((blocks, *tile), f32)
+
+    def last_step_local(field, coef):
+        vmem = pltpu.VMEM
+        return pl.pallas_call(
+            local_kernel,
+            out_shape=part_shape,
+            in_specs=[scalars] + [hbm] * 4,
+            out_specs=hbm,
+            scratch_shapes=[
+                vmem(field.shape, f32),
+                vmem(coef_shape, f32),
+                vmem((blocks, 5, 8, LANES), jnp.int32),
+                vmem(tile, f32),
+                vmem(part_shape.shape, f32),
+                dma((4,)),
+                dma((blocks,)),
+            ],
+            compiler_params=params(24),
+            name="local",
+        )(plan, kept(field), kept(coef), near, rate)
+
+    def last_step(part, received, coef):
+        vmem = pltpu.VMEM
+        return pl.pallas_call(
+            finish_kernel,
+            out_shape=pltpu.HBM(concentration.shape, f32),
+            in_specs=[scalars, hbm, full, hbm, hbm],
+            out_specs=hbm,
+            scratch_shapes=[
+                vmem(part_shape.shape, f32),
+                vmem(coef_shape, f32),
+                vmem((blocks, 5, 8, LANES), jnp.int32),
+                vmem(halo_shape.shape, f32),
+                vmem(concentration.shape, f32),
+                dma((1 + 2 * (blocks // 4),)),
+                dma((blocks // 4,)),
+            ],
+            compiler_params=params(24),
+            name="finish",
+        )(plan, kept(part), received, kept(coef), near)
+
     field = concentration
     per_hour = STEPS // HOURS
     coef = prepare(share(panel(0)))
-    for step in range(STEPS):
-        last = step == STEPS - 1
+    for step in range(STEPS - 1):
         early = rate
-        send, halo, new = rim_step(field, received, coef, last)
-        if not last:
-            received = lax.all_to_all(send, "region", 0, 0, tiled=True)
+        send, halo, new = rim_step(field, received, coef, False)
+        received = lax.all_to_all(send, "region", 0, 0, tiled=True)
         if step == 0:
             later, _ = lax.optimization_barrier((panel(1), new))
             row_panels = share_side(later, 0)
@@ -585,7 +762,8 @@
         field = bulk_step(field, halo, new, coef, early)
         if step == per_hour - 1:
             coef = later_coef
-    return field
+    part = last_step_local(field, coef)
+    return last_step(part, received, coef)
 
 
 def solution(mesh):

time: 242 us -> 235 us (0.971)
  waiting for transfers between devices: 57 us -> 49.5 us
    pallas_call x0 -> x2, Pallas kernels: none -> 17.3 us  [the longest x1 12.1 us: last_step_local(): pl.pallas_call(local_kernel, out_shape=part_shape, in_specs=[scalars] + [...]
    pallas_call x6 -> x5, Pallas kernels: 72.8 us -> 60.7 us  [bulk_step(): pl.pallas_call(bulk_kernel, out_shape=pltpu.HBM(field.shape, f32), in_spe...]
    all_to_all x6, waiting for transfers between devices: 30.3 us -> 22.9 us  [transport(): received = lax.all_to_all(send, 'region', 0, 0, tiled=True)]
    pallas_call x6 -> x5, Pallas kernels: 29.2 us -> 24.8 us  [rim_step(): pl.pallas_call(functools.partial(rim_kernel, last), out_shape=outs, in_sp...]
  transfers between devices with their start and end apart: 24 -> 24, of which waited for: 13 -> 12; matrix products, arithmetic and copies ran while one was open for 4% -> 4% of each run, Pallas kernels for 29% -> 35%
where the time goes in v4:
time: 235 us; the launch traced here: 234 us
  Pallas kernels  112 us (48%)
  starting transfers between devices  61.1 us (26%)
  waiting for transfers between devices  49.5 us (21%)
  other arithmetic  6.36 us (3%)
  local copies, waits for them, and re-layouts  5.33 us (2%)
    pallas_call x5, Pallas kernels, bulk_step(): pl.pallas_call(bulk_kernel, out_shape=pltpu.HBM(field.shape, f32), in_spe...  60.7 us
    all_to_all x6, starting transfers between devices, transport(): received = lax.all_to_all(send, 'region', 0, 0, tiled=True)  36.3 us
    ppermute x18, waiting for transfers between devices, share_side(): shifts.append(lax.ppermute(value, 'tracer', pairs))  26.6 us
    pallas_call x5, Pallas kernels, rim_step(): pl.pallas_call(functools.partial(rim_kernel, last), out_shape=outs, in_sp...  24.8 us
    ppermute x18, starting transfers between devices, share_side(): shifts.append(lax.ppermute(value, 'tracer', pairs))  24.8 us
    all_to_all x6, waiting for transfers between devices, transport(): received = lax.all_to_all(send, 'region', 0, 0, tiled=True)  22.9 us
    pallas_call x1, Pallas kernels, last_step_local(): pl.pallas_call(local_kernel, out_shape=part_shape, in_specs=[scalars] + [...  12.1 us
    pallas_call x2, Pallas kernels, prepare(): pl.pallas_call(prepare_kernel, out_shape=pltpu.HBM(coef_shape, f32), in_s...  6.2 us
  transfers between devices with their start and end apart: 24, of which 12 were waited for; matrix products, arithmetic and copies ran while one was open for 4% of the time, Pallas kernels for 35%

profile of v4, /device:TPU:1, one launch (start us, length us, event | category | flops | bytes accessed | tf_op | source)
XLA Modules:
  0.0 234.4 jit_solution(17176242456356600000)
XLA Ops:
  0.0 0.8 slice.56
  0.8 3.3 %collective-permute-start.2 = (f32[80,128]{1,0:T(8,128)S(1)}, f32[80,128]{1,0:T(8,128)S(1)}, u32[]{:S(2)}, u32[]{:S(2)}) collective-permute-start(f32[80,128]{1,0:T(8,128)S(1)} %bitcast.88), channel_id=1, source_target_pairs={{0,3},{1,0},{2,1},{3,2},{4,7},{5,4},{6,5},{7,6},{8,11},{9,8},{10,9... | collective-permute-start | bytes 122888 | tf_op jit(solution)/shard_map/ppermute | solution.py:518
  4.1 0.5 collective-permute-start.1
  4.6 0.6 collective-permute-start
  5.2 0.9 fusion.17
  6.2 0.9 fusion.18
  7.2 3.0 %collective-permute-start.7 = (f32[80,128]{1,0:T(8,128)S(1)}, f32[80,128]{1,0:T(8,128)S(1)}, u32[]{:S(2)}, u32[]{:S(2)}) collective-permute-start(f32[80,128]{1,0:T(8,128)S(1)} %fusion.2), channel_id=1, source_target_pairs={{0,8},{1,9},{2,10},{3,11},{4,12},{5,13},{6,14},{7,15},{8,0},{9,1},... | collective-permute-start | bytes 122888 | tf_op jit(solution)/shard_map/ppermute | solution.py:518
  10.2 0.4 collective-permute-start.6
  10.6 0.7 maximum_add_fusion
  11.7 0.6 broadcast_in_dim.67.lanes_ref.refs_0_
  12.3 2.5 %pack.1 = f32[16,10,8,128]{3,2,1,0:T(8,128)} custom-call(f32[40,8,2048]{2,1,0:T(8,128)} %field_hbm.3, s32[4,4,8,128]{3,2,1,0:T(8,128)} %broadcast_in_dim.67.lanes_ref.refs_0_), custom_call_target="tpu_custom_call" | custom-call | tf_op jit(solution)/shard_map/pack/pallas_call | solution.py:559
  14.8 10.7 %all-to-all-start = ((f32[16,10,8,128]{3,2,1,0:T(8,128)}), f32[16,10,8,128]{3,2,1,0:T(8,128)S(1)}, u32[]{:S(2)}, u32[]{:S(2)}) async-start(f32[16,10,8,128]{3,2,1,0:T(8,128)} %pack.1), calls=%async_computation | async-start | bytes 1310720 | tf_op jit(solution)/shard_map/all_to_all | solution.py:570
  25.6 0.4 fusion
  26.2 2.0 compare_reduce_fusion.1
  28.3 0.2 convert_reduce_fusion.1
  28.5 0.4 convert_reduce_fusion
  29.0 0.4 select_reduce_fusion.1
  29.5 0.2 select_reduce_fusion.2
  29.9 0.1 select_reduce_fusion
  30.3 0.8 pad_add_fusion.near_hbm
  31.1 2.3 collective-permute-start.8
  33.6 0.7 collective-permute-start.3
  34.3 2.1 collective-permute-start.5
  36.4 1.7 collective-permute-start.10
  38.1 1.1 collective-permute-start.9
  39.1 1.2 collective-permute-done.4
  40.4 2.1 collective-permute-start.11
  42.9 1.5 collective-permute-done.3
  44.5 0.4 collective-permute-done.9
  45.0 1.7 collective-permute-done.11
  46.7 3.1 %prepare.2.coef_hbm = f32[16,7,40,128]{3,2,1,0:T(8,128)} custom-call(s32[2]{0:T(128)S(1)} %pad_add_fusion.4.home_ref, f32[4,4,80,128]{3,2,1,0:T(8,128)S(1)} %pad_maximum_fusion.1.refs_0_, f32[4,4,80,128]{3,2,1,0:T(8,128)S(1)} %pad_maximum_fusion.2.refs_1_), custom_call_target="tpu_custom_call" | custom-call | tf_op jit(solution)/shard_map/prepare/pallas_call | solution.py:643
  49.8 0.8 broadcast_in_dim.124.rate_hbm.early_hbm
  50.6 5.0 %rim.5 = (f32[16,10,8,128]{3,2,1,0:T(8,128)}, f32[4,40,8,128]{3,2,1,0:T(8,128)}, f32[40,8,128]{2,1,0:T(8,128)}) custom-call(s32[16,44]{1,0:T(8,128)S(1)} %concatenate.25.plan_ref, f32[40,8,2048]{2,1,0:T(8,128)} %field_hbm.3, f32[16,10,8,128]{3,2,1,0:T(8,128)S(1)} %all-to-all-done.received_ref, f32[16,7,40,128]{3,2,1,0:T(8,128)} %prepare.2.coef_hbm, ...), custom_call_target="tpu_custom_call" | custom-call | tf_op jit(solution)/shard_map/rim/pallas_call | solution.py:673
  55.6 8.7 %all-to-all-start.1 = ((f32[16,10,8,128]{3,2,1,0:T(8,128)}), f32[16,10,8,128]{3,2,1,0:T(8,128)S(1)}, u32[]{:S(2)}, u32[]{:S(2)}) async-start(f32[16,10,8,128]{3,2,1,0:T(8,128)} %get-tuple-element.23), calls=%async_computation.1 | async-start | bytes 1310720 | tf_op jit(solution)/shard_map/all_to_all | solution.py:754
  64.2 12.1 %bulk.5.field_hbm = f32[40,8,2048]{2,1,0:T(8,128)} custom-call(s32[16,44]{1,0:T(8,128)S(1)} %concatenate.25.plan_ref, f32[40,8,2048]{2,1,0:T(8,128)} %field_hbm.3, f32[4,40,8,128]{3,2,1,0:T(8,128)} %get-tuple-element.21.halo_hbm, f32[40,8,128]{2,1,0:T(8,128)} %get-tuple-element.22.rim_hbm, f32[16,7,40,128]{3,2,1,0:T(8,128)} %prepare.2.coef_hbm, ...), custom_call_target="tpu_custom_call" | custom-call | tf_op jit(solution)/shard_map/bulk/pallas_call | solution.py:686
  76.4 7.8 %all-to-all-done.1.received_ref = f32[16,10,8,128]{3,2,1,0:T(8,128)S(1)} async-done(((f32[16,10,8,128]{3,2,1,0:T(8,128)}), f32[16,10,8,128]{3,2,1,0:T(8,128)S(1)}, u32[]{:S(2)}, u32[]{:S(2)}) %all-to-all-start.1) | async-done | bytes 655392 | tf_op jit(solution)/shard_map/all_to_all | solution.py:754
  84.2 5.0 %rim.6 = (f32[16,10,8,128]{3,2,1,0:T(8,128)}, f32[4,40,8,128]{3,2,1,0:T(8,128)}, f32[40,8,128]{2,1,0:T(8,128)}) custom-call(s32[16,44]{1,0:T(8,128)S(1)} %concatenate.25.plan_ref, f32[40,8,2048]{2,1,0:T(8,128)} %bulk.5.field_hbm, f32[16,10,8,128]{3,2,1,0:T(8,128)S(1)} %all-to-all-done.1.received_ref, f32[16,7,40,128]{3,2,1,0:T(8,128)} %prepare.2.coef_hbm, ...), custom_call_target="tpu_custom_call" | custom-call | tf_op jit(solution)/shard_map/rim/pallas_call | solution.py:673
  89.2 3.5 %all-to-all-start.2 = ((f32[16,10,8,128]{3,2,1,0:T(8,128)}), f32[16,10,8,128]{3,2,1,0:T(8,128)S(1)}, u32[]{:S(2)}, u32[]{:S(2)}) async-start(f32[16,10,8,128]{3,2,1,0:T(8,128)} %get-tuple-element.26), calls=%async_computation.2 | async-start | bytes 1310720 | tf_op jit(solution)/shard_map/all_to_all | solution.py:754
  92.7 12.2 %bulk.6.field_hbm = f32[40,8,2048]{2,1,0:T(8,128)} custom-call(s32[16,44]{1,0:T(8,128)S(1)} %concatenate.25.plan_ref, f32[40,8,2048]{2,1,0:T(8,128)} %bulk.5.field_hbm, f32[4,40,8,128]{3,2,1,0:T(8,128)} %get-tuple-element.24.halo_hbm, f32[40,8,128]{2,1,0:T(8,128)} %get-tuple-element.25.rim_hbm, f32[16,7,40,128]{3,2,1,0:T(8,128)} %prepare.2.coef_hbm, ...), custom_call_target="tpu_custom_call" | custom-call | tf_op jit(solution)/shard_map/bulk/pallas_call | solution.py:686
  104.9 7.4 %all-to-all-done.2.received_ref = f32[16,10,8,128]{3,2,1,0:T(8,128)S(1)} async-done(((f32[16,10,8,128]{3,2,1,0:T(8,128)}), f32[16,10,8,128]{3,2,1,0:T(8,128)S(1)}, u32[]{:S(2)}, u32[]{:S(2)}) %all-to-all-start.2) | async-done | bytes 655392 | tf_op jit(solution)/shard_map/all_to_all | solution.py:754
  112.2 5.0 %rim.7 = (f32[16,10,8,128]{3,2,1,0:T(8,128)}, f32[4,40,8,128]{3,2,1,0:T(8,128)}, f32[40,8,128]{2,1,0:T(8,128)}) custom-call(s32[16,44]{1,0:T(8,128)S(1)} %concatenate.25.plan_ref, f32[40,8,2048]{2,1,0:T(8,128)} %bulk.6.field_hbm, f32[16,10,8,128]{3,2,1,0:T(8,128)S(1)} %all-to-all-done.2.received_ref, f32[16,7,40,128]{3,2,1,0:T(8,128)} %prepare.2.coef_hbm, ...), custom_call_target="tpu_custom_call" | custom-call | tf_op jit(solution)/shard_map/rim/pallas_call | solution.py:673
  117.2 3.5 %all-to-all-start.3 = ((f32[16,10,8,128]{3,2,1,0:T(8,128)}), f32[16,10,8,128]{3,2,1,0:T(8,128)S(1)}, u32[]{:S(2)}, u32[]{:S(2)}) async-start(f32[16,10,8,128]{3,2,1,0:T(8,128)} %get-tuple-element.30), calls=%async_computation.3 | async-start | bytes 1310720 | tf_op jit(solution)/shard_map/all_to_all | solution.py:754
  120.8 2.9 %collective-permute-start.14 = (f32[160,128]{1,0:T(8,128)S(1)}, f32[160,128]{1,0:T(8,128)S(1)}, u32[]{:S(2)}, u32[]{:S(2)}) collective-permute-start(f32[160,128]{1,0:T(8,128)S(1)} %maximum_maximum_fusion), channel_id=1, source_target_pairs={{0,3},{1,0},{2,1},{3,2},{4,7},{5,4},{6,5},{7,6},{8,11},{9,8},{10,9... | collective-permute-start | bytes 245768 | tf_op jit(solution)/shard_map/ppermute | solution.py:518
  123.7 0.5 collective-permute-start.13
  124.2 0.2 collective-permute-start.12
  124.4 3.1 %collective-permute-done.14 = f32[160,128]{1,0:T(8,128)S(1)} collective-permute-done((f32[160,128]{1,0:T(8,128)S(1)}, f32[160,128]{1,0:T(8,128)S(1)}, u32[]{:S(2)}, u32[]{:S(2)}) %collective-permute-start.14) | collective-permute-done | bytes 81952 | tf_op jit(solution)/shard_map/ppermute | solution.py:518
  127.5 1.8 collective-permute-done.13
  129.3 2.0 collective-permute-done.12
  131.4 0.8 collective-permute-start.16
  132.2 2.2 collective-permute-start.15
  134.5 0.4 collective-permute-start.17
  134.9 6.9 %collective-permute-done.16 = f32[4,160,128]{2,1,0:T(8,128)S(1)} collective-permute-done((f32[4,160,128]{2,1,0:T(8,128)S(1)}, f32[4,160,128]{2,1,0:T(8,128)S(1)}, u32[]{:S(2)}, u32[]{:S(2)}) %collective-permute-start.16) | collective-permute-done | bytes 327712 | tf_op jit(solution)/shard_map/ppermute | solution.py:518
  141.9 7.8 %collective-permute-done.15 = f32[4,160,128]{2,1,0:T(8,128)S(1)} collective-permute-done((f32[4,160,128]{2,1,0:T(8,128)S(1)}, f32[4,160,128]{2,1,0:T(8,128)S(1)}, u32[]{:S(2)}, u32[]{:S(2)}) %collective-permute-start.15) | collective-permute-done | bytes 327712 | tf_op jit(solution)/shard_map/ppermute | solution.py:518
  149.8 3.1 %prepare.3.early_hbm.coef_hbm = f32[16,7,40,128]{3,2,1,0:T(8,128)} custom-call(s32[2]{0:T(128)S(1)} %pad_add_fusion.4.home_ref, f32[4,4,160,128]{3,2,1,0:T(8,128)S(1)} %pad_maximum_fusion.refs_0_), custom_call_target="tpu_custom_call" | custom-call | tf_op jit(solution)/shard_map/prepare/pallas_call | solution.py:643
  152.9 12.1 %bulk.7.field_hbm = f32[40,8,2048]{2,1,0:T(8,128)} custom-call(s32[16,44]{1,0:T(8,128)S(1)} %concatenate.25.plan_ref, f32[40,8,2048]{2,1,0:T(8,128)} %bulk.6.field_hbm, f32[4,40,8,128]{3,2,1,0:T(8,128)} %get-tuple-element.27.halo_hbm, f32[40,8,128]{2,1,0:T(8,128)} %get-tuple-element.28.rim_hbm, f32[16,7,40,128]{3,2,1,0:T(8,128)} %prepare.2.coef_hbm, ...), custom_call_target="tpu_custom_call" | custom-call | tf_op jit(solution)/shard_map/bulk/pallas_call | solution.py:686
  165.0 5.0 %rim.8 = (f32[16,10,8,128]{3,2,1,0:T(8,128)}, f32[4,40,8,128]{3,2,1,0:T(8,128)}, f32[40,8,128]{2,1,0:T(8,128)}) custom-call(s32[16,44]{1,0:T(8,128)S(1)} %concatenate.25.plan_ref, f32[40,8,2048]{2,1,0:T(8,128)} %bulk.7.field_hbm, f32[16,10,8,128]{3,2,1,0:T(8,128)S(1)} %all-to-all-done.3.received_ref, f32[16,7,40,128]{3,2,1,0:T(8,128)} %prepare.3.early_hbm.coef_hbm, ...), custom_call_target="tpu_custom_call" | custom-call | tf_op jit(solution)/shard_map/rim/pallas_call | solution.py:673
  170.0 6.4 %all-to-all-start.4 = ((f32[16,10,8,128]{3,2,1,0:T(8,128)}), f32[16,10,8,128]{3,2,1,0:T(8,128)S(1)}, u32[]{:S(2)}, u32[]{:S(2)}) async-start(f32[16,10,8,128]{3,2,1,0:T(8,128)} %get-tuple-element.33), calls=%async_computation.4 | async-start | bytes 1310720 | tf_op jit(solution)/shard_map/all_to_all | solution.py:754
  176.4 12.2 %bulk.8.field_hbm = f32[40,8,2048]{2,1,0:T(8,128)} custom-call(s32[16,44]{1,0:T(8,128)S(1)} %concatenate.25.plan_ref, f32[40,8,2048]{2,1,0:T(8,128)} %bulk.7.field_hbm, f32[4,40,8,128]{3,2,1,0:T(8,128)} %get-tuple-element.31.halo_hbm, f32[40,8,128]{2,1,0:T(8,128)} %get-tuple-element.32.rim_hbm, f32[16,7,40,128]{3,2,1,0:T(8,128)} %prepare.3.early_hbm.coef_hbm, ...), custom_call_target="tpu_custom_call" | custom-call | tf_op jit(solution)/shard_map/bulk/pallas_call | solution.py:686
  188.6 7.7 %all-to-all-done.4.received_ref = f32[16,10,8,128]{3,2,1,0:T(8,128)S(1)} async-done(((f32[16,10,8,128]{3,2,1,0:T(8,128)}), f32[16,10,8,128]{3,2,1,0:T(8,128)S(1)}, u32[]{:S(2)}, u32[]{:S(2)}) %all-to-all-start.4) | async-done | bytes 655392 | tf_op jit(solution)/shard_map/all_to_all | solution.py:754
  196.3 5.0 %rim.9 = (f32[16,10,8,128]{3,2,1,0:T(8,128)}, f32[4,40,8,128]{3,2,1,0:T(8,128)}, f32[40,8,128]{2,1,0:T(8,128)}) custom-call(s32[16,44]{1,0:T(8,128)S(1)} %concatenate.25.plan_ref, f32[40,8,2048]{2,1,0:T(8,128)} %bulk.8.field_hbm, f32[16,10,8,128]{3,2,1,0:T(8,128)S(1)} %all-to-all-done.4.received_ref, f32[16,7,40,128]{3,2,1,0:T(8,128)} %prepare.3.early_hbm.coef_hbm, ...), custom_call_target="tpu_custom_call" | custom-call | tf_op jit(solution)/shard_map/rim/pallas_call | solution.py:673
  201.3 3.5 %all-to-all-start.5 = ((f32[16,10,8,128]{3,2,1,0:T(8,128)}), f32[16,10,8,128]{3,2,1,0:T(8,128)S(1)}, u32[]{:S(2)}, u32[]{:S(2)}) async-start(f32[16,10,8,128]{3,2,1,0:T(8,128)} %get-tuple-element.36), calls=%async_computation.5 | async-start | bytes 1310720 | tf_op jit(solution)/shard_map/all_to_all | solution.py:754
  204.8 12.1 %bulk.9.field_hbm = f32[40,8,2048]{2,1,0:T(8,128)} custom-call(s32[16,44]{1,0:T(8,128)S(1)} %concatenate.25.plan_ref, f32[40,8,2048]{2,1,0:T(8,128)} %bulk.8.field_hbm, f32[4,40,8,128]{3,2,1,0:T(8,128)} %get-tuple-element.34.halo_hbm, f32[40,8,128]{2,1,0:T(8,128)} %get-tuple-element.35.rim_hbm, f32[16,7,40,128]{3,2,1,0:T(8,128)} %prepare.3.early_hbm.coef_hbm, ...), custom_call_target="tpu_custom_call" | custom-call | tf_op jit(solution)/shard_map/bulk/pallas_call | solution.py:686
  217.0 12.1 %local.1.part_hbm = f32[16,40,8,128]{3,2,1,0:T(8,128)} custom-call(s32[16,44]{1,0:T(8,128)S(1)} %concatenate.25.plan_ref, f32[40,8,2048]{2,1,0:T(8,128)} %bulk.9.field_hbm, f32[16,7,40,128]{3,2,1,0:T(8,128)} %prepare.3.early_hbm.coef_hbm, s32[16,5,8,128]{3,2,1,0:T(8,128)} %pad_add_fusion.near_hbm, f32[40,8,128]{2,1,0:T(8,128)} %broadcast_in_dim.124.rate_hbm.early_hbm), custom_call_target="tpu_custom_call" | custom-call | tf_op jit(solution)/shard_map/local/pallas_call | solution.py:710
  229.1 5.2 %finish.1 = f32[40,8,2048]{2,1,0:T(8,128)} custom-call(s32[16,44]{1,0:T(8,128)S(1)} %concatenate.25.plan_ref, f32[16,40,8,128]{3,2,1,0:T(8,128)} %local.1.part_hbm, f32[16,10,8,128]{3,2,1,0:T(8,128)S(1)} %all-to-all-done.5.received_ref, f32[16,7,40,128]{3,2,1,0:T(8,128)} %prepare.3.early_hbm.coef_hbm, s32[16,5,8,128]{3,2,1,0:T(8,128)} %pad_add_fusion.near_hbm), custom_call_target="tpu_custom_call" | custom-call | tf_op jit(solution)/shard_map/finish/pallas_call | solution.py:730
  (73 shorter events, 2.6 us)
Async XLA Ops:
  0.8 30.3 %collective-permute-start.2 = (f32[80,128]{1,0:T(8,128)S(1)}, f32[80,128]{1,0:T(8,128)S(1)}, u32[]{:S(2)}, u32[]{:S(2)}) collective-permute-start(f32[80,128]{1,0:T(8,128)S(1)} %bitcast.88), channel_id=1, source_target_pairs={{0,3},{1,0},{2,1},{3,2},{4,7},{5,4},{6,5},{7,6},{8,11},{9,8},{10,9... | collective-permute-start | bytes 122888 | tf_op jit(solution)/shard_map/ppermute | solution.py:518
  4.1 29.3 %collective-permute-start.1 = (f32[80,128]{1,0:T(8,128)S(1)}, f32[80,128]{1,0:T(8,128)S(1)}, u32[]{:S(2)}, u32[]{:S(2)}) collective-permute-start(f32[80,128]{1,0:T(8,128)S(1)} %bitcast.89), channel_id=1, source_target_pairs={{0,2},{1,3},{2,0},{3,1},{4,6},{5,7},{6,4},{7,5},{8,10},{9,11},{10,... | collective-permute-start | bytes 122888 | tf_op jit(solution)/shard_map/ppermute | solution.py:518
  4.6 28.7 %collective-permute-start = (f32[80,128]{1,0:T(8,128)S(1)}, f32[80,128]{1,0:T(8,128)S(1)}, u32[]{:S(2)}, u32[]{:S(2)}) collective-permute-start(f32[80,128]{1,0:T(8,128)S(1)} %bitcast.90), channel_id=1, source_target_pairs={{0,1},{1,2},{2,3},{3,0},{4,5},{5,6},{6,7},{7,4},{8,9},{9,10},{10,1... | collective-permute-start | bytes 122888 | tf_op jit(solution)/shard_map/ppermute | solution.py:518
  6.1 19.5 %copy-start.1 = (s32[3,2048]{1,0:T(4,128)S(1)}, s32[3,2048]{1,0:T(4,128)}, u32[]{:S(2)}) copy-start(s32[3,2048]{1,0:T(4,128)} %param.12) | copy-start | bytes 73732
  7.2 27.0 %collective-permute-start.7 = (f32[80,128]{1,0:T(8,128)S(1)}, f32[80,128]{1,0:T(8,128)S(1)}, u32[]{:S(2)}, u32[]{:S(2)}) collective-permute-start(f32[80,128]{1,0:T(8,128)S(1)} %fusion.2), channel_id=1, source_target_pairs={{0,8},{1,9},{2,10},{3,11},{4,12},{5,13},{6,14},{7,15},{8,0},{9,1},... | collective-permute-start | bytes 122888 | tf_op jit(solution)/shard_map/ppermute | solution.py:518
  10.2 26.2 %collective-permute-start.6 = (f32[80,128]{1,0:T(8,128)S(1)}, f32[80,128]{1,0:T(8,128)S(1)}, u32[]{:S(2)}, u32[]{:S(2)}) collective-permute-start(f32[80,128]{1,0:T(8,128)S(1)} %fusion.2), channel_id=1, source_target_pairs={{0,4},{1,5},{2,6},{3,7},{4,8},{5,9},{6,10},{7,11},{8,12},{9,13},{1... | collective-permute-start | bytes 122888 | tf_op jit(solution)/shard_map/ppermute | solution.py:518
  12.3 17.7 %copy-start.3 = (s32[8]{0:T(128)S(1)}, s32[8]{0:T(128)}, u32[]{:S(2)}) copy-start(s32[8]{0:T(128)} %param.11) | copy-start | bytes 100
  14.8 27.8 %copy-start.2 = (f32[40,8]{0,1:T(8,128)S(1)}, f32[40,8]{0,1:T(8,128)}, u32[]{:S(2)}) copy-start(f32[40,8]{0,1:T(8,128)} %param.10) | copy-start | bytes 3844
  14.8 35.0 %all-to-all-start = ((f32[16,10,8,128]{3,2,1,0:T(8,128)}), f32[16,10,8,128]{3,2,1,0:T(8,128)S(1)}, u32[]{:S(2)}, u32[]{:S(2)}) async-start(f32[16,10,8,128]{3,2,1,0:T(8,128)} %pack.1), calls=%async_computation | async-start | bytes 1310720 | tf_op jit(solution)/shard_map/all_to_all | solution.py:570
  31.1 5.3 %collective-permute-start.8 = (f32[80,128]{1,0:T(8,128)S(1)}, f32[80,128]{1,0:T(8,128)S(1)}, u32[]{:S(2)}, u32[]{:S(2)}) collective-permute-start(f32[80,128]{1,0:T(8,128)S(1)} %fusion.2), channel_id=1, source_target_pairs={{0,12},{1,13},{2,14},{3,15},{4,0},{5,1},{6,2},{7,3},{8,4},{9,5},{1... | collective-permute-start | bytes 122888 | tf_op jit(solution)/shard_map/ppermute | solution.py:518
  33.4 7.0 %collective-permute-start.4 = (f32[4,80,128]{2,1,0:T(8,128)S(1)}, f32[4,80,128]{2,1,0:T(8,128)S(1)}, u32[]{:S(2)}, u32[]{:S(2)}) collective-permute-start(f32[4,80,128]{2,1,0:T(8,128)S(1)} %get-tuple-element.52), channel_id=1, source_target_pairs={{0,8},{1,9},{2,10},{3,11},{4,12},{5,13},{6,14},{7,15},{8,0},{9,1},... | collective-permute-start | bytes 491528 | tf_op jit(solution)/shard_map/ppermute | solution.py:518
  33.6 10.8 %collective-permute-start.3 = (f32[4,80,128]{2,1,0:T(8,128)S(1)}, f32[4,80,128]{2,1,0:T(8,128)S(1)}, u32[]{:S(2)}, u32[]{:S(2)}) collective-permute-start(f32[4,80,128]{2,1,0:T(8,128)S(1)} %get-tuple-element.52), channel_id=1, source_target_pairs={{0,4},{1,5},{2,6},{3,7},{4,8},{5,9},{6,10},{7,11},{8,12},{9,13},{1... | collective-permute-start | bytes 491528 | tf_op jit(solution)/shard_map/ppermute | solution.py:518
  34.3 10.2 %collective-permute-start.5 = (f32[4,80,128]{2,1,0:T(8,128)S(1)}, f32[4,80,128]{2,1,0:T(8,128)S(1)}, u32[]{:S(2)}, u32[]{:S(2)}) collective-permute-start(f32[4,80,128]{2,1,0:T(8,128)S(1)} %get-tuple-element.52), channel_id=1, source_target_pairs={{0,12},{1,13},{2,14},{3,15},{4,0},{5,1},{6,2},{7,3},{8,4},{9,5},{1... | collective-permute-start | bytes 491528 | tf_op jit(solution)/shard_map/ppermute | solution.py:518
  36.4 8.1 %collective-permute-start.10 = (f32[4,80,128]{2,1,0:T(8,128)S(1)}, f32[4,80,128]{2,1,0:T(8,128)S(1)}, u32[]{:S(2)}, u32[]{:S(2)}) collective-permute-start(f32[4,80,128]{2,1,0:T(8,128)S(1)} %get-tuple-element.50), channel_id=1, source_target_pairs={{0,2},{1,3},{2,0},{3,1},{4,6},{5,7},{6,4},{7,5},{8,10},{9,11},{10,... | collective-permute-start | bytes 491528 | tf_op jit(solution)/shard_map/ppermute | solution.py:518
  38.1 6.9 %collective-permute-start.9 = (f32[4,80,128]{2,1,0:T(8,128)S(1)}, f32[4,80,128]{2,1,0:T(8,128)S(1)}, u32[]{:S(2)}, u32[]{:S(2)}) collective-permute-start(f32[4,80,128]{2,1,0:T(8,128)S(1)} %get-tuple-element.50), channel_id=1, source_target_pairs={{0,1},{1,2},{2,3},{3,0},{4,5},{5,6},{6,7},{7,4},{8,9},{9,10},{10,1... | collective-permute-start | bytes 491528 | tf_op jit(solution)/shard_map/ppermute | solution.py:518
  40.4 6.3 %collective-permute-start.11 = (f32[4,80,128]{2,1,0:T(8,128)S(1)}, f32[4,80,128]{2,1,0:T(8,128)S(1)}, u32[]{:S(2)}, u32[]{:S(2)}) collective-permute-start(f32[4,80,128]{2,1,0:T(8,128)S(1)} %get-tuple-element.50), channel_id=1, source_target_pairs={{0,3},{1,0},{2,1},{3,2},{4,7},{5,4},{6,5},{7,6},{8,11},{9,8},{10,9... | collective-permute-start | bytes 491528 | tf_op jit(solution)/shard_map/ppermute | solution.py:518
  44.5 6.1 %copy-start = (s32[4,4,8,128]{3,2,1,0:T(8,128)S(1)}, s32[4,4,8,128]{3,2,1,0:T(8,128)}, u32[]{:S(2)}) copy-start(s32[4,4,8,128]{3,2,1,0:T(8,128)} %broadcast_in_dim.67.lanes_ref.refs_0_) | copy-start | bytes 196612
  55.6 28.6 %all-to-all-start.1 = ((f32[16,10,8,128]{3,2,1,0:T(8,128)}), f32[16,10,8,128]{3,2,1,0:T(8,128)S(1)}, u32[]{:S(2)}, u32[]{:S(2)}) async-start(f32[16,10,8,128]{3,2,1,0:T(8,128)} %get-tuple-element.23), calls=%async_computation.1 | async-start | bytes 1310720 | tf_op jit(solution)/shard_map/all_to_all | solution.py:754
  89.2 23.1 %all-to-all-start.2 = ((f32[16,10,8,128]{3,2,1,0:T(8,128)}), f32[16,10,8,128]{3,2,1,0:T(8,128)S(1)}, u32[]{:S(2)}, u32[]{:S(2)}) async-start(f32[16,10,8,128]{3,2,1,0:T(8,128)} %get-tuple-element.26), calls=%async_computation.2 | async-start | bytes 1310720 | tf_op jit(solution)/shard_map/all_to_all | solution.py:754
  117.2 47.8 %all-to-all-start.3 = ((f32[16,10,8,128]{3,2,1,0:T(8,128)}), f32[16,10,8,128]{3,2,1,0:T(8,128)S(1)}, u32[]{:S(2)}, u32[]{:S(2)}) async-start(f32[16,10,8,128]{3,2,1,0:T(8,128)} %get-tuple-element.30), calls=%async_computation.3 | async-start | bytes 1310720 | tf_op jit(solution)/shard_map/all_to_all | solution.py:754
  120.8 6.7 %collective-permute-start.14 = (f32[160,128]{1,0:T(8,128)S(1)}, f32[160,128]{1,0:T(8,128)S(1)}, u32[]{:S(2)}, u32[]{:S(2)}) collective-permute-start(f32[160,128]{1,0:T(8,128)S(1)} %maximum_maximum_fusion), channel_id=1, source_target_pairs={{0,3},{1,0},{2,1},{3,2},{4,7},{5,4},{6,5},{7,6},{8,11},{9,8},{10,9... | collective-permute-start | bytes 245768 | tf_op jit(solution)/shard_map/ppermute | solution.py:518
  123.7 5.6 %collective-permute-start.13 = (f32[160,128]{1,0:T(8,128)S(1)}, f32[160,128]{1,0:T(8,128)S(1)}, u32[]{:S(2)}, u32[]{:S(2)}) collective-permute-start(f32[160,128]{1,0:T(8,128)S(1)} %maximum_maximum_fusion), channel_id=1, source_target_pairs={{0,2},{1,3},{2,0},{3,1},{4,6},{5,7},{6,4},{7,5},{8,10},{9,11},{10,... | collective-permute-start | bytes 245768 | tf_op jit(solution)/shard_map/ppermute | solution.py:518
  124.2 7.1 %collective-permute-start.12 = (f32[160,128]{1,0:T(8,128)S(1)}, f32[160,128]{1,0:T(8,128)S(1)}, u32[]{:S(2)}, u32[]{:S(2)}) collective-permute-start(f32[160,128]{1,0:T(8,128)S(1)} %maximum_maximum_fusion), channel_id=1, source_target_pairs={{0,1},{1,2},{2,3},{3,0},{4,5},{5,6},{6,7},{7,4},{8,9},{9,10},{10,1... | collective-permute-start | bytes 245768 | tf_op jit(solution)/shard_map/ppermute | solution.py:518
  131.4 10.4 %collective-permute-start.16 = (f32[4,160,128]{2,1,0:T(8,128)S(1)}, f32[4,160,128]{2,1,0:T(8,128)S(1)}, u32[]{:S(2)}, u32[]{:S(2)}) collective-permute-start(f32[4,160,128]{2,1,0:T(8,128)S(1)} %get-tuple-element.48), channel_id=1, source_target_pairs={{0,8},{1,9},{2,10},{3,11},{4,12},{5,13},{6,14},{7,15},{8,0},{9,1},... | collective-permute-start | bytes 983048 | tf_op jit(solution)/shard_map/ppermute | solution.py:518
  132.2 17.4 %collective-permute-start.15 = (f32[4,160,128]{2,1,0:T(8,128)S(1)}, f32[4,160,128]{2,1,0:T(8,128)S(1)}, u32[]{:S(2)}, u32[]{:S(2)}) collective-permute-start(f32[4,160,128]{2,1,0:T(8,128)S(1)} %get-tuple-element.48), channel_id=1, source_target_pairs={{0,4},{1,5},{2,6},{3,7},{4,8},{5,9},{6,10},{7,11},{8,12},{9,13},{1... | collective-permute-start | bytes 983048 | tf_op jit(solution)/shard_map/ppermute | solution.py:518
  134.5 15.2 %collective-permute-start.17 = (f32[4,160,128]{2,1,0:T(8,128)S(1)}, f32[4,160,128]{2,1,0:T(8,128)S(1)}, u32[]{:S(2)}, u32[]{:S(2)}) collective-permute-start(f32[4,160,128]{2,1,0:T(8,128)S(1)} %get-tuple-element.48), channel_id=1, source_target_pairs={{0,12},{1,13},{2,14},{3,15},{4,0},{5,1},{6,2},{7,3},{8,4},{9,5},{1... | collective-permute-start | bytes 983048 | tf_op jit(solution)/shard_map/ppermute | solution.py:518
  170.0 26.4 %all-to-all-start.4 = ((f32[16,10,8,128]{3,2,1,0:T(8,128)}), f32[16,10,8,128]{3,2,1,0:T(8,128)S(1)}, u32[]{:S(2)}, u32[]{:S(2)}) async-start(f32[16,10,8,128]{3,2,1,0:T(8,128)} %get-tuple-element.33), calls=%async_computation.4 | async-start | bytes 1310720 | tf_op jit(solution)/shard_map/all_to_all | solution.py:754
  201.3 27.7 %all-to-all-start.5 = ((f32[16,10,8,128]{3,2,1,0:T(8,128)}), f32[16,10,8,128]{3,2,1,0:T(8,128)S(1)}, u32[]{:S(2)}, u32[]{:S(2)}) async-start(f32[16,10,8,128]{3,2,1,0:T(8,128)} %get-tuple-element.36), calls=%async_computation.5 | async-start | bytes 1310720 | tf_op jit(solution)/shard_map/all_to_all | solution.py:754
